TPU v7x, 32 devices: a whole 2x2x4 slice. The times are simulated.
32 devices in a mesh: fsdp: 16 (over z, y, core), seq: 2 (over x).
Axes of the slice: x: 2, y: 2, z: 4, core: 2. Of those that a mesh axis runs over, the one named last changes fastest.
Arguments:
- img_in: bfloat16 [32, 1024, 1536], P('fsdp', 'seq'), may hold values from -6 to 6
- txt_in: bfloat16 [32, 162, 1536], P('fsdp', 'seq'), may hold values from -6 to 6
- cond: bfloat16 [32, 1536], P('fsdp'), may hold values from -6 to 6
- text_counts: int32 [32, 2], P('fsdp'), may hold values from 1 to 81, 154 in all within a row
- ada_w: bfloat16 [2, 1536, 9216], P(None, 'fsdp'), may hold values from -0.15625 to 0.15625
- qkv_w: bfloat16 [2, 1536, 4608], P(None, 'fsdp'), may hold values from -0.15625 to 0.15625
- proj_w: bfloat16 [2, 1536, 1536], P(None, 'fsdp'), may hold values from -0.625 to 0.625
- fc1_w: bfloat16 [2, 1536, 6144], P(None, 'fsdp'), may hold values from -0.15625 to 0.15625
- fc2_w: bfloat16 [2, 6144, 1536], P(None, 'fsdp'), may hold values from -0.078125 to 0.078125
- qk_gain: float32 [2, 128], replicated, may hold values from 1 to 2
- img_cot: bfloat16 [32, 1024, 1536], P('fsdp', 'seq'), may hold values from -6 to 6
- txt_cot: bfloat16 [32, 162, 1536], P('fsdp', 'seq'), may hold values from -6 to 6
Outputs:
- img_out: bfloat16 [32, 1024, 1536], P('fsdp', 'seq')
- txt_out: bfloat16 [32, 162, 1536], P('fsdp', 'seq')
- img_grad: float32 [32, 1024, 1536], P('fsdp', 'seq')
- txt_grad: float32 [32, 162, 1536], P('fsdp', 'seq')
- cond_grad: float32 [32, 1536], P('fsdp')
- ada_grad: float32 [2, 1536, 9216], P(None, ('fsdp', 'seq'))
- qkv_grad: float32 [2, 1536, 4608], P(None, ('fsdp', 'seq'))
- proj_grad: float32 [2, 1536, 1536], P(None, ('fsdp', 'seq'))
- fc1_grad: float32 [2, 1536, 6144], P(None, ('fsdp', 'seq'))
- fc2_grad: float32 [2, 6144, 1536], P(None, ('fsdp', 'seq'))
- gain_grad: float32 [2, 128], replicated
Inputs may be any that keep to these rules, and one draw needn't show every extreme that they name: `text_counts`: row s gives how many live text tokens each of the 2 members of seq holds for sequence s, in its first slots; each row sums to 154.
All inputs are finite; a program needn't handle non-finite values.
Results may differ from a plain program's by a relative error of at most 0.014.
The roundings to bfloat16 on the way count: a program that leaves them out, or rounds other values in their place, can miss the bound.
Values may be sent and summed in bfloat16 or wider, within the bound.
A program may use at most 704 MiB of HBM per device.

v0:
```python
import jax
import jax.numpy as jnp
from jax import lax
from jax.sharding import PartitionSpec as P

HEAD = 64


def layer_norm(values):
    average = jnp.mean(values, axis=-1, keepdims=True)
    centred = values - average
    variance = jnp.mean(centred * centred, axis=-1, keepdims=True)
    return centred * lax.rsqrt(variance + 1e-06)


def modulate(values, shift_vec, scale_vec):
    return layer_norm(values) * (1.0 + scale_vec[:, None, :]) + shift_vec[:, None, :]


def rms_heads(values, gain_vec):
    shaped = values.reshape(values.shape[:-1] + (values.shape[-1] // HEAD, HEAD))
    square = jnp.mean(shaped * shaped, axis=-1, keepdims=True)
    return (shaped * lax.rsqrt(square + 1e-06) * gain_vec).reshape(values.shape)


def qk_norms(query_raw, key_raw, gain_vec):
    return (rms_heads(query_raw, gain_vec[:HEAD]), rms_heads(key_raw, gain_vec[HEAD:]))


def gelu_tanh(values):
    return jax.nn.gelu(values, approximate=True)


def head_split(values):
    return values.reshape(values.shape[0], values.shape[1] // HEAD, HEAD)


def masked_scores(query_heads, key_heads, keys_live):
    scores = jnp.einsum(
        "qhe,khe->hqk", query_heads, key_heads, preferred_element_type=jnp.float32
    ) * HEAD ** (-0.5)
    return jnp.where(keys_live > 0.5, scores, -1000000000.0)


def attend(items):
    joint_qkv, keys_live = items
    query_heads = head_split(joint_qkv[0])
    key_heads = head_split(joint_qkv[1])
    value_heads = head_split(joint_qkv[2])
    scores = masked_scores(query_heads, key_heads, keys_live)
    row_max = jnp.max(scores, axis=-1, keepdims=True)
    exponent = jnp.exp(scores - row_max)
    row_sum = jnp.sum(exponent, axis=-1, keepdims=True)
    weights_low = (exponent / row_sum).astype(jnp.bfloat16)
    attended = jnp.einsum(
        "hqk,khe->qhe", weights_low, value_heads, preferred_element_type=jnp.float32
    )
    attended = attended.astype(jnp.bfloat16).reshape(joint_qkv.shape[1], joint_qkv.shape[2])
    return (attended, (row_max + jnp.log(row_sum))[..., 0])


def attend_back(items):
    joint_qkv, keys_live, log_norm, attended_grad = items
    query_heads = head_split(joint_qkv[0])
    key_heads = head_split(joint_qkv[1])
    value_heads = head_split(joint_qkv[2])
    scores = masked_scores(query_heads, key_heads, keys_live)
    probabilities = jnp.exp(scores - log_norm[..., None])
    grad_heads = head_split(attended_grad)
    prob_grad = jnp.einsum(
        "qhe,khe->hqk", grad_heads, value_heads, preferred_element_type=jnp.float32
    )
    row_delta = jnp.sum(probabilities * prob_grad, axis=-1, keepdims=True)
    score_grad = (probabilities * (prob_grad - row_delta)).astype(jnp.bfloat16)
    scale_factor = HEAD ** (-0.5)
    query_grad = (
        jnp.einsum("hqk,khe->qhe", score_grad, key_heads, preferred_element_type=jnp.float32)
        * scale_factor
    ).astype(jnp.bfloat16)
    key_grad = (
        jnp.einsum("hqk,qhe->khe", score_grad, query_heads, preferred_element_type=jnp.float32)
        * scale_factor
    ).astype(jnp.bfloat16)
    value_grad = jnp.einsum(
        "hqk,qhe->khe",
        probabilities.astype(jnp.bfloat16),
        grad_heads,
        preferred_element_type=jnp.float32,
    ).astype(jnp.bfloat16)
    return jnp.stack([query_grad, key_grad, value_grad]).reshape(joint_qkv.shape)


def reduce_rows(row_term, own_rows):
    return lax.psum_scatter(
        row_term(jnp.int32(0), lax.axis_size(("fsdp", "seq")) * own_rows),
        ("fsdp", "seq"),
        scatter_dimension=0,
        tiled=True,
    )


def flat_rows(values):
    return jnp.concatenate([item.reshape(-1, item.shape[-1]) for item in values], axis=0)


def body(
    img_in, txt_in, cond, text_counts, ada_w, qkv_w, proj_w, fc1_w, fc2_w, qk_gain, img_cot, txt_cot
):
    members = lax.axis_size("seq")
    member = lax.axis_index("seq")
    seq_local, img_local, model_width = img_in.shape
    slot_count = txt_in.shape[1]
    per_batch = seq_local // 2
    replica_count = lax.axis_size(("fsdp", "seq"))
    cond_act = jax.nn.silu(cond.astype(jnp.float32)).astype(jnp.bfloat16)
    every_cond = lax.all_gather(cond_act, "fsdp", axis=0, tiled=True)
    shard_rows = ada_w.shape[1]
    cond_cols = lax.dynamic_slice_in_dim(
        every_cond, lax.axis_index("fsdp") * shard_rows, shard_rows, 1
    )
    modulation = lax.psum_scatter(
        jnp.einsum("sd,tdm->stm", cond_cols, ada_w, preferred_element_type=jnp.float32),
        "fsdp",
        scatter_dimension=0,
        tiled=True,
    )
    slot_ids = lax.broadcasted_iota(jnp.int32, (seq_local, members, slot_count), 2)
    member_live = (slot_ids < text_counts[:, :, None]).astype(jnp.float32)
    own_count = lax.dynamic_slice_in_dim(text_counts, member, 1, 1)
    text_live = (slot_ids[:, 0, :] < own_count).astype(jnp.float32)
    image_live = jnp.ones((seq_local, members, img_local), jnp.float32)
    keys_live = jnp.concatenate([image_live, member_live], axis=2).reshape(seq_local, -1)
    w_qkv, w_proj, w_fc1, w_fc2 = (
        lax.all_gather(qkv_w, "fsdp", axis=1, tiled=True),
        lax.all_gather(proj_w, "fsdp", axis=1, tiled=True),
        lax.all_gather(fc1_w, "fsdp", axis=1, tiled=True),
        lax.all_gather(fc2_w, "fsdp", axis=1, tiled=True),
    )
    out_parts = ([], [])
    saved = []
    for micro_batch in range(2):
        first = micro_batch * per_batch
        last = first + per_batch
        text_rows = text_live[first:last][:, :, None]
        inputs = (img_in[first:last].astype(jnp.float32), txt_in[first:last].astype(jnp.float32))
        cotangents = (
            img_cot[first:last].astype(jnp.float32),
            txt_cot[first:last].astype(jnp.float32) * text_rows,
        )
        mod_rows = modulation[first:last]
        live_rows = keys_live[first:last]
        stored = []
        stacked = []
        for modality in range(2):
            pieces = jnp.split(mod_rows[:, modality], 6, axis=-1)
            token_in = inputs[modality]
            normed_in = modulate(token_in, pieces[0], pieces[1]).astype(jnp.bfloat16)
            qkv_raw = jnp.einsum(
                "bnd,de->bne", normed_in, w_qkv[modality], preferred_element_type=jnp.float32
            )
            query_raw = qkv_raw[..., :model_width]
            key_raw = qkv_raw[..., model_width : 2 * model_width]
            query_new, key_new = qk_norms(query_raw, key_raw, qk_gain[modality])
            stacked.append(
                jnp.stack(
                    [
                        query_new.astype(jnp.bfloat16),
                        key_new.astype(jnp.bfloat16),
                        qkv_raw[..., 2 * model_width :].astype(jnp.bfloat16),
                    ],
                    axis=1,
                )
            )
            stored.append((token_in, pieces, normed_in, query_raw, key_raw))
        joint_qkv = jnp.concatenate(stacked, axis=2)
        heads_in = lax.all_to_all(joint_qkv, "seq", split_axis=3, concat_axis=2, tiled=True)
        attended_heads, log_norm = lax.map(attend, (heads_in, live_rows))
        attended_tok = lax.all_to_all(
            attended_heads, "seq", split_axis=1, concat_axis=2, tiled=True
        )
        forward_kept = []
        for modality in range(2):
            token_in, pieces, normed_in, query_raw, key_raw = stored[modality]
            portion = attended_tok[:, :img_local] if modality == 0 else attended_tok[:, img_local:]
            branch = jnp.einsum(
                "bnc,cd->bnd", portion, w_proj[modality], preferred_element_type=jnp.float32
            )
            middle = token_in + pieces[2][:, None, :] * branch
            normed_mid = modulate(middle, pieces[3], pieces[4]).astype(jnp.bfloat16)
            hidden = jnp.einsum(
                "bnd,df->bnf", normed_mid, w_fc1[modality], preferred_element_type=jnp.float32
            )
            activated_low = gelu_tanh(hidden).astype(jnp.bfloat16)
            mlp_out = jnp.einsum(
                "bnf,fd->bnd", activated_low, w_fc2[modality], preferred_element_type=jnp.float32
            )
            result = middle + pieces[5][:, None, :] * mlp_out
            if modality == 1:
                result = result * text_rows
            out_parts[modality].append(result.astype(jnp.bfloat16))
            forward_kept.append(
                (portion, branch, middle, normed_mid, hidden, activated_low, mlp_out)
            )
        saved.append((cotangents, live_rows, stored, heads_in, log_norm, forward_kept))
    kept_act = ([], [])
    kept_mlp_grad = ([], [])
    kept_normed_mid = ([], [])
    kept_hidden_grad = ([], [])
    kept_attended = ([], [])
    kept_branch_grad = ([], [])
    kept_normed_in = ([], [])
    kept_raw_grad = ([], [])
    mlp_later = []
    for micro_batch in range(2):
        cotangents, live_rows, stored, heads_in, log_norm, forward_kept = saved[micro_batch]
        batch_later = []
        for modality in range(2):
            pieces = stored[modality][1]
            portion, branch, middle, normed_mid, hidden, activated_low, mlp_out = forward_kept[
                modality
            ]
            out_grad = cotangents[modality]
            gate_mlp_grad = jnp.sum(out_grad * mlp_out, axis=1)
            mlp_grad = (pieces[5][:, None, :] * out_grad).astype(jnp.bfloat16)
            activated_grad = jnp.einsum(
                "bnd,fd->bnf", mlp_grad, w_fc2[modality], preferred_element_type=jnp.float32
            )
            _, gelu_pull = jax.vjp(gelu_tanh, hidden)
            hidden_grad = gelu_pull(activated_grad)[0].astype(jnp.bfloat16)
            mid_grad = jnp.einsum(
                "bnf,df->bnd", hidden_grad, w_fc1[modality], preferred_element_type=jnp.float32
            )
            _, mid_pull = jax.vjp(modulate, middle, pieces[3], pieces[4])
            middle_norm_grad, shift_mlp_grad, scale_mlp_grad = mid_pull(mid_grad)
            kept_act[modality].append(activated_low)
            kept_mlp_grad[modality].append(mlp_grad)
            kept_normed_mid[modality].append(normed_mid)
            kept_hidden_grad[modality].append(hidden_grad)
            batch_later.append(
                (out_grad + middle_norm_grad, shift_mlp_grad, scale_mlp_grad, gate_mlp_grad)
            )
        mlp_later.append(batch_later)
    gain_gradient = jnp.zeros(qk_gain.shape, jnp.float32)
    in_grads = ([], [])
    mod_grads = ([], [])
    for micro_batch in range(2):
        cotangents, live_rows, stored, heads_in, log_norm, forward_kept = saved[micro_batch]
        attended_grads = []
        later = []
        for modality in range(2):
            pieces = stored[modality][1]
            portion, branch = (forward_kept[modality][0], forward_kept[modality][1])
            middle_grad, shift_mlp_grad, scale_mlp_grad, gate_mlp_grad = mlp_later[micro_batch][
                modality
            ]
            gate_attn_grad = jnp.sum(middle_grad * branch, axis=1)
            branch_grad = (pieces[2][:, None, :] * middle_grad).astype(jnp.bfloat16)
            kept_attended[modality].append(portion)
            kept_branch_grad[modality].append(branch_grad)
            attended_grads.append(
                jnp.einsum(
                    "bnd,cd->bnc", branch_grad, w_proj[modality], preferred_element_type=jnp.float32
                ).astype(jnp.bfloat16)
            )
            later.append(
                (middle_grad, gate_attn_grad, shift_mlp_grad, scale_mlp_grad, gate_mlp_grad)
            )
        attended_grad = jnp.concatenate(attended_grads, axis=1)
        grad_heads = lax.all_to_all(attended_grad, "seq", split_axis=2, concat_axis=1, tiled=True)
        qkv_grad_heads = lax.map(attend_back, (heads_in, live_rows, log_norm, grad_heads))
        qkv_grad_tok = lax.all_to_all(
            qkv_grad_heads, "seq", split_axis=2, concat_axis=3, tiled=True
        )
        for modality in range(2):
            token_in, pieces, normed_in, query_raw, key_raw = stored[modality]
            middle_grad, gate_attn_grad, shift_mlp_grad, scale_mlp_grad, gate_mlp_grad = later[
                modality
            ]
            portion = (
                qkv_grad_tok[:, :, :img_local] if modality == 0 else qkv_grad_tok[:, :, img_local:]
            )
            _, norm_pull = jax.vjp(qk_norms, query_raw, key_raw, qk_gain[modality])
            query_raw_grad, key_raw_grad, gain_delta = norm_pull(
                (portion[:, 0].astype(jnp.float32), portion[:, 1].astype(jnp.float32))
            )
            gain_gradient = gain_gradient.at[modality].add(gain_delta)
            raw_grad = jnp.concatenate(
                [query_raw_grad, key_raw_grad, portion[:, 2].astype(jnp.float32)], axis=-1
            ).astype(jnp.bfloat16)
            kept_normed_in[modality].append(normed_in)
            kept_raw_grad[modality].append(raw_grad)
            in_grad = jnp.einsum(
                "bne,de->bnd", raw_grad, w_qkv[modality], preferred_element_type=jnp.float32
            )
            _, in_pull = jax.vjp(modulate, token_in, pieces[0], pieces[1])
            token_norm_grad, shift_attn_grad, scale_attn_grad = in_pull(in_grad)
            in_grads[modality].append(middle_grad + token_norm_grad)
            mod_grads[modality].append(
                jnp.concatenate(
                    [
                        shift_attn_grad,
                        scale_attn_grad,
                        gate_attn_grad,
                        shift_mlp_grad,
                        scale_mlp_grad,
                        gate_mlp_grad,
                    ],
                    axis=-1,
                )
            )
    attended_all = [flat_rows(kept_attended[m]) for m in range(2)]
    branch_all = [flat_rows(kept_branch_grad[m]) for m in range(2)]
    normed_in_all = [flat_rows(kept_normed_in[m]) for m in range(2)]
    raw_all = [flat_rows(kept_raw_grad[m]) for m in range(2)]
    normed_mid_all = [flat_rows(kept_normed_mid[m]) for m in range(2)]
    hidden_all = [flat_rows(kept_hidden_grad[m]) for m in range(2)]
    act_all = [flat_rows(kept_act[m]) for m in range(2)]
    mlp_all = [flat_rows(kept_mlp_grad[m]) for m in range(2)]

    def width_term(first_row, row_count):
        columns = []
        for modality in range(2):
            left_att = attended_all[modality]
            columns.append(
                jnp.einsum(
                    "nr,nc->rc", left_att, branch_all[modality], preferred_element_type=jnp.float32
                )
            )
            left_in = normed_in_all[modality]
            columns.append(
                jnp.einsum(
                    "nr,nc->rc", left_in, raw_all[modality], preferred_element_type=jnp.float32
                )
            )
            left_mid = normed_mid_all[modality]
            columns.append(
                jnp.einsum(
                    "nr,nc->rc", left_mid, hidden_all[modality], preferred_element_type=jnp.float32
                )
            )
        return jnp.concatenate(columns, axis=-1)

    def hidden_term(first_row, row_count):
        columns = []
        for modality in range(2):
            left_act = act_all[modality]
            columns.append(
                jnp.einsum(
                    "nr,nc->rc", left_act, mlp_all[modality], preferred_element_type=jnp.float32
                )
            )
        return jnp.concatenate(columns, axis=-1)

    width_rows = model_width // replica_count
    hidden_rows = fc2_w.shape[1] * lax.axis_size("fsdp") // replica_count
    width_total = reduce_rows(width_term, width_rows)
    hidden_total = reduce_rows(hidden_term, hidden_rows)
    width_split = width_total.reshape(width_rows, 2, -1).transpose(1, 0, 2)
    proj_grad = width_split[..., :model_width]
    qkv_grad = width_split[..., model_width : 4 * model_width]
    fc1_grad = width_split[..., 4 * model_width :]
    fc2_grad = hidden_total.reshape(hidden_rows, 2, model_width).transpose(1, 0, 2)
    gain_grad = lax.psum(gain_gradient, ("fsdp", "seq"))
    img_out = jnp.concatenate(out_parts[0], axis=0)
    txt_out = jnp.concatenate(out_parts[1], axis=0)
    img_grad = jnp.concatenate(in_grads[0], axis=0)
    txt_grad = jnp.concatenate(in_grads[1], axis=0)
    mod_local = jnp.stack(
        [jnp.concatenate(mod_grads[0], axis=0), jnp.concatenate(mod_grads[1], axis=0)], axis=1
    )
    mod_total = lax.psum(mod_local.astype(jnp.bfloat16), "seq")
    every_mod = lax.all_gather(mod_total, "fsdp", axis=0, tiled=True)
    out_rows = model_width // replica_count
    own_cols = lax.dynamic_slice_in_dim(
        every_cond, lax.axis_index(("fsdp", "seq")) * out_rows, out_rows, 1
    )
    ada_grad = jnp.einsum("sr,stm->trm", own_cols, every_mod, preferred_element_type=jnp.float32)
    cond_part = jnp.einsum("stm,tdm->sd", every_mod, ada_w, preferred_element_type=jnp.float32)
    cond_full = lax.all_to_all(cond_part, "fsdp", split_axis=0, concat_axis=1, tiled=True)
    _, silu_pull = jax.vjp(jax.nn.silu, cond.astype(jnp.float32))
    cond_grad = silu_pull(cond_full)[0]
    return (
        img_out,
        txt_out,
        img_grad,
        txt_grad,
        cond_grad,
        ada_grad,
        qkv_grad,
        proj_grad,
        fc1_grad,
        fc2_grad,
        gain_grad,
    )


def solution(mesh):
    in_specs = (
        P("fsdp", "seq", None),
        P("fsdp", "seq", None),
        P("fsdp", None),
        P("fsdp", None),
        P(None, "fsdp", None),
        P(None, "fsdp", None),
        P(None, "fsdp", None),
        P(None, "fsdp", None),
        P(None, "fsdp", None),
        P(),
        P("fsdp", "seq", None),
        P("fsdp", "seq", None),
    )
    out_specs = (
        P("fsdp", "seq", None),
        P("fsdp", "seq", None),
        P("fsdp", "seq", None),
        P("fsdp", "seq", None),
        P("fsdp", None),
        P(None, ("fsdp", "seq"), None),
        P(None, ("fsdp", "seq"), None),
        P(None, ("fsdp", "seq"), None),
        P(None, ("fsdp", "seq"), None),
        P(None, ("fsdp", "seq"), None),
        P(),
    )
    return jax.shard_map(body, mesh=mesh, in_specs=in_specs, out_specs=out_specs, check_vma=False)
```

profile of v0, /device:TPU:0, one launch (start us, length us, event | category | flops | bytes accessed | tf_op | source)
XLA Modules:
  0.0 4504.1 jit_solution(5044231636964697243)
XLA Ops:
  8.1 24.9 all-gather
  56.1 77.9 %all-reduce.15.cloned.1.call-done = f32[32,2,9216]{2,0,1:T(8,128)} async-done(((f32[32,2,9216]{2,0,1:T(8,128)}), f32[32,2,9216]{2,0,1:T(8,128)}) %all-reduce.15.cloned.1.call-update) | async-done | bytes 2359312
  145.1 132.9 %all-gather.7.cloned.1.call-done = bf16[2,1536,4608]{2,1,0:T(8,128)(2,1)} async-done(((bf16[2,96,4608]{2,1,0:T(8,128)(2,1)}), bf16[2,1536,4608]{2,1,0:T(8,128)(2,1)}) %all-gather.7.cloned.1.call-update) | async-done | bytes 28311568 | tf_op jit(solution)/shard_map/all_gather | solution.py:134
  416.4 80.7 %all-to-all-done = bf16[1,3,593,1536]{2,1,0,3:T(4,128)(2,1)} async-done(((bf16[1,3,593,1536]{2,1,0,3:T(4,128)(2,1)}), bf16[1,3,593,1536]{2,1,0,3:T(4,128)(2,1)}, u32[]{:S(2)}, u32[]{:S(2)}) %all-to-all-start) | async-done | bytes 5465120 | tf_op jit(solution)/shard_map/all_to_all | solution.py:176
  529.2 31.3 fusion.386
  560.6 25.5 fusion.2
  586.0 28.7 fusion.97
  766.9 20.5 multiply_convert_fusion.3
  787.4 21.7 fusion.20
  901.0 21.1 all-to-all-done.4
  951.0 27.0 fusion.102
  978.0 47.9 %multiply_reduce_fusion.1 = (f32[12,1186]{1,0:T(8,128)}, f32[12,1186,1186]{1,2,0:T(8,128)}) fusion(f32[12,1186,1186]{1,2,0:T(8,128)} %get-tuple-element.347, f32[12,1186]{1,0:T(8,128)} %log_add_fusion.1, bf16[1186,12,64]{0,2,1:T(8,128)(2,1)} %reshape.2738, bf16[1186,12,64]{0,2,1:T(8,128)(2,1)} %squeeze.155), kind=kOutput, calls=%fused_computation.9 | convolution fusion | flops 2211154688 | bytes 138790464 | tf_op jit(solution)/shard_map/while/body/eval_jaxpr/qhe,khe->hqk/dot_general | solution.py:70
  1025.9 58.3 %multiply_convert_fusion.1 = bf16[12,1186,1186]{1,2,0:T(8,128)(2,1)} fusion(f32[12,1186,1186]{1,2,0:T(8,128)} %get-tuple-element.356, f32[12,1186,1186]{1,2,0:T(8,128)} %get-tuple-element.347, f32[12,1186]{1,0:T(8,128)} %get-tuple-element.355, f32[12,1186]{1,0:T(8,128)} %log_add_fusion.1), kind=kLoop, calls=%fused_computation.8 | loop fusion | flops 67516608 | bytes 168905376 | tf_op jit(solution)/shard_map/while/body/eval_jaxpr/convert_element_type | solution.py:74
  1168.4 78.6 %all-to-all-done.5 = bf16[1,3,1186,768]{3,1,0,2:T(4,128)(2,1)} async-done(((bf16[1,3,1186,768]{3,1,0,2:T(4,128)(2,1)}), bf16[1,3,1186,768]{3,1,0,2:T(4,128)(2,1)}, u32[]{:S(2)}, u32[]{:S(2)}) %all-to-all-start.5) | async-done | bytes 5465120 | tf_op jit(solution)/shard_map/all_to_all | solution.py:271
  1407.8 85.6 %all-to-all-done.2 = bf16[1,3,593,1536]{2,1,0,3:T(4,128)(2,1)} async-done(((bf16[1,3,593,1536]{2,1,0,3:T(4,128)(2,1)}), bf16[1,3,593,1536]{2,1,0,3:T(4,128)(2,1)}, u32[]{:S(2)}, u32[]{:S(2)}) %all-to-all-start.2) | async-done | bytes 5465120 | tf_op jit(solution)/shard_map/all_to_all | solution.py:176
  1525.5 29.3 fusion.387
  1554.8 25.1 fusion.3
  1579.9 27.6 fusion.96
  1707.7 20.6 multiply_convert_fusion.2
  1728.3 21.6 fusion.27
  1928.0 27.0 fusion.105
  1955.0 47.9 %multiply_reduce_fusion = (f32[12,1186]{1,0:T(8,128)}, f32[12,1186,1186]{1,2,0:T(8,128)}) fusion(f32[12,1186,1186]{1,2,0:T(8,128)} %get-tuple-element.359, f32[12,1186]{1,0:T(8,128)} %log_add_fusion, bf16[1186,12,64]{0,2,1:T(8,128)(2,1)} %reshape.2743, bf16[1186,12,64]{0,2,1:T(8,128)(2,1)} %squeeze.163), kind=kOutput, calls=%fused_computation.6 | convolution fusion | flops 2211154688 | bytes 138790464 | tf_op jit(solution)/shard_map/while/body/eval_jaxpr/qhe,khe->hqk/dot_general | solution.py:70
  2002.8 58.3 %multiply_convert_fusion = bf16[12,1186,1186]{1,2,0:T(8,128)(2,1)} fusion(f32[12,1186,1186]{1,2,0:T(8,128)} %get-tuple-element.370, f32[12,1186,1186]{1,2,0:T(8,128)} %get-tuple-element.359, f32[12,1186]{1,0:T(8,128)} %get-tuple-element.369, f32[12,1186]{1,0:T(8,128)} %log_add_fusion), kind=kLoop, calls=%fused_computation.5 | loop fusion | flops 67516608 | bytes 168905376 | tf_op jit(solution)/shard_map/while/body/eval_jaxpr/convert_element_type | solution.py:74
  2143.7 28.2 fusion.31
  2171.9 48.5 %all-to-all-done.7 = bf16[1,3,1186,768]{3,1,0,2:T(4,128)(2,1)} async-done(((bf16[1,3,1186,768]{3,1,0,2:T(4,128)(2,1)}), bf16[1,3,1186,768]{3,1,0,2:T(4,128)(2,1)}, u32[]{:S(2)}, u32[]{:S(2)}) %all-to-all-start.7) | async-done | bytes 5465120 | tf_op jit(solution)/shard_map/all_to_all | solution.py:271
  2439.1 48.9 %pad_maximum_fusion = f32[6144,3072]{0,1:T(8,128)} fusion(f32[6144,1536]{0,1:T(8,128)} %fusion.190, f32[6144,1536]{0,1:T(8,128)} %fusion.31), kind=kLoop, calls=%fused_computation.4 | loop fusion | flops 18874368 | bytes 150994944 | tf_op jit(solution)/shard_map/concatenate | solution.py:352
  2488.1 73.0 %copy.474 = f32[6144,3072]{1,0:T(8,128)} copy(f32[6144,3072]{0,1:T(8,128)} %pad_maximum_fusion) | data formatting | bytes 150994944
  2575.7 28.9 convolution_dynamic-update-slice_fusion.3
  2604.6 31.5 convolution_dynamic-update-slice_fusion.1
  2698.8 43.2 psum.15
  2767.1 452.8 %reduce-scatter.8.cloned.1.call-done = f32[192,3072]{1,0:T(8,128)} async-done(((f32[6144,3072]{1,0:T(8,128)}), f32[192,3072]{1,0:T(8,128)}) %reduce-scatter.8.cloned.1.call-update) | async-done | bytes 2359312
  3226.7 1264.3 %reduce-scatter.6.cloned.1.call-done = f32[48,24576]{1,0:T(8,128)} async-done(((f32[1536,24576]{1,0:T(8,128)}), f32[48,24576]{1,0:T(8,128)}) %reduce-scatter.6.cloned.1.call-update) | async-done | bytes 4718608 | tf_op jit(solution)/shard_map/reduce_scatter | solution.py:94
  (837 shorter events, 1447.3 us)
Async XLA Ops:
  7.2 27.4 copy-start
  7.2 126.8 %all-reduce.15.cloned.1.call-start = ((), (), s32[]{:S(2)}) async-start(), calls=%async_computation.19 | async-start | bytes 4718592
  37.4 240.6 %all-gather.7.cloned.1.call-start = ((), (), s32[]{:S(2)}) async-start(), calls=%async_computation.11 | async-start | bytes 30081024 | tf_op jit(solution)/shard_map/all_gather | solution.py:134
  38.1 663.8 %all-gather.9.cloned.1.call-start = ((), (), s32[]{:S(2)}) async-start(), calls=%async_computation.12 | async-start | bytes 10027008 | tf_op jit(solution)/shard_map/all_gather | solution.py:135
  38.9 678.7 %all-gather.11.cloned.1.call-start = ((), (), s32[]{:S(2)}) async-start(), calls=%async_computation.13 | async-start | bytes 40108032 | tf_op jit(solution)/shard_map/all_gather | solution.py:136
  39.5 699.0 %all-gather.13.cloned.1.call-start = ((), (), s32[]{:S(2)}) async-start(), calls=%async_computation.14 | async-start | bytes 40108032 | tf_op jit(solution)/shard_map/all_gather | solution.py:137
  44.7 338.5 %copy-start.88 = (f32[1536]{0:T(1024)}, f32[1536]{0:T(1024)S(1)}, u32[]{:S(2)}) copy-start(f32[1536]{0:T(1024)S(1)} %mul.2164) | copy-start | bytes 18436
  46.7 336.4 %copy-start.91 = (f32[1536]{0:T(1024)}, f32[1536]{0:T(1024)S(1)}, u32[]{:S(2)}) copy-start(f32[1536]{0:T(1024)S(1)} %mul.2173) | copy-start | bytes 18436
  403.2 93.8 %all-to-all-start = ((bf16[1,3,593,1536]{2,1,0,3:T(4,128)(2,1)}), bf16[1,3,593,1536]{2,1,0,3:T(4,128)(2,1)}, u32[]{:S(2)}, u32[]{:S(2)}) async-start(bf16[1,3,593,1536]{2,1,0,3:T(4,128)(2,1)} %copy.381), calls=%async_computation | async-start | bytes 15728640 | tf_op jit(solution)/shard_map/all_to_all | solution.py:176
  642.6 25.4 all-to-all-start.1
  766.9 20.5 copy-start.40
  787.4 21.7 copy-start.133
  828.4 20.4 copy-start.138
  828.4 20.4 copy-start.140
  894.8 27.4 all-to-all-start.4
  1159.9 87.2 %all-to-all-start.5 = ((bf16[1,3,1186,768]{3,1,0,2:T(4,128)(2,1)}), bf16[1,3,1186,768]{3,1,0,2:T(4,128)(2,1)}, u32[]{:S(2)}, u32[]{:S(2)}) async-start(bf16[1,3,1186,768]{3,1,0,2:T(4,128)(2,1)} %pad_maximum_fusion.1), calls=%async_computation.5 | async-start | bytes 14573568 | tf_op jit(solution)/shard_map/all_to_all | solution.py:271
  1400.8 92.6 %all-to-all-start.2 = ((bf16[1,3,593,1536]{2,1,0,3:T(4,128)(2,1)}), bf16[1,3,593,1536]{2,1,0,3:T(4,128)(2,1)}, u32[]{:S(2)}, u32[]{:S(2)}) async-start(bf16[1,3,593,1536]{2,1,0,3:T(4,128)(2,1)} %copy.395), calls=%async_computation.2 | async-start | bytes 15728640 | tf_op jit(solution)/shard_map/all_to_all | solution.py:176
  1634.9 24.7 all-to-all-start.3
  1707.7 20.6 copy-start.41
  1707.7 20.6 copy-start.46
  1750.0 19.9 copy-start.124
  1875.2 23.9 all-to-all-start.6
  2137.1 83.3 %all-to-all-start.7 = ((bf16[1,3,1186,768]{3,1,0,2:T(4,128)(2,1)}), bf16[1,3,1186,768]{3,1,0,2:T(4,128)(2,1)}, u32[]{:S(2)}, u32[]{:S(2)}) async-start(bf16[1,3,1186,768]{3,1,0,2:T(4,128)(2,1)} %pad_maximum_fusion.2), calls=%async_computation.7 | async-start | bytes 14573568 | tf_op jit(solution)/shard_map/all_to_all | solution.py:271
  2143.7 293.8 %all-reduce.13.cloned.1.call-start = ((), (), s32[]{:S(2)}) async-start(), calls=%async_computation.15 | async-start | bytes 147456 | tf_op jit(solution)/shard_map/psum | solution.py:371
  2417.5 330.5 %all-gather.15.cloned.1.call-start = ((), (), s32[]{:S(2)}) async-start(), calls=%async_computation.16 | async-start | bytes 1253376 | tf_op jit(solution)/shard_map/all_gather | solution.py:372
  2439.1 780.8 %reduce-scatter.8.cloned.1.call-start = ((), (), s32[]{:S(2)}) async-start(), calls=%async_computation.18 | async-start | bytes 77856768
  2561.1 1929.9 %reduce-scatter.6.cloned.1.call-start = ((), (), s32[]{:S(2)}) async-start(), calls=%async_computation.17 | async-start | bytes 155713536 | tf_op jit(solution)/shard_map/reduce_scatter | solution.py:94
  2604.6 31.6 copy-start.54
  2604.6 31.6 copy-start.55
  2604.6 31.6 copy-start.57
  2604.6 31.6 copy-start.59
  2751.3 12.4 all-to-all-start.8
  (199 other events, 1315.8 us)
Sparse Core Ops, SparseCore 0:
  37.5 96.4 all-reduce.14
  135.5 142.3 all-gather.6
  280.3 81.4 all-gather.8
  363.2 185.9 all-gather.10
  550.6 187.7 all-gather.12
  2417.7 19.7 all-reduce.12
  2439.8 38.5 all-gather.14
  2561.2 658.6 reduce-scatter.7
  3227.5 1263.4 reduce-scatter.5
where the time goes:
time: 4520 us; the launch traced here: 4500 us
  waiting for transfers between devices  2290 us (51%)
  matrix products  878 us (19%)
  local copies, waits for them, and re-layouts  674 us (15%)
  other arithmetic  520 us (12%)
  blocking collectives  68.1 us (2%)
  starting transfers between devices  52 us (1%)
    reduce_scatter x1, waiting for transfers between devices, reduce_rows(): lax.psum_scatter(row_term(jnp.int32(0), lax.axis_size(('fsdp', 'seq')) *...  1260 us
    unnamed x11, waiting for transfers between devices  533 us
    unnamed x463, local copies, waits for them, and re-layouts  168 us
    all_to_all x2, waiting for transfers between devices, body(): lax.all_to_all(joint_qkv, 'seq', split_axis=3, concat_axis=2, tiled=True)  166 us
    all_gather x1, waiting for transfers between devices, body(): lax.all_gather(qkv_w, 'fsdp', axis=1, tiled=True)  133 us
    all_to_all x2, waiting for transfers between devices, body(): lax.all_to_all(qkv_grad_heads, 'seq', split_axis=2, concat_axis=3, tiled=...  127 us
    convert_element_type x2, other arithmetic, attend_back(): score_grad = (probabilities * (prob_grad - row_delta)).astype(jnp.bfloat16)  117 us
    dot_general x2, matrix products, attend_back(): jnp.einsum('qhe,khe->hqk', grad_heads, value_heads, preferred_element_typ...  95.7 us
  transfers between devices with their start and end apart: 18, of which 15 were waited for; matrix products, arithmetic and copies ran while one was open for 16% of the time, Pallas kernels for 0%

commit v1 on v0

v1 whole, which is shorter than its diff:
```python
import math

import jax
import jax.numpy as jnp
from jax import lax
from jax.experimental import pallas as pl
from jax.experimental.pallas import tpu as pltpu
from jax.sharding import PartitionSpec as P

HEAD = 64
LANES = 128
BLOCK = 256
BF16 = jnp.bfloat16
F32 = jnp.float32
SCALE = HEAD**-0.5
SCALE2 = SCALE * math.log2(math.e)
VMEM_LIMIT = 56 * 1024 * 1024
NT = (((1,), (1,)), ((), ()))
NN = (((1,), (0,)), ((), ()))


def dot(left, right, dims=NN):
    return lax.dot_general(left, right, dims, preferred_element_type=F32)


def low_lanes():
    return lax.broadcasted_iota(jnp.int32, (1, LANES), 1) < HEAD


def head_mean(values):
    low = low_lanes()
    first = jnp.sum(jnp.where(low, values, 0.0), axis=-1, keepdims=True)
    second = jnp.sum(jnp.where(low, 0.0, values), axis=-1, keepdims=True)
    return jnp.where(low, first, second) * (1.0 / HEAD)


def rms(values):
    return lax.rsqrt(head_mean(values * values) + 1e-06)


def blocks_of(total, size):
    return [(start, min(size, total - start)) for start in range(0, total, size)]


def attend_kernel(rows, img_total, *refs):
    count = len(rows)
    raw, refs = refs[: 3 * count], refs[3 * count :]
    gain_ref, live_ref = refs[:2]
    out, refs = refs[2 : 2 + count], refs[2 + count :]
    norm_ref, q_s, k0_s, k1_s, v0_s, v1_s, o_s = refs
    low = low_lanes()
    offset = 0
    for i, size in enumerate(rows):
        text = offset >= img_total
        place = pl.ds(offset, size)
        gain = 2 if text else 0
        query, key, value = (raw[3 * i + part][0] for part in range(3))
        q_s[place, :] = (query * rms(query) * gain_ref[gain : gain + 1, :]).astype(BF16)
        key = key * rms(key) * gain_ref[gain + 1 : gain + 2, :]
        k0_s[place, :] = jnp.where(low, key, 0.0).astype(BF16)
        k1_s[place, :] = jnp.where(low, 0.0, key).astype(BF16)
        if text:
            live = live_ref[0, pl.ds(offset - img_total, size), :]
            value = value * live
        else:
            live = jnp.ones_like(value)
        v0_s[place, :] = jnp.where(low, value, live).astype(BF16)
        v1_s[place, :] = jnp.where(low, live, value).astype(BF16)
        offset += size

    def block(start, size):
        place = pl.ds(start, size)
        query = q_s[place, :]
        sums = []
        for key_ref, value_ref in ((k0_s, v0_s), (k1_s, v1_s)):
            weights = jnp.exp2(dot(query, key_ref[...], NT) * SCALE2).astype(BF16)
            sums.append(dot(weights, value_ref[...]))
        top = jnp.where(low, sums[0], sums[1])
        bottom = pltpu.roll(jnp.where(low, sums[1], sums[0]), HEAD, 1)
        o_s[place, :] = (top / bottom).astype(BF16)
        turned = jnp.log2(bottom).T
        norm_ref[0, 0, 0:8, place] = turned[0:8]
        norm_ref[0, 0, 8:16, place] = turned[HEAD : HEAD + 8]

    def step(i, carry):
        block(pl.multiple_of(i * BLOCK, BLOCK), BLOCK)
        return carry

    lax.fori_loop(0, img_total // BLOCK, step, 0)
    for start, size in blocks_of(offset - img_total, BLOCK):
        block(img_total + start, size)
    offset = 0
    for i, size in enumerate(rows):
        out[i][0] = o_s[pl.ds(offset, size), :]
        offset += size


def attend_back_kernel(rows, img_total, width, *refs):
    count = len(rows)
    raw, refs = refs[: 3 * count], refs[3 * count :]
    grad, refs = refs[:count], refs[count:]
    done, refs = refs[:count], refs[count:]
    norm_ref, gain_ref, live_ref = refs[:3]
    out, refs = refs[3 : 3 + count], refs[3 + count :]
    gain_out, q_s, k_s, v_s, kt_s, do_s, o_s, dq_s, dk_s, dv_s = refs
    low = low_lanes()
    pair = pl.program_id(1)
    offset = 0
    for i, size in enumerate(rows):
        text = offset >= img_total
        place = pl.ds(offset, size)
        gain = 2 if text else 0
        query, key, value = (raw[3 * i + part][0] for part in range(3))
        q_s[place, :] = (query * rms(query) * gain_ref[gain : gain + 1, :]).astype(BF16)
        key = (key * rms(key) * gain_ref[gain + 1 : gain + 2, :]).astype(BF16)
        k_s[place, :] = key
        v_s[place, :] = value.astype(BF16)
        do_s[place, :] = grad[i][0]
        o_s[place, :] = done[i][0]
        offset += size
    total = offset
    key_blocks = blocks_of(img_total, BLOCK) + [
        (img_total + start, size) for start, size in blocks_of(total - img_total, BLOCK)
    ]
    for start, size in key_blocks:
        key = k_s[pl.ds(start, size), :].astype(F32)
        if start >= img_total:
            key = key * live_ref[0, pl.ds(start - img_total, size), :]
        kt_s[:, pl.ds(start, size)] = key.T.astype(BF16)
    dk_s[...] = jnp.zeros_like(dk_s)
    dv_s[...] = jnp.zeros_like(dv_s)

    def block(start, size):
        place = pl.ds(start, size)
        query = q_s[place, :]
        grads = do_s[place, :]
        both = (grads.astype(F32) * o_s[place, :].astype(F32)).T
        turned = []
        for h in range(2):
            delta = jnp.sum(both[h * HEAD : (h + 1) * HEAD], axis=0, keepdims=True)
            norm = norm_ref[0, 0, 8 * h : 8 * h + 1, place]
            own = low if h == 0 else jnp.logical_not(low)
            query_h = jnp.where(own, query, jnp.zeros_like(query))
            grads_h = jnp.where(own, grads, jnp.zeros_like(grads))
            total_t = jnp.zeros((HEAD, size), F32)
            for key_start, key_size in key_blocks:
                keys = pl.ds(key_start, key_size)
                prob = jnp.exp2(dot(k_s[keys, :], query_h, NT) * SCALE2 - norm)
                prob_grad = dot(v_s[keys, :], grads_h, NT)
                score_grad = (prob * (prob_grad - delta)).astype(BF16)
                dv_s[keys, :] += dot(prob.astype(BF16), grads_h)
                dk_s[keys, :] += dot(score_grad, query_h)
                total_t += dot(kt_s[h * HEAD : (h + 1) * HEAD, keys], score_grad)
            turned.append(total_t)
        dq_s[place, :] = jnp.concatenate(turned, axis=0).T

    def step(i, carry):
        block(pl.multiple_of(i * BLOCK, BLOCK), BLOCK)
        return carry

    lax.fori_loop(0, img_total // BLOCK, step, 0)
    for start, size in blocks_of(total - img_total, BLOCK):
        block(img_total + start, size)

    gain_sums = [jnp.zeros((1, LANES), F32) for _ in range(4)]
    offset = 0
    for i, size in enumerate(rows):
        text = offset >= img_total
        place = pl.ds(offset, size)
        value_grad = dv_s[place, :]
        key_grad = dk_s[place, :]
        if text:
            live = live_ref[0, pl.ds(offset - img_total, size), :]
            value_grad = value_grad * live
            key_grad = key_grad * live
        for part, change in enumerate((dq_s[place, :], key_grad)):
            row = (2 if text else 0) + part
            change = (change * SCALE).astype(BF16).astype(F32)
            values = raw[3 * i + part][0]
            root = rms(values)
            unit = values * root
            gain_sums[row] += jnp.sum(change * unit, axis=0, keepdims=True)
            change = change * gain_ref[row : row + 1, :]
            change = root * (change - unit * head_mean(change * unit))
            column = pl.multiple_of(part * width + pair * LANES, LANES)
            out[i][0, :, pl.ds(column, LANES)] = change.astype(BF16)
        column = pl.multiple_of(2 * width + pair * LANES, LANES)
        out[i][0, :, pl.ds(column, LANES)] = value_grad.astype(BF16)
        offset += size
    for row in range(4):
        gain_out[0, 0, row : row + 1, :] = gain_sums[row]
    gain_out[0, 0, 4:8, :] = jnp.zeros((4, LANES), F32)


def raw_specs(rows, pairs):
    return [
        pl.BlockSpec((1, size, LANES), lambda s, p, part=part: (s, 0, part * pairs + p))
        for size in rows
        for part in range(3)
    ]


def head_specs(rows):
    return [pl.BlockSpec((1, size, LANES), lambda s, p: (s, 0, p)) for size in rows]


def attend(raw, gains, live, img_total):
    sequences, _, triple = raw[0].shape
    width = triple // 3
    pairs = width // LANES
    rows = [piece.shape[1] for piece in raw]
    total = sum(rows)

    def kernel(*refs):
        attend_kernel(rows, img_total, *refs)

    work = sequences * pairs * 2 * total * total
    outputs = pl.pallas_call(
        kernel,
        grid=(sequences, pairs),
        in_specs=raw_specs(rows, pairs)
        + [
            pl.BlockSpec((4, LANES), lambda s, p: (0, 0)),
            pl.BlockSpec((1, total - img_total, LANES), lambda s, p: (s, 0, 0)),
        ],
        out_specs=head_specs(rows) + [pl.BlockSpec((1, 1, 16, total), lambda s, p: (s, p, 0, 0))],
        out_shape=[jax.ShapeDtypeStruct((sequences, size, width), BF16) for size in rows]
        + [jax.ShapeDtypeStruct((sequences, pairs, 16, total), F32)],
        scratch_shapes=[pltpu.VMEM((total, LANES), BF16)] * 6,
        compiler_params=pltpu.CompilerParams(vmem_limit_bytes=VMEM_LIMIT),
        cost_estimate=pl.CostEstimate(
            flops=work * 4 * LANES, bytes_accessed=sequences * total * width * 14, transcendentals=work
        ),
        name="attend",
    )(*[piece for piece in raw for _ in range(3)], gains, live)
    return (outputs[:-1], outputs[-1])


def attend_back(raw, grads, done, norm, gains, live, img_total):
    sequences, _, triple = raw[0].shape
    width = triple // 3
    pairs = width // LANES
    rows = [piece.shape[1] for piece in raw]
    total = sum(rows)

    def kernel(*refs):
        attend_back_kernel(rows, img_total, width, *refs)

    work = sequences * pairs * 2 * total * total
    outputs = pl.pallas_call(
        kernel,
        grid=(sequences, pairs),
        in_specs=raw_specs(rows, pairs)
        + head_specs(rows)
        + head_specs(rows)
        + [
            pl.BlockSpec((1, 1, 16, total), lambda s, p: (s, p, 0, 0)),
            pl.BlockSpec((4, LANES), lambda s, p: (0, 0)),
            pl.BlockSpec((1, total - img_total, LANES), lambda s, p: (s, 0, 0)),
        ],
        out_specs=[pl.BlockSpec((1, size, triple), lambda s, p: (s, 0, 0)) for size in rows]
        + [pl.BlockSpec((1, 1, 8, LANES), lambda s, p: (s, p, 0, 0))],
        out_shape=[jax.ShapeDtypeStruct((sequences, size, triple), BF16) for size in rows]
        + [jax.ShapeDtypeStruct((sequences, pairs, 8, LANES), F32)],
        scratch_shapes=[pltpu.VMEM((total, LANES), BF16)] * 3
        + [pltpu.VMEM((LANES, total), BF16)]
        + [pltpu.VMEM((total, LANES), BF16)] * 2
        + [pltpu.VMEM((total, LANES), F32)] * 3,
        compiler_params=pltpu.CompilerParams(vmem_limit_bytes=VMEM_LIMIT),
        cost_estimate=pl.CostEstimate(
            flops=work * 10 * LANES, bytes_accessed=sequences * total * width * 22, transcendentals=work
        ),
        name="attend_back",
    )(*[piece for piece in raw for _ in range(3)], *grads, *done, norm, gains, live)
    return (outputs[:-1], outputs[-1])


def shift_seq(values, amount):
    members = lax.axis_size("seq")
    return lax.ppermute(values, "seq", [(i, (i + amount) % members) for i in range(members)])


def gather_seq(values):
    return [values] + [shift_seq(values, k) for k in range(1, lax.axis_size("seq"))]


def sum_seq(parts):
    total = parts[0]
    for k in range(1, len(parts)):
        total = total + shift_seq(parts[k].astype(BF16), -k).astype(F32)
    return total


def pick(values, index, axis):
    return lax.dynamic_index_in_dim(values, index, axis, keepdims=False)


def reduce_fsdp(values):
    size = lax.axis_size("fsdp")
    me = lax.axis_index("fsdp")
    terms = [values]
    bit = 1
    while bit < size:
        mine = (me // bit) % 2
        halves = [t.reshape((t.shape[0] // 2, 2) + t.shape[1:]) for t in terms]
        away = sum(pick(t, 1 - mine, 1).astype(F32) for t in halves).astype(BF16)
        swap = [(i, i ^ bit) for i in range(size)]
        came = lax.ppermute(away, "fsdp", swap)
        terms = [pick(t, mine, 1) for t in halves] + [came]
        bit *= 2
    return sum(t.astype(F32) for t in terms)[0]


def rows_to_members(values):
    members = lax.axis_size("seq")
    me = lax.axis_index("seq")
    blocks = values.reshape((members, values.shape[0] // members) + values.shape[1:])
    parts = [pick(blocks, me, 0)]
    for k in range(1, members):
        parts.append(shift_seq(pick(blocks, (me + k) % members, 0), k))
    return [pick(jnp.stack(parts), (me - i) % members, 0) for i in range(members)]


def statistics(values):
    average = jnp.mean(values, axis=-1, keepdims=True)
    centred = values - average
    return (average, lax.rsqrt(jnp.mean(centred * centred, axis=-1, keepdims=True) + 1e-06))


def norm_back(grad, unit, root):
    return root * (
        grad
        - jnp.mean(grad, axis=-1, keepdims=True)
        - unit * jnp.mean(grad * unit, axis=-1, keepdims=True)
    )


def times(left, right):
    return lax.dot_general(left, right, (((2,), (0,)), ((), ())), preferred_element_type=F32)


def times_t(left, right):
    return lax.dot_general(left, right, (((2,), (1,)), ((), ())), preferred_element_type=F32)


def outer(lefts, rights):
    total = 0.0
    for left, right in zip(lefts, rights):
        total = total + lax.dot_general(
            left, right, (((0, 1), (0, 1)), ((), ())), preferred_element_type=F32
        )
    return total.astype(BF16)


def gelu_tanh(values):
    return jax.nn.gelu(values, approximate=True)


def pad_rows(values, rows):
    return jnp.pad(values, ((0, 0), (0, rows - values.shape[1]), (0, 0)))


def body(
    img_in, txt_in, cond, text_counts, ada_w, qkv_w, proj_w, fc1_w, fc2_w, qk_gain, img_cot, txt_cot
):
    members = lax.axis_size("seq")
    member = lax.axis_index("seq")
    shards = lax.axis_size("fsdp")
    sequences, img_local, width = img_in.shape
    slots = txt_in.shape[1]
    padded = -(-slots // 16) * 16
    img_total = members * img_local
    head_width = width // members
    head_padded = -(-head_width // LANES) * LANES
    hidden_width = fc1_w.shape[2]
    shard_rows = ada_w.shape[1]

    own_qkv = pick(qkv_w.reshape(2, shard_rows, 3, members, head_width), member, 3)
    if head_padded > head_width:
        own_qkv = jnp.pad(own_qkv, ((0, 0), (0, 0), (0, 0), (0, head_padded - head_width)))
    own_qkv = own_qkv.reshape(2, shard_rows, 3 * head_padded)
    unit_rows = hidden_width // (shards * members)
    own_fc1 = pick(fc1_w.reshape(2, shard_rows, shards, members, unit_rows), member, 3)
    own_fc1 = own_fc1.reshape(2, shard_rows, shards * unit_rows)
    own_fc2 = pick(fc2_w.reshape(2, members, unit_rows, width), member, 1)
    w_qkv = lax.all_gather(own_qkv, "fsdp", axis=1, tiled=True)
    w_proj = lax.all_gather(proj_w, "fsdp", axis=1, tiled=True)
    w_fc1 = lax.all_gather(own_fc1, "fsdp", axis=1, tiled=True)
    w_fc2 = lax.all_gather(own_fc2, "fsdp", axis=1, tiled=True)

    cond_act = jax.nn.silu(cond.astype(F32)).astype(BF16)
    cond_cols = lax.all_to_all(
        cond_act.reshape(sequences, shards, shard_rows), "fsdp", split_axis=1, concat_axis=0, tiled=True
    ).reshape(shards * sequences, shard_rows)
    mod_width = ada_w.shape[2]
    share = mod_width // members
    own_ada = lax.dynamic_slice_in_dim(ada_w, member * share, share, 2)
    mod_part = jnp.einsum("sd,tdm->stm", cond_cols, own_ada, preferred_element_type=F32)
    mod_part = mod_part.reshape(shards, sequences, 2, share)
    mod_sum = jnp.sum(
        lax.all_to_all(mod_part, "fsdp", split_axis=0, concat_axis=0, tiled=True), axis=0
    )
    mod_shares = jnp.stack(gather_seq(mod_sum))
    modulation = jnp.concatenate(
        [pick(mod_shares, (member - i) % members, 0) for i in range(members)], axis=-1
    )

    counts = jnp.stack([pick(text_counts, (member - k) % members, 1) for k in range(members)], axis=1)
    slot_ids = lax.broadcasted_iota(jnp.int32, (sequences, members, padded), 2)
    live = (slot_ids < counts[:, :, None]).astype(F32)
    text_rows = live[:, 0, :, None]
    live_lanes = jnp.broadcast_to(
        live.reshape(sequences, members * padded, 1), (sequences, members * padded, LANES)
    )
    gains = jnp.tile(qk_gain.reshape(4, HEAD), (1, 2))

    inputs = (img_in.astype(F32), pad_rows(txt_in, padded).astype(F32))
    out_grads = (img_cot.astype(F32), pad_rows(txt_cot, padded).astype(F32) * text_rows)
    pieces = [
        [piece[:, None, :] for piece in jnp.split(modulation[:, t], 6, axis=-1)] for t in range(2)
    ]

    normed_in, in_stats = [], []
    for t in range(2):
        average, root = statistics(inputs[t])
        in_stats.append((average, root))
        shift, scale = pieces[t][0], pieces[t][1]
        normed = (((inputs[t] - average) * root) * (1.0 + scale) + shift).astype(BF16)
        normed_in.append(gather_seq(normed))
    raw = [times(normed_in[t][k], w_qkv[t]) for t in range(2) for k in range(members)]
    attended, norm = attend(raw, gains, live_lanes, img_total)
    own_attended = []
    for t in range(2):
        parts = attended[t * members : (t + 1) * members]
        parts = [parts[0]] + [shift_seq(parts[k], -k) for k in range(1, members)]
        parts = [part[..., :head_width] for part in parts]
        own_attended.append(jnp.roll(jnp.concatenate(parts, axis=-1), member * head_width, axis=-1))

    middle, branch, mid_stats, normed_mid, mlp_grad = [], [], [], [], []
    for t in range(2):
        gate = pieces[t][2]
        branch.append(times(own_attended[t], w_proj[t]))
        middle.append(inputs[t] + gate * branch[t])
        average, root = statistics(middle[t])
        mid_stats.append((average, root))
        shift, scale = pieces[t][3], pieces[t][4]
        normed = (((middle[t] - average) * root) * (1.0 + scale) + shift).astype(BF16)
        normed_mid.append(gather_seq(normed))
        mlp_grad.append(gather_seq((pieces[t][5] * out_grads[t]).astype(BF16)))
    outs, mid_grad, fc1_sum, fc2_sum, gate_mlp_grad = [], [], [], [], []
    for t in range(2):
        hidden = [times(normed_mid[t][k], w_fc1[t]) for k in range(members)]
        active = [gelu_tanh(h).astype(BF16) for h in hidden]
        hidden_grad = []
        for k in range(members):
            active_grad = times_t(mlp_grad[t][k], w_fc2[t])
            hidden_grad.append(jax.vjp(gelu_tanh, hidden[k])[1](active_grad)[0].astype(BF16))
        mid_grad.append(sum_seq([times_t(hidden_grad[k], w_fc1[t]) for k in range(members)]))
        mlp_out = sum_seq([times(active[k], w_fc2[t]) for k in range(members)])
        result = middle[t] + pieces[t][5] * mlp_out
        outs.append(result)
        gate_mlp_grad.append(jnp.sum(out_grads[t] * mlp_out, axis=1))
        fc2_sum.append(
            reduce_fsdp(outer(active, mlp_grad[t]).reshape(shards, unit_rows, width))
        )
        fc1_sum.append(
            reduce_fsdp(outer(normed_mid[t], hidden_grad).reshape(shards, shard_rows, -1))
        )
    img_out = outs[0].astype(BF16)
    txt_out = (outs[1] * text_rows).astype(BF16)[:, :slots]

    middle_grad, head_grads, proj_sum, mod_grads = [], [], [], []
    for t in range(2):
        average, root = mid_stats[t]
        unit = (middle[t] - average) * root
        scale_mlp_grad = jnp.sum(mid_grad[t] * unit, axis=1)
        shift_mlp_grad = jnp.sum(mid_grad[t], axis=1)
        total = out_grads[t] + norm_back(mid_grad[t] * (1.0 + pieces[t][4]), unit, root)
        middle_grad.append(total)
        gate_attn_grad = jnp.sum(total * branch[t], axis=1)
        mod_grads.append([gate_attn_grad, shift_mlp_grad, scale_mlp_grad, gate_mlp_grad[t]])
        branch_grad = (pieces[t][2] * total).astype(BF16)
        attended_grad = times_t(branch_grad, w_proj[t]).astype(BF16)
        attended_grad = jnp.roll(attended_grad, -member * head_width, axis=-1)
        for k in range(members):
            part = attended_grad[..., k * head_width : (k + 1) * head_width]
            if head_padded > head_width:
                part = jnp.pad(part, ((0, 0), (0, 0), (0, head_padded - head_width)))
            head_grads.append(shift_seq(part, k) if k else part)
        proj_sum.append(
            reduce_fsdp(
                outer([own_attended[t]], [branch_grad]).reshape(shards, shard_rows, width)
            )
        )
    raw_grads, gain_parts = attend_back(
        raw, head_grads, attended, norm, gains, live_lanes, img_total
    )
    raw_grads = [raw_grads[t * members : (t + 1) * members] for t in range(2)]
    qkv_sum, in_grads = [], []
    for t in range(2):
        qkv_sum.append(
            reduce_fsdp(
                outer(normed_in[t], raw_grads[t]).reshape(shards, shard_rows, 3 * head_padded)
            )
        )
        in_grad = sum_seq([times_t(raw_grads[t][k], w_qkv[t]) for k in range(members)])
        average, root = in_stats[t]
        unit = (inputs[t] - average) * root
        scale_attn_grad = jnp.sum(in_grad * unit, axis=1)
        shift_attn_grad = jnp.sum(in_grad, axis=1)
        in_grads.append(middle_grad[t] + norm_back(in_grad * (1.0 + pieces[t][1]), unit, root))
        mod_grads[t] = jnp.concatenate([shift_attn_grad, scale_attn_grad] + mod_grads[t], axis=-1)
    img_grad, txt_grad = in_grads[0], in_grads[1][:, :slots]

    fc2_grad = jnp.stack(fc2_sum)
    fc1_grad, qkv_grad, proj_grad = [], [], []
    for t in range(2):
        parts = rows_to_members(fc1_sum[t])
        parts = [part.reshape(part.shape[0], shards, 1, unit_rows) for part in parts]
        fc1_grad.append(jnp.concatenate(parts, axis=2).reshape(-1, hidden_width))
        parts = rows_to_members(qkv_sum[t])
        parts = [part.reshape(-1, 3, 1, head_padded)[..., :head_width] for part in parts]
        qkv_grad.append(jnp.concatenate(parts, axis=2).reshape(-1, 3 * width))
        blocks = proj_sum[t].reshape(members, -1, width)
        total = pick(blocks, member, 0)
        for k in range(1, members):
            total = total + shift_seq(pick(blocks, (member + k) % members, 0), k)
        proj_grad.append(total)
    fc1_grad, qkv_grad, proj_grad = jnp.stack(fc1_grad), jnp.stack(qkv_grad), jnp.stack(proj_grad)

    gain_own = jnp.sum(gain_parts, axis=(0, 1))[:4]
    gain_own = (gain_own[:, :HEAD] + gain_own[:, HEAD:]).reshape(-1)
    mod_own = jnp.stack(mod_grads, axis=1).reshape(-1)
    both = jnp.concatenate([mod_own, gain_own])
    both = sum(gather_seq(both))
    mod_count = mod_own.shape[0]
    gain_high = both[mod_count:].astype(BF16)
    gain_low = (both[mod_count:] - gain_high.astype(F32)).astype(BF16)
    packed = jnp.concatenate([both[:mod_count].astype(BF16), gain_high, gain_low])[None]
    every = lax.all_gather(packed, "fsdp", axis=0, tiled=True)
    every_mod = every[:, :mod_count].reshape(shards * sequences, 2, mod_width)
    gain_grad = jnp.sum(every[:, mod_count:].astype(F32), axis=0).reshape(2, 2, 2 * HEAD).sum(axis=0)
    out_rows = width // (shards * members)
    own_cols = lax.dynamic_slice_in_dim(cond_cols, member * out_rows, out_rows, 1)
    ada_grad = jnp.einsum("sr,stm->trm", own_cols, every_mod, preferred_element_type=F32)
    cond_part = jnp.einsum("stm,tdm->sd", every_mod, ada_w, preferred_element_type=F32)
    cond_full = lax.all_to_all(cond_part, "fsdp", split_axis=0, concat_axis=1, tiled=True)
    cond_grad = jax.vjp(jax.nn.silu, cond.astype(F32))[1](cond_full)[0]
    return (
        img_out,
        txt_out,
        img_grad,
        txt_grad,
        cond_grad,
        ada_grad,
        qkv_grad,
        proj_grad,
        fc1_grad,
        fc2_grad,
        gain_grad,
    )


def solution(mesh):
    tokens, rows = P("fsdp", "seq", None), P("fsdp", None)
    weight, weight_grad = P(None, "fsdp", None), P(None, ("fsdp", "seq"), None)
    in_specs = (tokens, tokens, rows, rows) + (weight,) * 5 + (P(), tokens, tokens)
    out_specs = (tokens,) * 4 + (rows,) + (weight_grad,) * 5 + (P(),)
    return jax.shard_map(body, mesh=mesh, in_specs=in_specs, out_specs=out_specs, check_vma=False)
```

time: 4520 us -> 1710 us (0.38)
  waiting for transfers between devices: 2290 us -> 487 us
  local copies, waits for them, and re-layouts: 674 us -> 205 us
  matrix products: 878 us -> 478 us
  other arithmetic: 520 us -> 148 us
  Pallas kernels: 0 us -> 242 us
  starting transfers between devices: 52 us -> 126 us
  blocking collectives: 68.1 us -> 0 us
    reduce_scatter x1 -> x0, waiting for transfers between devices: 1260 us -> none  [reduce_rows(): lax.psum_scatter(row_term(jnp.int32(0), lax.axis_size(('fsdp', 'seq')) *...]
    unnamed x11 -> x5, waiting for transfers between devices: 533 us -> 0.76 us
    ppermute x0 -> x56, waiting for transfers between devices: none -> 424 us  [the longest x24 221 us: shift_seq(): lax.ppermute(values, 'seq', [(i, (i + amount) % members) for i in range(m...]
    dot_general x55 -> x45, matrix products: 878 us -> 478 us  [the longest x14 164 us: outer(): lax.dot_general(left, right, (((0, 1), (0, 1)), ((), ())), preferred_elem...]
    all_to_all x8 -> x2, waiting for transfers between devices: 347 us -> 43.8 us  [the longest x1 37.3 us: body(): lax.all_to_all(mod_part, 'fsdp', split_axis=0, concat_axis=0, tiled=True)]
    pallas_call x0 -> x2, Pallas kernels: none -> 242 us  [the longest x1 173 us: attend_back(): pl.pallas_call(kernel, grid=(sequences, pairs), in_specs=raw_specs(rows,...]
    all_to_all x20 -> x2, local copies, waits for them, and re-layouts: 157 us -> 0.6 us  [body(): lax.all_to_all(cond_act.reshape(sequences, shards, shard_rows), 'fsdp', s...]
    reduce_sum x51 -> x10, other arithmetic: 164 us -> 11.1 us  [the longest x2 2.56 us: body(): jnp.sum(every[:, mod_count:].astype(F32), axis=0).reshape(2, 2, 2 * HEAD)]
  transfers between devices with their start and end apart: 18 -> 64, of which waited for: 15 -> 25; matrix products, arithmetic and copies ran while one was open for 16% -> 46% of each run, Pallas kernels for 0% -> 14%
where the time goes in v1:
time: 1710 us; the launch traced here: 1700 us
  waiting for transfers between devices  487 us (28%)
  matrix products  478 us (28%)
  Pallas kernels  242 us (14%)
  local copies, waits for them, and re-layouts  205 us (12%)
  other arithmetic  148 us (9%)
  starting transfers between devices  126 us (7%)
    ppermute x24, waiting for transfers between devices, shift_seq(): lax.ppermute(values, 'seq', [(i, (i + amount) % members) for i in range(m...  221 us
    ppermute x32, waiting for transfers between devices, reduce_fsdp(): came = lax.ppermute(away, 'fsdp', swap)  204 us
    pallas_call x1, Pallas kernels, attend_back(): pl.pallas_call(kernel, grid=(sequences, pairs), in_specs=raw_specs(rows,...  173 us
    dot_general x14, matrix products, outer(): lax.dot_general(left, right, (((0, 1), (0, 1)), ((), ())), preferred_elem...  164 us
    dot_general x14, matrix products, times_t(): lax.dot_general(left, right, (((2,), (1,)), ((), ())), preferred_element_...  163 us
    dot_general x14, matrix products, times(): lax.dot_general(left, right, (((2,), (0,)), ((), ())), preferred_element_...  145 us
    dynamic_slice x26, local copies, waits for them, and re-layouts, pick(): return lax.dynamic_index_in_dim(values, index, axis, keepdims=False)  108 us
    ppermute x32, starting transfers between devices, reduce_fsdp(): came = lax.ppermute(away, 'fsdp', swap)  83 us
  transfers between devices with their start and end apart: 64, of which 25 were waited for; matrix products, arithmetic and copies ran while one was open for 46% of the time, Pallas kernels for 14%

profile of v1, /device:TPU:0, one launch (start us, length us, event | category | flops | bytes accessed | tf_op | source)
XLA Modules:
  0.0 1703.0 jit_solution(523832776913682072)
XLA Ops:
  80.7 37.3 %all-to-all-done.1 = f32[16,2,2,4608]{3,2,1,0:T(2,128)} async-done(((f32[16,2,2,4608]{3,2,1,0:T(2,128)}), f32[16,2,2,4608]{3,2,1,0:T(2,128)}, u32[]{:S(2)}, u32[]{:S(2)}) %all-to-all-start.1) | async-done | bytes 1179680 | tf_op jit(solution)/shard_map/all_to_all | solution.py:401
  182.8 29.8 %collective-permute-done.1 = bf16[2,512,1536]{2,1,0:T(8,128)(2,1)} collective-permute-done((bf16[2,512,1536]{2,1,0:T(8,128)(2,1)}, bf16[2,512,1536]{2,1,0:T(8,128)(2,1)}, u32[]{:S(2)}, u32[]{:S(2)}) %collective-permute-start.1) | collective-permute-done | bytes 3145760 | tf_op jit(solution)/shard_map/ppermute | solution.py:280
  224.7 69.9 %attend.1 = (bf16[2,512,768]{2,1,0:T(8,128)(2,1)}, bf16[2,512,768]{2,1,0:T(8,128)(2,1)}, bf16[2,96,768]{2,1,0:T(8,128)(2,1)}, bf16[2,96,768]{2,1,0:T(8,128)(2,1)}, f32[2,6,16,1216]{3,2,1,0:T(8,128)}) custom-call(f32[2,512,2304]{2,1,0:T(8,128)} %fusion.55.refs_0_.refs_1_.refs_2_, f32[2,512,2304]{2,1,0:T(8,128)} %fusion.55.refs_0_.refs_1_.refs_2_, ...), custom_call_target="tpu_custom_call" | custom-call | flops 18169724928 | bytes 26148864 | tf_op jit(solution)/shard_map/attend/pallas_call | solution.py:218
  298.0 30.7 %collective-permute-done.3 = bf16[2,512,768]{2,1,0:T(8,128)(2,1)} collective-permute-done((bf16[2,512,768]{2,1,0:T(8,128)(2,1)}, bf16[2,512,768]{2,1,0:T(8,128)(2,1)}, u32[]{:S(2)}, u32[]{:S(2)}) %collective-permute-start.3) | collective-permute-done | bytes 1572896 | tf_op jit(solution)/shard_map/ppermute | solution.py:280
  359.5 136.7 %collective-permute-done.6 = bf16[2,96,768]{2,1,0:T(8,128)(2,1)S(1)} collective-permute-done((bf16[2,96,768]{2,1,0:T(8,128)(2,1)S(1)}, bf16[2,96,768]{2,1,0:T(8,128)(2,1)S(1)}, u32[]{:S(2)}, u32[]{:S(2)}) %collective-permute-start.6) | collective-permute-done | bytes 294944 | tf_op jit(solution)/shard_map/ppermute | solution.py:280
  501.9 16.1 fusion.38
  518.0 23.3 %fusion.19 = bf16[2,512,3072]{2,1,0:T(8,128)(2,1)} fusion(f32[2,512,3072]{2,1,0:T(8,128)} %fusion.38, bf16[2,512,1536]{2,1,0:T(8,128)(2,1)} %collective-permute-done.9, bf16[2,1,3072,1536]{3,2,1,0:T(8,128)(2,1)} %all-gather.15.cloned.1.call-done), kind=kOutput, calls=%fused_computation.29 | convolution fusion | flops 9726590976 | bytes 31457280 | tf_op jit(solution)/shard_map/dot_general | solution.py:343
  541.3 15.7 fusion.67
  558.5 16.1 fusion.66
  657.7 15.1 fusion.39
  672.8 19.2 %fusion.176 = f32[3072,1536,1]{1,0,2:T(8,128)} fusion(bf16[2,512,1536]{2,1,0:T(8,128)(2,1)} %fusion.34, f32[2,512,3072]{2,1,0:T(8,128)} %fusion.39), kind=kOutput, calls=%fused_computation.422 | convolution fusion | flops 9691987968 | bytes 34603008 | tf_op jit(solution)/shard_map/dot_general | solution.py:349
  692.0 23.1 %fusion.12 = bf16[2,512,3072]{2,1,0:T(8,128)(2,1)} fusion(f32[2,512,3072]{2,1,0:T(8,128)} %fusion.39, bf16[2,512,1536]{2,1,0:T(8,128)(2,1)} %fusion.34, bf16[2,1,3072,1536]{3,2,1,0:T(8,128)(2,1)} %all-gather.15.cloned.1.call-done), kind=kOutput, calls=%fused_computation.22 | convolution fusion | flops 9726590976 | bytes 31457280 | tf_op jit(solution)/shard_map/dot_general | solution.py:343
  715.0 15.9 fusion.185
  731.0 13.9 fusion
  753.1 21.1 %fusion.1 = bf16[3072,1536]{1,0:T(8,128)(2,1)} fusion(f32[3072,1536,1]{1,0,2:T(8,128)} %fusion.176, bf16[2,512,1536]{2,1,0:T(8,128)(2,1)} %collective-permute-done.9, f32[2,512,3072]{2,1,0:T(8,128)} %fusion.38), kind=kOutput, calls=%fused_computation.3 | convolution fusion | flops 9701425152 | bytes 44040192 | tf_op jit(solution)/shard_map/dot_general | solution.py:349
  786.1 18.1 %fusion.3 = bf16[1536,3072]{1,0:T(8,128)(2,1)} fusion(f32[1536,3072,1]{1,0,2:T(8,128)} %fusion.185, bf16[2,512,1536]{2,1,0:T(8,128)(2,1)} %collective-permute-done.4, bf16[2,512,3072]{2,1,0:T(8,128)(2,1)} %fusion.19), kind=kOutput, calls=%fused_computation.7 | convolution fusion | flops 9673113600 | bytes 37748736 | tf_op jit(solution)/shard_map/dot_general | solution.py:349
  848.2 19.1 %multiply_reduce_fusion = (f32[2,1536]{1,0:T(2,128)}, f32[2,512]{1,0:T(2,128)S(1)}, f32[2,512]{1,0:T(2,128)S(1)}, f32[2,1536]{1,0:T(2,128)}, f32[2,512,1536]{2,1,0:T(8,128)}) fusion(f32[2,512,1536]{2,1,0:T(8,128)S(1)} %bitcast.450, f32[2,512]{1,0:T(2,128)S(1)} %copy-done.94, f32[2,512]{1,0:T(2,128)S(1)} %copy-done.86, f32[2,1536]{1,0:T(2,128)S(1)} %copy-done.74, ...), kind=kOutput, calls=%fused_computation.69 | convolution fusion | flops 9680969728 | bytes 31510528 | tf_op jit(solution)/shard_map/dot_general | solution.py:343
  870.0 24.5 %fusion.35 = (f32[2,1536]{1,0:T(2,128)}, bf16[2,512,1536]{2,1,0:T(8,128)(2,1)}, f32[2,1536]{1,0:T(2,128)}, f32[2,512,1536]{2,1,0:T(8,128)}) fusion(bf16[2,512,1536]{2,1,0:T(8,128)(2,1)} %param.26, f32[2,512,1536]{2,1,0:T(8,128)} %copy-done.3, f32[2,1536]{1,0:T(2,128)} %get-tuple-element.169, f32[2,512,1536]{2,1,0:T(8,128)} %get-tuple-element.177, ...), kind=kOutput, calls=%fused_computation.62 | convolution fusion | flops 9720293376 | bytes 56688640 | tf_op jit(solution)/shard_map/dot_general | solution.py:339
  964.9 172.6 %attend_back.1 = (bf16[2,512,2304]{2,1,0:T(8,128)(2,1)}, bf16[2,512,2304]{2,1,0:T(8,128)(2,1)}, bf16[2,96,2304]{2,1,0:T(8,128)(2,1)}, bf16[2,96,2304]{2,1,0:T(8,128)(2,1)}, f32[2,6,8,128]{3,2,1,0:T(8,128)}) custom-call(f32[2,512,2304]{2,1,0:T(8,128)} %fusion.55.refs_0_.refs_1_.refs_2_, f32[2,512,2304]{2,1,0:T(8,128)} %fusion.55.refs_0_.refs_1_.refs_2_, ...), custom_call_target="tpu_custom_call" | custom-call | flops 45424312320 | bytes 41091072 | tf_op jit(solution)/shard_map/attend_back/pallas_call | solution.py:250
  1158.4 14.9 fusion.184
  1184.3 13.8 fusion.5
  1222.1 14.8 collective-permute-start.35
  1266.8 22.5 %collective-permute-done.29 = bf16[4,96,1536]{2,1,0:T(8,128)(2,1)S(1)} collective-permute-done((bf16[4,96,1536]{2,1,0:T(8,128)(2,1)S(1)}, bf16[4,96,1536]{2,1,0:T(8,128)(2,1)S(1)}, u32[]{:S(2)}, u32[]{:S(2)}) %collective-permute-start.29) | collective-permute-done | bytes 1179680 | tf_op jit(solution)/shard_map/ppermute | solution.py:308
  1293.7 14.6 collective-permute-start.30
  1321.0 18.9 %collective-permute-done.49 = bf16[4,192,1536]{2,1,0:T(8,128)(2,1)S(1)} collective-permute-done((bf16[4,192,1536]{2,1,0:T(8,128)(2,1)S(1)}, bf16[4,192,1536]{2,1,0:T(8,128)(2,1)S(1)}, u32[]{:S(2)}, u32[]{:S(2)}) %collective-permute-start.49) | collective-permute-done | bytes 2359328 | tf_op jit(solution)/shard_map/ppermute | solution.py:308
  1340.0 14.8 collective-permute-start.45
  1383.8 14.5 collective-permute-start.54
  1401.4 15.7 collective-permute-done.40
  1419.0 46.9 %collective-permute-done.54 = bf16[2,192,1536]{2,1,0:T(8,128)(2,1)} collective-permute-done((bf16[2,192,1536]{2,1,0:T(8,128)(2,1)}, bf16[2,192,1536]{2,1,0:T(8,128)(2,1)}, u32[]{:S(2)}, u32[]{:S(2)}) %collective-permute-start.54) | collective-permute-done | bytes 1179680 | tf_op jit(solution)/shard_map/ppermute | solution.py:308
  1467.6 20.1 %collective-permute-done.50 = bf16[2,192,1536]{2,1,0:T(8,128)(2,1)} collective-permute-done((bf16[2,192,1536]{2,1,0:T(8,128)(2,1)}, bf16[2,192,1536]{2,1,0:T(8,128)(2,1)}, u32[]{:S(2)}, u32[]{:S(2)}) %collective-permute-start.50) | collective-permute-done | bytes 1179680 | tf_op jit(solution)/shard_map/ppermute | solution.py:308
  1508.4 20.9 %collective-permute-done.41 = bf16[1,96,3072]{2,1,0:T(8,128)(2,1)S(1)} collective-permute-done((bf16[1,96,3072]{2,1,0:T(8,128)(2,1)S(1)}, bf16[1,96,3072]{2,1,0:T(8,128)(2,1)S(1)}, u32[]{:S(2)}, u32[]{:S(2)}) %collective-permute-start.41) | collective-permute-done | bytes 589856 | tf_op jit(solution)/shard_map/ppermute | solution.py:308
  1641.0 16.8 collective-permute-done.21
  (641 shorter events, 719.7 us)
Async XLA Ops:
  7.2 151.9 %all-gather.9.cloned.1.call-start = ((), (), s32[]{:S(2)}) async-start(), calls=%async_computation.3 | async-start | bytes 15040512 | tf_op jit(solution)/shard_map/all_gather | solution.py:386
  22.9 314.0 %all-gather.11.cloned.1.call-start = ((), (), s32[]{:S(2)}) async-start(), calls=%async_computation.4 | async-start | bytes 10027008 | tf_op jit(solution)/shard_map/all_gather | solution.py:387
  23.6 478.3 %all-gather.13.cloned.1.call-start = ((), (), s32[]{:S(2)}) async-start(), calls=%async_computation.5 | async-start | bytes 20054016 | tf_op jit(solution)/shard_map/all_gather | solution.py:388
  50.2 467.8 %all-gather.15.cloned.1.call-start = ((), (), s32[]{:S(2)}) async-start(), calls=%async_computation.6 | async-start | bytes 20054016 | tf_op jit(solution)/shard_map/all_gather | solution.py:389
  73.9 1519.0 %all-gather.17.cloned.1.call-start = ((), (), s32[]{:S(2)}) async-start(), calls=%async_computation.7 | async-start | bytes 2541568 | tf_op jit(solution)/shard_map/all_gather | solution.py:540
  144.0 68.7 %collective-permute-start.1 = (bf16[2,512,1536]{2,1,0:T(8,128)(2,1)}, bf16[2,512,1536]{2,1,0:T(8,128)(2,1)}, u32[]{:S(2)}, u32[]{:S(2)}) collective-permute-start(bf16[2,512,1536]{2,1,0:T(8,128)(2,1)} %fusion.27), channel_id=1, source_target_pairs={{0,1},{1,0},{2,3},{3,2},{4,5},{5,4},{6,7},{7,6},{8,9},{9,8},{10,11... | collective-permute-start | bytes 9437192 | tf_op jit(solution)/shard_map/ppermute | solution.py:280
  351.3 150.6 %collective-permute-start.4 = (bf16[2,512,1536]{2,1,0:T(8,128)(2,1)S(1)}, bf16[2,512,1536]{2,1,0:T(8,128)(2,1)}, u32[]{:S(2)}, u32[]{:S(2)}) collective-permute-start(bf16[2,512,1536]{2,1,0:T(8,128)(2,1)S(1)} %add_convert_fusion.1), channel_id=1, source_target_pairs={{0,1},{1,0},{2,3},{3,2},{4,5},{5,4},{6,7},{7,6},{8,9},{9,8},{10,11... | collective-permute-start | bytes 9437192 | tf_op jit(solution)/shard_map/ppermute | solution.py:280
  354.8 163.2 %collective-permute-start.9 = (bf16[2,512,1536]{2,1,0:T(8,128)(2,1)}, bf16[2,512,1536]{2,1,0:T(8,128)(2,1)}, u32[]{:S(2)}, u32[]{:S(2)}) collective-permute-start(bf16[2,512,1536]{2,1,0:T(8,128)(2,1)} %fusion.34), channel_id=1, source_target_pairs={{0,1},{1,0},{2,3},{3,2},{4,5},{5,4},{6,7},{7,6},{8,9},{9,8},{10,11... | collective-permute-start | bytes 9437192 | tf_op jit(solution)/shard_map/ppermute | solution.py:280
  356.4 139.8 %collective-permute-start.6 = (bf16[2,96,768]{2,1,0:T(8,128)(2,1)S(1)}, bf16[2,96,768]{2,1,0:T(8,128)(2,1)S(1)}, u32[]{:S(2)}, u32[]{:S(2)}) collective-permute-start(bf16[2,96,768]{2,1,0:T(8,128)(2,1)S(1)} %copy-done.120), channel_id=1, source_target_pairs={{0,1},{1,0},{2,3},{3,2},{4,5},{5,4},{6,7},{7,6},{8,9},{9,8},{10,11... | collective-permute-start | bytes 884744 | tf_op jit(solution)/shard_map/ppermute | solution.py:280
  357.9 223.2 %collective-permute-start.12 = (bf16[2,96,1536]{2,1,0:T(8,128)(2,1)}, bf16[2,96,1536]{2,1,0:T(8,128)(2,1)}, u32[]{:S(2)}, u32[]{:S(2)}) collective-permute-start(bf16[2,96,1536]{2,1,0:T(8,128)(2,1)} %multiply_convert_fusion.8), channel_id=1, source_target_pairs={{0,1},{1,0},{2,3},{3,2},{4,5},{5,4},{6,7},{7,6},{8,9},{9,8},{10,11... | collective-permute-start | bytes 1769480 | tf_op jit(solution)/shard_map/ppermute | solution.py:280
  501.5 73.7 %collective-permute-start.7 = (bf16[2,96,1536]{2,1,0:T(8,128)(2,1)}, bf16[2,96,1536]{2,1,0:T(8,128)(2,1)}, u32[]{:S(2)}, u32[]{:S(2)}) collective-permute-start(bf16[2,96,1536]{2,1,0:T(8,128)(2,1)} %add_convert_fusion.18), channel_id=1, source_target_pairs={{0,1},{1,0},{2,3},{3,2},{4,5},{5,4},{6,7},{7,6},{8,9},{9,8},{10,11... | collective-permute-start | bytes 1769480 | tf_op jit(solution)/shard_map/ppermute | solution.py:280
  557.0 290.8 %collective-permute-start.10 = (bf16[2,512,1536]{2,1,0:T(8,128)(2,1)}, bf16[2,512,1536]{2,1,0:T(8,128)(2,1)}, u32[]{:S(2)}, u32[]{:S(2)}) collective-permute-start(bf16[2,512,1536]{2,1,0:T(8,128)(2,1)} %fusion.67), channel_id=1, source_target_pairs={{0,1},{1,0},{2,3},{3,2},{4,5},{5,4},{6,7},{7,6},{8,9},{9,8},{10,11... | collective-permute-start | bytes 9437192 | tf_op jit(solution)/shard_map/ppermute | solution.py:280
  574.6 293.9 %collective-permute-start.5 = (bf16[2,512,1536]{2,1,0:T(8,128)(2,1)}, bf16[2,512,1536]{2,1,0:T(8,128)(2,1)}, u32[]{:S(2)}, u32[]{:S(2)}) collective-permute-start(bf16[2,512,1536]{2,1,0:T(8,128)(2,1)} %fusion.66), channel_id=1, source_target_pairs={{0,1},{1,0},{2,3},{3,2},{4,5},{5,4},{6,7},{7,6},{8,9},{9,8},{10,11... | collective-permute-start | bytes 9437192 | tf_op jit(solution)/shard_map/ppermute | solution.py:280
  597.4 218.6 %collective-permute-start.13 = (bf16[2,96,1536]{2,1,0:T(8,128)(2,1)}, bf16[2,96,1536]{2,1,0:T(8,128)(2,1)}, u32[]{:S(2)}, u32[]{:S(2)}) collective-permute-start(bf16[2,96,1536]{2,1,0:T(8,128)(2,1)} %fusion.78), channel_id=1, source_target_pairs={{0,1},{1,0},{2,3},{3,2},{4,5},{5,4},{6,7},{7,6},{8,9},{9,8},{10,11... | collective-permute-start | bytes 1769480 | tf_op jit(solution)/shard_map/ppermute | solution.py:280
  605.6 219.7 %collective-permute-start.8 = (bf16[2,96,1536]{2,1,0:T(8,128)(2,1)}, bf16[2,96,1536]{2,1,0:T(8,128)(2,1)}, u32[]{:S(2)}, u32[]{:S(2)}) collective-permute-start(bf16[2,96,1536]{2,1,0:T(8,128)(2,1)} %fusion.77), channel_id=1, source_target_pairs={{0,1},{1,0},{2,3},{3,2},{4,5},{5,4},{6,7},{7,6},{8,9},{9,8},{10,11... | collective-permute-start | bytes 1769480 | tf_op jit(solution)/shard_map/ppermute | solution.py:280
  657.7 275.6 %collective-permute-start.43 = (bf16[8,96,3072]{2,1,0:T(8,128)(2,1)}, bf16[8,96,3072]{2,1,0:T(8,128)(2,1)}, u32[]{:S(2)}, u32[]{:S(2)}) collective-permute-start(bf16[8,96,3072]{2,1,0:T(8,128)(2,1)} %get-tuple-element.124), channel_id=1, source_target_pairs={{0,2},{2,0},{4,6},{6,4},{8,10},{10,8},{12,14},{14,12},{16,18},{18,... | collective-permute-start | bytes 14155784 | tf_op jit(solution)/shard_map/ppermute | solution.py:308
  816.0 128.7 %collective-permute-start.38 = (bf16[8,96,3072]{2,1,0:T(8,128)(2,1)}, bf16[8,96,3072]{2,1,0:T(8,128)(2,1)}, u32[]{:S(2)}, u32[]{:S(2)}) collective-permute-start(bf16[8,96,3072]{2,1,0:T(8,128)(2,1)} %get-tuple-element.122), channel_id=1, source_target_pairs={{0,2},{2,0},{4,6},{6,4},{8,10},{10,8},{12,14},{14,12},{16,18},{18,... | collective-permute-start | bytes 14155784 | tf_op jit(solution)/shard_map/ppermute | solution.py:308
  845.9 74.5 %collective-permute-start.52 = (bf16[8,192,1536]{2,1,0:T(8,128)(2,1)}, bf16[8,192,1536]{2,1,0:T(8,128)(2,1)}, u32[]{:S(2)}, u32[]{:S(2)}) collective-permute-start(bf16[8,192,1536]{2,1,0:T(8,128)(2,1)} %get-tuple-element.120), channel_id=1, source_target_pairs={{0,2},{2,0},{4,6},{6,4},{8,10},{10,8},{12,14},{14,12},{16,18},{18,... | collective-permute-start | bytes 14155784 | tf_op jit(solution)/shard_map/ppermute | solution.py:308
  847.8 80.1 %collective-permute-start.48 = (bf16[8,192,1536]{2,1,0:T(8,128)(2,1)}, bf16[8,192,1536]{2,1,0:T(8,128)(2,1)}, u32[]{:S(2)}, u32[]{:S(2)}) collective-permute-start(bf16[8,192,1536]{2,1,0:T(8,128)(2,1)} %get-tuple-element.118), channel_id=1, source_target_pairs={{0,2},{2,0},{4,6},{6,4},{8,10},{10,8},{12,14},{14,12},{16,18},{18,... | collective-permute-start | bytes 14155784 | tf_op jit(solution)/shard_map/ppermute | solution.py:308
  868.5 87.9 %collective-permute-start.14 = (bf16[2,96,768]{2,1,0:T(8,128)(2,1)}, bf16[2,96,768]{2,1,0:T(8,128)(2,1)}, u32[]{:S(2)}, u32[]{:S(2)}) collective-permute-start(bf16[2,96,768]{2,1,0:T(8,128)(2,1)} %get-tuple-element.155), channel_id=1, source_target_pairs={{0,1},{1,0},{2,3},{3,2},{4,5},{5,4},{6,7},{7,6},{8,9},{9,8},{10,11... | collective-permute-start | bytes 884744 | tf_op jit(solution)/shard_map/ppermute | solution.py:280
  920.4 300.2 %collective-permute-start.34 = (bf16[4,96,1536]{2,1,0:T(8,128)(2,1)}, bf16[4,96,1536]{2,1,0:T(8,128)(2,1)}, u32[]{:S(2)}, u32[]{:S(2)}) collective-permute-start(bf16[4,96,1536]{2,1,0:T(8,128)(2,1)} %fusion.106), channel_id=1, source_target_pairs={{0,4},{2,6},{4,0},{6,2},{8,12},{10,14},{12,8},{14,10},{16,20},{18,... | collective-permute-start | bytes 3538952 | tf_op jit(solution)/shard_map/ppermute | solution.py:308
  933.3 285.7 %collective-permute-start.28 = (bf16[8,96,1536]{2,1,0:T(8,128)(2,1)}, bf16[8,96,1536]{2,1,0:T(8,128)(2,1)}, u32[]{:S(2)}, u32[]{:S(2)}) collective-permute-start(bf16[8,96,1536]{2,1,0:T(8,128)(2,1)} %get-tuple-element.134), channel_id=1, source_target_pairs={{0,2},{2,0},{4,6},{6,4},{8,10},{10,8},{12,14},{14,12},{16,18},{18,... | collective-permute-start | bytes 7077896 | tf_op jit(solution)/shard_map/ppermute | solution.py:308
  944.7 349.0 %collective-permute-start.44 = (bf16[4,96,3072]{2,1,0:T(8,128)(2,1)}, bf16[4,96,3072]{2,1,0:T(8,128)(2,1)}, u32[]{:S(2)}, u32[]{:S(2)}) collective-permute-start(bf16[4,96,3072]{2,1,0:T(8,128)(2,1)} %fusion.94), channel_id=1, source_target_pairs={{0,4},{2,6},{4,0},{6,2},{8,12},{10,14},{12,8},{14,10},{16,20},{18,... | collective-permute-start | bytes 7077896 | tf_op jit(solution)/shard_map/ppermute | solution.py:308
  956.4 354.9 %collective-permute-start.39 = (bf16[4,96,3072]{2,1,0:T(8,128)(2,1)}, bf16[4,96,3072]{2,1,0:T(8,128)(2,1)}, u32[]{:S(2)}, u32[]{:S(2)}) collective-permute-start(bf16[4,96,3072]{2,1,0:T(8,128)(2,1)} %fusion.93), channel_id=1, source_target_pairs={{0,4},{2,6},{4,0},{6,2},{8,12},{10,14},{12,8},{14,10},{16,20},{18,... | collective-permute-start | bytes 7077896 | tf_op jit(solution)/shard_map/ppermute | solution.py:308
  1212.3 106.9 %collective-permute-start.53 = (bf16[4,192,1536]{2,1,0:T(8,128)(2,1)S(1)}, bf16[4,192,1536]{2,1,0:T(8,128)(2,1)S(1)}, u32[]{:S(2)}, u32[]{:S(2)}) collective-permute-start(bf16[4,192,1536]{2,1,0:T(8,128)(2,1)S(1)} %copy-done.49), channel_id=1, source_target_pairs={{0,4},{2,6},{4,0},{6,2},{8,12},{10,14},{12,8},{14,10},{16,20},{18,... | collective-permute-start | bytes 7077896 | tf_op jit(solution)/shard_map/ppermute | solution.py:308
  1311.3 178.7 %collective-permute-start.23 = (bf16[8,96,2304]{2,1,0:T(8,128)(2,1)}, bf16[8,96,2304]{2,1,0:T(8,128)(2,1)}, u32[]{:S(2)}, u32[]{:S(2)}) collective-permute-start(bf16[8,96,2304]{2,1,0:T(8,128)(2,1)} %get-tuple-element.128), channel_id=1, source_target_pairs={{0,2},{2,0},{4,6},{6,4},{8,10},{10,8},{12,14},{14,12},{16,18},{18,... | collective-permute-start | bytes 10616840 | tf_op jit(solution)/shard_map/ppermute | solution.py:308
  1319.1 179.2 %collective-permute-start.18 = (bf16[8,96,2304]{2,1,0:T(8,128)(2,1)}, bf16[8,96,2304]{2,1,0:T(8,128)(2,1)}, u32[]{:S(2)}, u32[]{:S(2)}) collective-permute-start(bf16[8,96,2304]{2,1,0:T(8,128)(2,1)} %get-tuple-element.126), channel_id=1, source_target_pairs={{0,2},{2,0},{4,6},{6,4},{8,10},{10,8},{12,14},{14,12},{16,18},{18,... | collective-permute-start | bytes 10616840 | tf_op jit(solution)/shard_map/ppermute | solution.py:308
  1383.8 82.1 %collective-permute-start.54 = (bf16[2,192,1536]{2,1,0:T(8,128)(2,1)}, bf16[2,192,1536]{2,1,0:T(8,128)(2,1)}, u32[]{:S(2)}, u32[]{:S(2)}) collective-permute-start(bf16[2,192,1536]{2,1,0:T(8,128)(2,1)} %fusion.110), channel_id=1, source_target_pairs={{0,8},{2,10},{4,12},{6,14},{8,0},{10,2},{12,4},{14,6},{16,24},{18,... | collective-permute-start | bytes 3538952 | tf_op jit(solution)/shard_map/ppermute | solution.py:308
  1398.4 89.3 %collective-permute-start.50 = (bf16[2,192,1536]{2,1,0:T(8,128)(2,1)}, bf16[2,192,1536]{2,1,0:T(8,128)(2,1)}, u32[]{:S(2)}, u32[]{:S(2)}) collective-permute-start(bf16[2,192,1536]{2,1,0:T(8,128)(2,1)} %fusion.109), channel_id=1, source_target_pairs={{0,8},{2,10},{4,12},{6,14},{8,0},{10,2},{12,4},{14,6},{16,24},{18,... | collective-permute-start | bytes 3538952 | tf_op jit(solution)/shard_map/ppermute | solution.py:308
  1417.1 88.5 %collective-permute-start.46 = (bf16[1,96,3072]{2,1,0:T(8,128)(2,1)S(1)}, bf16[1,96,3072]{2,1,0:T(8,128)(2,1)S(1)}, u32[]{:S(2)}, u32[]{:S(2)}) collective-permute-start(bf16[1,96,3072]{2,1,0:T(8,128)(2,1)S(1)} %fusion.115), channel_id=1, source_target_pairs={{0,16},{2,18},{4,20},{6,22},{8,24},{10,26},{12,28},{14,30},{16,0},... | collective-permute-start | bytes 1769480 | tf_op jit(solution)/shard_map/ppermute | solution.py:308
  1498.3 87.4 %collective-permute-start.24 = (bf16[4,96,2304]{2,1,0:T(8,128)(2,1)}, bf16[4,96,2304]{2,1,0:T(8,128)(2,1)}, u32[]{:S(2)}, u32[]{:S(2)}) collective-permute-start(bf16[4,96,2304]{2,1,0:T(8,128)(2,1)} %fusion.98), channel_id=1, source_target_pairs={{0,4},{2,6},{4,0},{6,2},{8,12},{10,14},{12,8},{14,10},{16,20},{18,... | collective-permute-start | bytes 5308424 | tf_op jit(solution)/shard_map/ppermute | solution.py:308
  1505.6 82.7 %collective-permute-start.19 = (bf16[4,96,2304]{2,1,0:T(8,128)(2,1)}, bf16[4,96,2304]{2,1,0:T(8,128)(2,1)}, u32[]{:S(2)}, u32[]{:S(2)}) collective-permute-start(bf16[4,96,2304]{2,1,0:T(8,128)(2,1)} %fusion.97), channel_id=1, source_target_pairs={{0,4},{2,6},{4,0},{6,2},{8,12},{10,14},{12,8},{14,10},{16,20},{18,... | collective-permute-start | bytes 5308424 | tf_op jit(solution)/shard_map/ppermute | solution.py:308
  (178 other events, 4171.8 us)
Sparse Core Ops, SparseCore 0:
  23.0 136.0 all-gather.8
  161.4 80.3 all-gather.10
  243.9 97.0 all-gather.12
  343.1 98.9 all-gather.14
  1399.4 46.9 all-gather.16

commit v2 on v1

v2 whole, which is shorter than its diff:
```python
import math

import jax
import jax.numpy as jnp
from jax import lax
from jax.experimental import pallas as pl
from jax.experimental.pallas import tpu as pltpu
from jax.sharding import PartitionSpec as P

HEAD = 64
LANES = 128
BLOCK = 512
BF16 = jnp.bfloat16
F32 = jnp.float32
SCALE = HEAD**-0.5
SCALE2 = SCALE * math.log2(math.e)
VMEM_LIMIT = 56 * 1024 * 1024
NT = (((1,), (1,)), ((), ()))
NN = (((1,), (0,)), ((), ()))


def dot(left, right, dims=NN):
    return lax.dot_general(left, right, dims, preferred_element_type=F32)


def low_lanes():
    return lax.broadcasted_iota(jnp.int32, (1, LANES), 1) < HEAD


def head_mean(values):
    low = low_lanes()
    first = jnp.sum(jnp.where(low, values, 0.0), axis=-1, keepdims=True)
    second = jnp.sum(jnp.where(low, 0.0, values), axis=-1, keepdims=True)
    return jnp.where(low, first, second) * (1.0 / HEAD)


def rms(values):
    return lax.rsqrt(head_mean(values * values) + 1e-06)


def blocks_of(total, size):
    return [(start, min(size, total - start)) for start in range(0, total, size)]


def attend_kernel(rows, img_total, *refs):
    count = len(rows)
    raw, refs = refs[: 3 * count], refs[3 * count :]
    gain_ref, live_ref = refs[:2]
    out, refs = refs[2 : 2 + count], refs[2 + count :]
    norm_ref, q_s, k0_s, k1_s, v0_s, v1_s, o_s = refs
    low = low_lanes()
    offset = 0
    for i, size in enumerate(rows):
        text = offset >= img_total
        place = pl.ds(offset, size)
        gain = 2 if text else 0
        query, key, value = (raw[3 * i + part][0] for part in range(3))
        q_s[place, :] = (query * rms(query) * gain_ref[gain : gain + 1, :]).astype(BF16)
        key = key * rms(key) * gain_ref[gain + 1 : gain + 2, :]
        k0_s[place, :] = jnp.where(low, key, 0.0).astype(BF16)
        k1_s[place, :] = jnp.where(low, 0.0, key).astype(BF16)
        if text:
            live = live_ref[0, pl.ds(offset - img_total, size), :]
            value = value * live
        else:
            live = jnp.ones_like(value)
        v0_s[place, :] = jnp.where(low, value, live).astype(BF16)
        v1_s[place, :] = jnp.where(low, live, value).astype(BF16)
        offset += size

    def block(start, size):
        place = pl.ds(start, size)
        query = q_s[place, :]
        sums = []
        for key_ref, value_ref in ((k0_s, v0_s), (k1_s, v1_s)):
            weights = jnp.exp2(dot(query, key_ref[...], NT) * SCALE2).astype(BF16)
            sums.append(dot(weights, value_ref[...]))
        top = jnp.where(low, sums[0], sums[1])
        bottom = pltpu.roll(jnp.where(low, sums[1], sums[0]), HEAD, 1)
        o_s[place, :] = (top / bottom).astype(BF16)
        turned = jnp.log2(bottom).T
        norm_ref[0, 0, 0:8, place] = turned[0:8]
        norm_ref[0, 0, 8:16, place] = turned[HEAD : HEAD + 8]

    def step(i, carry):
        block(pl.multiple_of(i * BLOCK, BLOCK), BLOCK)
        return carry

    lax.fori_loop(0, img_total // BLOCK, step, 0)
    for start, size in blocks_of(offset - img_total, BLOCK):
        block(img_total + start, size)
    offset = 0
    for i, size in enumerate(rows):
        out[i][0] = o_s[pl.ds(offset, size), :]
        offset += size


def attend_back_kernel(rows, img_total, width, *refs):
    count = len(rows)
    raw, refs = refs[: 3 * count], refs[3 * count :]
    grad, refs = refs[:count], refs[count:]
    done, refs = refs[:count], refs[count:]
    norm_ref, gain_ref, live_ref = refs[:3]
    out, refs = refs[3 : 3 + count], refs[3 + count :]
    gain_out, q_s, k_s, v_s, kt_s, do_s, o_s, dq_s, dk_s, dv_s = refs
    low = low_lanes()
    pair = pl.program_id(0)
    offset = 0
    for i, size in enumerate(rows):
        text = offset >= img_total
        place = pl.ds(offset, size)
        gain = 2 if text else 0
        query, key, value = (raw[3 * i + part][0] for part in range(3))
        q_s[place, :] = (query * rms(query) * gain_ref[gain : gain + 1, :]).astype(BF16)
        key = (key * rms(key) * gain_ref[gain + 1 : gain + 2, :]).astype(BF16)
        k_s[place, :] = key
        v_s[place, :] = value.astype(BF16)
        do_s[place, :] = grad[i][0]
        o_s[place, :] = done[i][0]
        offset += size
    total = offset
    key_blocks = blocks_of(img_total, BLOCK) + [
        (img_total + start, size) for start, size in blocks_of(total - img_total, BLOCK)
    ]
    for start, size in key_blocks:
        key = k_s[pl.ds(start, size), :].astype(F32)
        if start >= img_total:
            key = key * live_ref[0, pl.ds(start - img_total, size), :]
        kt_s[:, pl.ds(start, size)] = key.T.astype(BF16)
    dk_s[...] = jnp.zeros_like(dk_s)
    dv_s[...] = jnp.zeros_like(dv_s)

    def block(start, size):
        place = pl.ds(start, size)
        query = q_s[place, :]
        grads = do_s[place, :]
        both = (grads.astype(F32) * o_s[place, :].astype(F32)).T
        side = []
        for h in range(2):
            delta = jnp.sum(both[h * HEAD : (h + 1) * HEAD], axis=0, keepdims=True)
            norm = norm_ref[0, 0, 8 * h : 8 * h + 1, place]
            own = low if h == 0 else jnp.logical_not(low)
            query_h = jnp.where(own, query, jnp.zeros_like(query))
            grads_h = jnp.where(own, grads, jnp.zeros_like(grads))
            side.append((delta, norm, query_h, grads_h))
        probs, changes = [], []
        for delta, norm, query_h, grads_h in side:
            prob = jnp.exp2(dot(k_s[...], query_h, NT) * SCALE2 - norm)
            prob_grad = dot(v_s[...], grads_h, NT)
            changes.append((prob * (prob_grad - delta)).astype(BF16))
            probs.append(prob.astype(BF16))
        dv_s[...] += dot(probs[0], side[0][3]) + dot(probs[1], side[1][3])
        dk_s[...] += dot(changes[0], side[0][2]) + dot(changes[1], side[1][2])
        turned = [dot(kt_s[h * HEAD : (h + 1) * HEAD, :], changes[h]) for h in range(2)]
        dq_s[place, :] = jnp.concatenate(turned, axis=0).T

    def step(i, carry):
        block(pl.multiple_of(i * BLOCK, BLOCK), BLOCK)
        return carry

    lax.fori_loop(0, img_total // BLOCK, step, 0)
    for start, size in blocks_of(total - img_total, BLOCK):
        block(img_total + start, size)

    gain_sums = [jnp.zeros((1, LANES), F32) for _ in range(4)]
    offset = 0
    for i, size in enumerate(rows):
        text = offset >= img_total
        place = pl.ds(offset, size)
        value_grad = dv_s[place, :]
        key_grad = dk_s[place, :]
        if text:
            live = live_ref[0, pl.ds(offset - img_total, size), :]
            value_grad = value_grad * live
            key_grad = key_grad * live
        for part, change in enumerate((dq_s[place, :], key_grad)):
            row = (2 if text else 0) + part
            change = (change * SCALE).astype(BF16).astype(F32)
            values = raw[3 * i + part][0]
            root = rms(values)
            unit = values * root
            gain_sums[row] += jnp.sum(change * unit, axis=0, keepdims=True)
            change = change * gain_ref[row : row + 1, :]
            change = root * (change - unit * head_mean(change * unit))
            column = pl.multiple_of(part * width + pair * LANES, LANES)
            out[i][0, :, pl.ds(column, LANES)] = change.astype(BF16)
        column = pl.multiple_of(2 * width + pair * LANES, LANES)
        out[i][0, :, pl.ds(column, LANES)] = value_grad.astype(BF16)
        offset += size
    for row in range(4):
        gain_out[0, row : row + 1, :] = gain_sums[row]
    gain_out[0, 4:8, :] = jnp.zeros((4, LANES), F32)


def cost(flops, bytes_accessed, transcendentals=0):
    return pl.CostEstimate(
        flops=flops, bytes_accessed=bytes_accessed, transcendentals=transcendentals
    )


PARAMS = pltpu.CompilerParams(vmem_limit_bytes=VMEM_LIMIT)


def raw_specs(raw, group, count):
    return [
        pl.BlockSpec(
            (1, array.shape[1], LANES),
            lambda p, sel=sel, part=part: (sel, 0, (group * 3 + part) * count + p),
        )
        for array, sel in raw
        for part in range(3)
    ]


def rows_of(pieces):
    return [array.shape[1] for array, _ in pieces]


def attend(raw, gains, live, sequence, img_total, groups):
    width = raw[0][0].shape[2] // 3
    pairs = width // LANES
    count = pairs // groups
    rows = rows_of(raw)
    total = sum(rows)

    def kernel(*refs):
        attend_kernel(rows, img_total, *refs)

    work = pairs * 2 * total * total
    outputs = pl.pallas_call(
        kernel,
        grid=(pairs,),
        in_specs=[
            pl.BlockSpec(
                (1, array.shape[1], LANES),
                lambda p, sel=sel, part=part: (
                    sel,
                    0,
                    (p // count * 3 + part) * count + p % count,
                ),
            )
            for array, sel in raw
            for part in range(3)
        ]
        + [
            pl.BlockSpec((4, LANES), lambda p: (0, 0)),
            pl.BlockSpec((1, total - img_total, LANES), lambda p: (sequence, 0, 0)),
        ],
        out_specs=[pl.BlockSpec((1, size, LANES), lambda p: (0, 0, p)) for size in rows]
        + [pl.BlockSpec((1, 1, 16, total), lambda p: (0, p, 0, 0))],
        out_shape=[jax.ShapeDtypeStruct((1, size, width), BF16) for size in rows]
        + [jax.ShapeDtypeStruct((1, pairs, 16, total), F32)],
        scratch_shapes=[pltpu.VMEM((total, LANES), BF16)] * 6,
        compiler_params=PARAMS,
        cost_estimate=cost(work * 4 * LANES, total * width * 14, work),
        name="attend",
    )(*[array for array, _ in raw for _ in range(3)], gains, live)
    return (list(outputs[:-1]), outputs[-1])


def attend_back(raw, grads, done, norm, gains, live, sequence, img_total, groups, group, before):
    triple = raw[0][0].shape[2]
    width = triple // 3
    pairs = width // LANES
    count = pairs // groups
    rows = rows_of(raw)
    total = sum(rows)
    pieces = len(rows)

    def kernel(*refs):
        if before is not None:
            refs = refs[pieces:]
        attend_back_kernel(rows, img_total, count * LANES, *refs)

    head_specs = [
        pl.BlockSpec((1, size, LANES), lambda p: (0, 0, group * count + p)) for size in rows
    ]
    in_specs = (
        raw_specs(raw, group, count)
        + head_specs
        + head_specs
        + [
            pl.BlockSpec((1, 1, 16, total), lambda p: (0, group * count + p, 0, 0)),
            pl.BlockSpec((4, LANES), lambda p: (0, 0)),
            pl.BlockSpec((1, total - img_total, LANES), lambda p: (sequence, 0, 0)),
        ]
    )
    operands = [array for array, _ in raw for _ in range(3)]
    operands += [*grads, *done, norm, gains, live]
    aliases = {}
    if before is not None:
        in_specs = [pl.BlockSpec(memory_space=pl.ANY)] * pieces + in_specs
        operands = list(before) + operands
        aliases = {i: i for i in range(pieces)}
    work = count * 2 * total * total
    outputs = pl.pallas_call(
        kernel,
        grid=(count,),
        in_specs=in_specs,
        out_specs=[
            pl.BlockSpec((1, size, 3 * count * LANES), lambda p: (0, 0, group)) for size in rows
        ]
        + [pl.BlockSpec((1, 8, LANES), lambda p: (p, 0, 0))],
        out_shape=[jax.ShapeDtypeStruct((1, size, triple), BF16) for size in rows]
        + [jax.ShapeDtypeStruct((count, 8, LANES), F32)],
        scratch_shapes=[pltpu.VMEM((total, LANES), BF16)] * 3
        + [pltpu.VMEM((LANES, total), BF16)]
        + [pltpu.VMEM((total, LANES), BF16)] * 2
        + [pltpu.VMEM((total, LANES), F32)] * 3,
        compiler_params=PARAMS,
        input_output_aliases=aliases,
        cost_estimate=cost(work * 10 * LANES, total * count * LANES * 22, work),
        name="attend_back",
    )(*operands)
    return (list(outputs[:-1]), outputs[-1])


def tile_of(extent):
    for size in (1024, 768, 512, 384, 256, 128):
        if extent % size == 0:
            return size
    return extent


def hidden_back(hidden, grads, weight, modality):
    width = weight.shape[2]
    units = weight.shape[1]
    tile = tile_of(units)
    rows = rows_of(hidden)
    count = len(rows)

    def kernel(*refs):
        weight_ref = refs[2 * count]
        for i in range(count):
            value = refs[i][0]
            grad = dot(refs[count + i][0], weight_ref[0], NT)
            square = value * value
            slope = math.sqrt(2 / math.pi)
            bent = jnp.tanh(value * (slope + (slope * 0.044715) * square))
            half = 0.5 * value
            rise = 0.5 + 0.5 * bent
            refs[2 * count + 1 + i][0] = (half + half * bent).astype(BF16)
            rise = rise + half * (1.0 - bent * bent) * (slope + (3 * slope * 0.044715) * square)
            refs[3 * count + 1 + i][0] = (grad * rise).astype(BF16)

    total = sum(rows)
    outputs = pl.pallas_call(
        kernel,
        grid=(units // tile,),
        in_specs=[
            pl.BlockSpec((1, size, tile), lambda j, sel=sel: (sel, 0, j))
            for (_, sel), size in zip(hidden, rows)
        ]
        + [
            pl.BlockSpec((1, size, width), lambda j, sel=sel: (sel, 0, 0))
            for (_, sel), size in zip(grads, rows)
        ]
        + [pl.BlockSpec((1, tile, width), lambda j: (modality, j, 0))],
        out_specs=[pl.BlockSpec((1, size, tile), lambda j: (0, 0, j)) for size in rows] * 2,
        out_shape=[jax.ShapeDtypeStruct((1, size, units), BF16) for size in rows] * 2,
        compiler_params=PARAMS,
        cost_estimate=cost(
            2 * total * width * units, total * (2 * width + 8 * units) + 2 * units * width, total * units
        ),
        name="hidden_back",
    )(*[a for a, _ in hidden], *[a for a, _ in grads], weight)
    return (list(outputs[:count]), list(outputs[count:]))


def weight_sum(lefts, rights, blocks, bit=None, before=None, place=0, places=1):
    rows = lefts[0][0].shape[2]
    columns = rights[0][0].shape[2]
    block = rows // blocks
    row_tile = max(size for size in (768, 512, 384, rows) if rows % size == 0 and size % (2 * block) == 0)
    tile = tile_of(columns)
    sizes = rows_of(lefts)
    count = len(sizes)
    run = row_tile // block

    def kernel(*refs):
        bit_ref, refs = refs[0], refs[len(first) :]
        total = None
        for i in range(count):
            part = lax.dot_general(
                refs[i][0], refs[count + i][0], (((0,), (0,)), ((), ())), preferred_element_type=F32
            )
            total = part if total is None else total + part
        if bit is None:
            for j in range(run):
                refs[2 * count][j, 0] = total[j * block : (j + 1) * block].astype(BF16)
        else:
            keep_ref, away_ref = refs[2 * count :]
            odd = bit_ref[0] == 1
            for j in range(run // 2):
                even_rows = total[2 * j * block : (2 * j + 1) * block]
                odd_rows = total[(2 * j + 1) * block : (2 * j + 2) * block]
                keep_ref[j] = jnp.where(odd, odd_rows, even_rows).astype(BF16)
                away_ref[j] = jnp.where(odd, even_rows, odd_rows).astype(BF16)

    total = sum(sizes)
    if bit is None:
        out_shape = jax.ShapeDtypeStruct((blocks, places, block, columns), BF16)
        out_specs = pl.BlockSpec((run, 1, block, tile), lambda i, j: (i, place, 0, j))
    else:
        out_shape = [jax.ShapeDtypeStruct((blocks // 2, block, columns), BF16)] * 2
        out_specs = [pl.BlockSpec((run // 2, block, tile), lambda i, j: (i, 0, j))] * 2
    first_specs, first = [], []
    if bit is not None:
        first_specs, first = [pl.BlockSpec(memory_space=pltpu.SMEM)], [bit]
    elif before is not None:
        first_specs, first = [pl.BlockSpec(memory_space=pl.ANY)], [before]
    return pl.pallas_call(
        kernel,
        grid=(rows // row_tile, columns // tile),
        in_specs=first_specs
        + [
            pl.BlockSpec((1, size, row_tile), lambda i, j, sel=sel: (sel, 0, i))
            for (_, sel), size in zip(lefts, sizes)
        ]
        + [
            pl.BlockSpec((1, size, tile), lambda i, j, sel=sel: (sel, 0, j))
            for (_, sel), size in zip(rights, sizes)
        ],
        out_specs=out_specs,
        out_shape=out_shape,
        compiler_params=PARAMS,
        input_output_aliases={} if before is None else {0: 0},
        cost_estimate=cost(
            2 * total * rows * columns, 2 * (total * (rows + columns) + rows * columns)
        ),
        name="weight_sum",
    )(*first, *[a for a, _ in lefts], *[a for a, _ in rights])


def pick_heads(weight, other, member, members, groups, group_width):
    rows, columns = weight.shape
    width = columns // 3
    head_width = width // members
    size = lambda group: min(group_width, head_width - group * group_width)

    def kernel(member_ref, in_ref, other_ref, out_ref):
        for m in range(members):

            @pl.when(member_ref[0] == m)
            def _():
                for group in range(groups):
                    for part in range(3):
                        start = part * width + m * head_width + group * group_width
                        piece = in_ref[:, start : start + size(group)]
                        if size(group) < group_width:
                            blank = jnp.zeros((rows, group_width - size(group)), piece.dtype)
                            piece = jnp.concatenate([piece, blank], axis=1)
                        place = (group * 3 + part) * group_width
                        out_ref[:, place : place + group_width] = piece

        out_ref[:, 3 * groups * group_width :] = other_ref[...]

    total = 3 * groups * group_width + other.shape[1]
    return pl.pallas_call(
        kernel,
        in_specs=[pl.BlockSpec(memory_space=pltpu.SMEM)]
        + [pl.BlockSpec(memory_space=pltpu.VMEM)] * 2,
        out_specs=pl.BlockSpec(memory_space=pltpu.VMEM),
        out_shape=jax.ShapeDtypeStruct((rows, total), weight.dtype),
        compiler_params=PARAMS,
        cost_estimate=cost(0, 4 * rows * columns),
        name="pick_heads",
    )(member, weight, other)


def pick_units(weight, member, members, shards):
    rows, columns = weight.shape
    unit = columns // (shards * members)

    def kernel(member_ref, in_ref, out_ref):
        for m in range(members):

            @pl.when(member_ref[0] == m)
            def _():
                out_ref[...] = jnp.concatenate(
                    [
                        in_ref[:, (f * members + m) * unit : (f * members + m + 1) * unit]
                        for f in range(shards)
                    ],
                    axis=1,
                )

    return pl.pallas_call(
        kernel,
        in_specs=[pl.BlockSpec(memory_space=pltpu.SMEM), pl.BlockSpec(memory_space=pltpu.VMEM)],
        out_specs=pl.BlockSpec(memory_space=pltpu.VMEM),
        out_shape=jax.ShapeDtypeStruct((rows, columns // members), weight.dtype),
        compiler_params=PARAMS,
        cost_estimate=cost(0, 2 * rows * columns * 2),
        name="pick_units",
    )(member, weight)


def join_units(parts, shards):
    rows, columns = parts[0].shape
    unit = columns // shards

    def kernel(*refs):
        refs[-1][...] = jnp.concatenate(
            [ref[:, f * unit : (f + 1) * unit] for f in range(shards) for ref in refs[:-1]], axis=1
        )

    return pl.pallas_call(
        kernel,
        in_specs=[pl.BlockSpec(memory_space=pltpu.VMEM)] * len(parts),
        out_specs=pl.BlockSpec(memory_space=pltpu.VMEM),
        out_shape=jax.ShapeDtypeStruct((rows, columns * len(parts)), parts[0].dtype),
        compiler_params=PARAMS,
        cost_estimate=cost(0, 8 * rows * columns * len(parts)),
        name="join_units",
    )(*parts)


def shift_seq(values, amount):
    members = lax.axis_size("seq")
    return lax.ppermute(values, "seq", [(i, (i + amount) % members) for i in range(members)])


def gather_seq(values):
    return [values] + [shift_seq(values, k) for k in range(1, lax.axis_size("seq"))]


def pick(values, index, axis):
    return lax.dynamic_index_in_dim(values, index, axis, keepdims=False)


class Reduction:
    def __init__(self, halves):
        self.terms, self.away = [halves[0]], halves[1]
        self.bit, self.came = 1, None

    def send(self):
        size = lax.axis_size("fsdp")
        self.came = lax.ppermute(self.away, "fsdp", [(i, i ^ self.bit) for i in range(size)])

    def land(self):
        self.terms.append(self.came)
        self.bit, self.came = self.bit * 2, None
        if self.bit < lax.axis_size("fsdp"):
            mine = (lax.axis_index("fsdp") // self.bit) % 2
            terms = [t.reshape((t.shape[0] // 2, 2) + t.shape[1:]) for t in self.terms]
            self.away = sum(pick(t, 1 - mine, 1).astype(F32) for t in terms).astype(BF16)
            self.terms = [pick(t, mine, 1) for t in terms]

    def result(self):
        return sum(t.astype(F32) for t in self.terms)[0]


def gate(first, *others):
    return lax.optimization_barrier((first, *others))


class Order:
    def __init__(self):
        self.marks, self.closed = [], False

    def __call__(self, *arrays):
        if not arrays:
            return []
        self.closed = True
        return list(gate(*arrays, *self.marks)[: len(arrays)])

    def mark(self, *arrays):
        if self.closed:
            self.marks, self.closed = [], False
        self.marks += arrays


def statistics(values):
    average = jnp.mean(values, axis=-1, keepdims=True)
    centred = values - average
    return (average, lax.rsqrt(jnp.mean(centred * centred, axis=-1, keepdims=True) + 1e-06))


def modulated(values, stats, shift, scale):
    return (((values - stats[0]) * stats[1]) * (1.0 + scale) + shift).astype(BF16)


def norm_back(grad, unit, root):
    return root * (
        grad
        - jnp.mean(grad, axis=-1, keepdims=True)
        - unit * jnp.mean(grad * unit, axis=-1, keepdims=True)
    )


def times(left, right):
    return lax.dot_general(left, right, (((2,), (0,)), ((), ())), preferred_element_type=F32)


def times_t(left, right):
    return lax.dot_general(left, right, (((2,), (1,)), ((), ())), preferred_element_type=F32)


def pad_rows(values, rows):
    return jnp.pad(values, ((0, 0), (0, rows - values.shape[1]), (0, 0)))


def body(
    img_in, txt_in, cond, text_counts, ada_w, qkv_w, proj_w, fc1_w, fc2_w, qk_gain, img_cot, txt_cot
):
    members = lax.axis_size("seq")
    member = lax.axis_index("seq")
    shards = lax.axis_size("fsdp")
    sequences, img_local, width = img_in.shape
    slots = txt_in.shape[1]
    padded = -(-slots // 16) * 16
    img_total = members * img_local
    head_width = width // members
    head_padded = -(-head_width // LANES) * LANES
    groups = 2 if (head_padded // LANES) % 2 == 0 else 1
    group_width = head_padded // groups
    hidden_width = fc1_w.shape[2]
    shard_rows = ada_w.shape[1]
    unit_rows = hidden_width // (shards * members)
    member_index = member.reshape(1)
    own_bit = (lax.axis_index("fsdp") % 2).reshape(1)
    every = range(members)
    both = range(sequences)

    txt_in, txt_cot = pad_rows(txt_in, padded), pad_rows(txt_cot, padded)
    img_all, txt_all = gather_seq(img_in), gather_seq(txt_in)
    ready = gate(img_cot, txt_cot, *img_all[1:])
    img_cots, txt_cots = gather_seq(ready[0]), gather_seq(ready[1])

    own_both = pick_heads(
        qkv_w.reshape(2 * shard_rows, 3 * width),
        proj_w.reshape(2 * shard_rows, width),
        member_index,
        members,
        groups,
        group_width,
    )
    w_both = lax.all_gather(own_both.reshape(2, shard_rows, -1), "fsdp", axis=1, tiled=True)
    triple = 3 * head_padded
    w_qkv = [w_both[t, :, :triple] for t in range(2)]
    w_proj = [w_both[t, :, triple:] for t in range(2)]

    cond_act = jax.nn.silu(cond.astype(F32)).astype(BF16)
    cond_cols = lax.all_to_all(
        cond_act.reshape(sequences, shards, shard_rows), "fsdp", split_axis=1, concat_axis=0, tiled=True
    ).reshape(shards * sequences, shard_rows)
    mod_width = ada_w.shape[2]
    share = mod_width // members
    own_ada = lax.dynamic_slice_in_dim(ada_w, member * share, share, 2)
    mod_part = jnp.einsum("sd,tdm->stm", cond_cols, own_ada, preferred_element_type=F32)
    mod_part = mod_part.reshape(shards, sequences, 2, share)
    mod_part, fc1_w, fc2_w = gate(mod_part, fc1_w, fc2_w)
    mod_sum = jnp.sum(
        lax.all_to_all(mod_part, "fsdp", split_axis=0, concat_axis=0, tiled=True), axis=0
    )
    mod_shares = jnp.stack(gather_seq(mod_sum))
    modulation = jnp.concatenate(
        [pick(mod_shares, (member - i) % members, 0) for i in every], axis=-1
    )

    own_fc1 = pick_units(fc1_w.reshape(2 * shard_rows, hidden_width), member_index, members, shards)
    own_fc2 = pick(fc2_w.reshape(2, members, unit_rows, width), member, 1)
    w_fc1 = lax.all_gather(own_fc1.reshape(2, shard_rows, -1), "fsdp", axis=1, tiled=True)
    w_fc2 = lax.all_gather(own_fc2, "fsdp", axis=1, tiled=True)

    counts = jnp.stack([pick(text_counts, (member - k) % members, 1) for k in every], axis=1)
    slot_ids = lax.broadcasted_iota(jnp.int32, (sequences, members, padded), 2)
    live = (slot_ids < counts[:, :, None]).astype(F32)
    live_rows = jnp.transpose(live, (1, 0, 2)).reshape(members * sequences, padded, 1)
    text_rows = live_rows[:sequences]
    live_lanes = jnp.broadcast_to(
        live.reshape(sequences, members * padded, 1), (sequences, members * padded, LANES)
    )
    gains = jnp.tile(qk_gain.reshape(4, HEAD), (1, 2))
    pieces = [
        [piece[:, None, :] for piece in jnp.split(modulation[:, t], 6, axis=-1)] for t in range(2)
    ]

    def text_all(vector):
        return jnp.tile(vector, (members, 1, 1))

    ready = gate(modulation, *img_all[1:], *txt_all[1:])
    img_all, txt_all = [img_all[0], *ready[1:members]], [txt_all[0], *ready[members:]]
    img_f32 = [values.astype(F32) for values in img_all]
    img_stats = [statistics(values) for values in img_f32]
    txt_f32 = jnp.concatenate(txt_all, axis=0).astype(F32)
    txt_stats = statistics(txt_f32)
    normed_img = [modulated(img_f32[k], img_stats[k], pieces[0][0], pieces[0][1]) for k in every]
    normed_txt = modulated(txt_f32, txt_stats, text_all(pieces[1][0]), text_all(pieces[1][1]))
    raw_img = [times(normed_img[k], w_qkv[0]) for k in every]
    raw_txt = times(normed_txt, w_qkv[1])
    raw = [
        [(raw_img[k], s) for k in every] + [(raw_txt, k * sequences + s) for k in every]
        for s in both
    ]
    attended, norms = [], []
    order = Order()
    for s in both:
        values, norm = attend(raw[s], order(gains)[0], live_lanes, s, img_total, groups)
        attended.append(values)
        norms.append(norm)
        order.mark(norm)

    def advance(land, send):
        for red in land:
            if red.came is not None:
                red.came = order(red.came)[0]
                red.land()
                order.mark(*(red.terms if red.bit == shards else [red.away]))
        for red in send:
            if red.bit < shards:
                order.mark(red.away)
                red.send()

    def to_members(parts):
        return [parts[0]] + [shift_seq(parts[k], -k) for k in range(1, members)]

    came_attended = [to_members(attended[s][:members]) for s in both]
    came_attended_txt = [to_members(attended[s][members:]) for s in both]

    came_attended[0] = order(*came_attended[0])
    ready = gate(came_attended[0][0], *order(*img_cots[1:], *txt_cots[1:]))[1:]
    img_cots, txt_cots = [img_cots[0], *ready[: members - 1]], [txt_cots[0], *ready[members - 1 :]]
    mlp_img = [(pieces[0][5] * values.astype(F32)).astype(BF16) for values in img_cots]
    txt_grads = jnp.concatenate(txt_cots, axis=0).astype(F32) * live_rows
    mlp_txt = (text_all(pieces[1][5]) * txt_grads).astype(BF16)
    order.mark(*mlp_img, mlp_txt)

    vectors = [[p[s : s + 1] for p in pieces[0]] for s in both] + [pieces[1]]
    kinds = [0] * sequences + [1]
    units = range(sequences + 1)
    text = sequences

    def own_in():
        img, txt = order(img_in, txt_in)
        return [img[s : s + 1].astype(F32) for s in both] + [txt.astype(F32)]

    def own_grad():
        img, txt = order(img_cot, txt_cot)
        return [img[s : s + 1].astype(F32) for s in both] + [txt.astype(F32) * text_rows]

    def heads_together(parts):
        parts = [part[..., :head_width] for part in parts]
        return jnp.roll(jnp.concatenate(parts, axis=-1), member * head_width, axis=-1)

    own_attended, middle, branch, mid_stats, normed_mid = [], [], [], [], []
    tokens = own_in()
    for u in units:
        t = kinds[u]
        if t == 0:
            own_attended.append(heads_together(order(*came_attended[u])))
        else:
            parts = order(*[part for parts in came_attended_txt for part in parts])
            parts = [parts[s * members : (s + 1) * members] for s in both]
            own_attended.append(
                jnp.concatenate([heads_together(parts[s]) for s in both], axis=0)
            )
        branch.append(times(own_attended[u], w_proj[t]))
        middle.append(tokens[u] + vectors[u][2] * branch[u])
        mid_stats.append(statistics(middle[u]))
        normed = modulated(middle[u], mid_stats[u], vectors[u][3], vectors[u][4])
        order.mark(normed)
        normed_mid.append(gather_seq(normed))

    hidden = [[None] * members for _ in both] + [None]
    mlp_pieces = [[(mlp_img[k], s) for k in every] for s in both]
    mlp_pieces.append([(mlp_txt.reshape(1, -1, width), 0)])

    def rise(u, k):
        values = order(normed_mid[u][k])[0]
        normed_mid[u][k] = values
        hidden[u][k] = times(values, w_fc1[0])
        order.mark(hidden[u][k])

    def reduction(lefts, rights):
        red = Reduction(weight_sum(lefts, rights, shards, own_bit))
        order.mark(red.away)
        return red

    def scattered(lefts, rights):
        summed = weight_sum(lefts, rights, shards)
        order.mark(summed)
        return lax.psum_scatter(summed, "fsdp", scatter_dimension=0, tiled=True)[0, 0]

    def at_first(arrays):
        return [(array, 0) for array in arrays]

    def of(lists, t):
        return [array for u in units if kinds[u] == t for array in lists[u]]

    def to_owners(products):
        return [shift_seq(p.astype(BF16), -k) for k, p in enumerate(products, 1)]

    def text_members(products):
        return jnp.split(products.reshape(-1, padded, width), members, axis=0)

    active, hidden_grad = [None] * len(units), [None] * len(units)
    came_mid = [None] * len(units)
    own_text = {}

    def feed(u):
        t = kinds[u]
        hidden[u][0] = order(hidden[u][0])[0]
        active[u], hidden_grad[u] = hidden_back(
            [(h, 0) for h in hidden[u]], mlp_pieces[u], w_fc2, t
        )
        if t == 0:
            products = [times_t(values, w_fc1[t]).astype(BF16) for values in hidden_grad[u][1:]]
            order.mark(*products)
        else:
            parts = text_members(times_t(hidden_grad[u][0], w_fc1[t]))
            own_text["mid"], products = parts[0], parts[1:]
            order.mark(parts[0])
        came_mid[u] = to_owners(products)

    for s in both:
        rise(s, 0)
    for k in range(1, members):
        rise(0, k)
    values = order(*normed_mid[text])
    normed_mid[text] = [jnp.concatenate(values, axis=0).reshape(1, -1, width)]
    hidden[text] = [times(normed_mid[text][0], w_fc1[1])]
    order.mark(hidden[text][0])
    for s in range(1, sequences):
        for k in range(1, members):
            rise(s, k)
    feed(text)
    ready = order(active[text][0], hidden_grad[text][0])
    fc2_txt = scattered(at_first(ready[:1]), mlp_pieces[text])
    fc1_txt = scattered(at_first(normed_mid[text]), at_first(ready[1:]))
    feed(0)
    for s in range(1, sequences):
        feed(s)
    active[0][0] = order(active[0][0])[0]
    fc2_img = scattered(
        at_first(of(active, 0)), [p for u in units if kinds[u] == 0 for p in mlp_pieces[u]]
    )

    middle_grad, late_grads, head_grads, branch_grad = {}, {}, {}, {}
    grads_now = own_grad()
    for u in [0, text, *range(1, sequences)]:
        t = kinds[u]
        came = order(*came_mid[u])
        if t == 0:
            mid_grad = times_t(hidden_grad[u][0], w_fc1[t])
        else:
            mid_grad = own_text["mid"]
        for values in came:
            mid_grad = mid_grad + values.astype(F32)
        average, root = mid_stats[u]
        unit = (middle[u] - average) * root
        scale_mlp_grad = jnp.sum(mid_grad * unit, axis=1)
        shift_mlp_grad = jnp.sum(mid_grad, axis=1)
        total = grads_now[u] + norm_back(mid_grad * (1.0 + vectors[u][4]), unit, root)
        middle_grad[u] = total
        gate_attn_grad = jnp.sum(total * branch[u], axis=1)
        late_grads[u] = [gate_attn_grad, shift_mlp_grad, scale_mlp_grad]
        branch_grad[u] = (vectors[u][2] * total).astype(BF16)
        attended_grad = times_t(branch_grad[u], w_proj[t]).astype(BF16)
        attended_grad = jnp.roll(attended_grad, -member * head_width, axis=-1)
        parts = []
        for k in every:
            part = attended_grad[..., k * head_width : (k + 1) * head_width]
            if head_padded > head_width:
                part = jnp.pad(part, ((0, 0), (0, 0), (0, head_padded - head_width)))
            parts.append(part)
        order.mark(*parts)
        head_grads[u] = [shift_seq(part, k) if k else part for k, part in enumerate(parts)]
    ready = order(branch_grad[text], branch_grad[0])
    branch_grad[text], branch_grad[0] = ready
    proj_both = None
    for t in range(2):
        proj_both = weight_sum(
            at_first([own_attended[u].reshape(1, -1, width) for u in units if kinds[u] == t]),
            at_first([branch_grad[u].reshape(1, -1, width) for u in units if kinds[u] == t]),
            shards,
            before=proj_both,
            place=t,
            places=2,
        )
    order.mark(proj_both)
    proj_both = lax.psum_scatter(proj_both, "fsdp", scatter_dimension=0, tiled=True)[0]
    hidden_grad[0][0] = order(hidden_grad[0][0])[0]
    fc1_img = reduction(at_first(of(normed_mid, 0)), at_first(of(hidden_grad, 0)))
    advance([], [fc1_img])
    grads = [
        [head_grads[s][k] for k in every] + [head_grads[text][k][s : s + 1] for k in every]
        for s in both
    ]
    steps = {
        (0, 0): [fc1_img],
        (0, groups - 1): [fc1_img],
        (sequences - 1, 0): [fc1_img],
        (sequences - 1, groups - 1): [fc1_img],
    }
    gain_parts, raw_grads, came_in, came_mlp = [], [], [], None

    def in_products(s):
        values = order(*raw_grads[s][1:members])
        products = [times_t(v, w_qkv[0]).astype(BF16) for v in values]
        order.mark(*products)
        return to_owners(products)

    for s in both:
        before = None
        for group in range(groups):
            before, gain_part = attend_back(
                raw[s],
                grads[s],
                attended[s],
                norms[s],
                order(gains)[0],
                live_lanes,
                s,
                img_total,
                groups,
                group,
                before,
            )
            gain_parts.append(gain_part)
            order.mark(gain_part)
            reds = steps.pop((s, group), [])
            advance(reds, reds)
        raw_grads.append(before)
        if came_mlp is None:
            came_mlp = []
            for u in units:
                values = order(*active[u])
                active[u] = values
                if kinds[u] == 0:
                    products = [times(v, w_fc2[0]).astype(BF16) for v in values[1:]]
                    order.mark(*products)
                else:
                    parts = text_members(times(values[0], w_fc2[1]))
                    own_text["mlp"], products = parts[0], parts[1:]
                    order.mark(parts[0])
                came_mlp.append(to_owners(products))
        if s < sequences - 1:
            came_in.append(in_products(s))
    came_mlp = [order(*came) for came in came_mlp]
    values = gate(*order(*raw_grads[-1][:members]), *[v for came in came_mlp for v in came])[:members]
    raw_grads[-1] = [*values, *raw_grads[-1][members:]]
    qkv_img = reduction(
        [(normed_img[k], s) for s in both for k in every],
        at_first([raw_grads[s][k] for s in both for k in every]),
    )
    advance([], [qkv_img])
    came_in.append(in_products(sequences - 1))
    advance([qkv_img], [qkv_img])
    raw_text = jnp.concatenate([raw_grads[s][members + k] for k in every for s in both], axis=0)
    raw_text = order(raw_text)[0]
    parts = text_members(times_t(raw_text, w_qkv[1]))
    own_text["in"] = parts[0]
    came_in.append(to_owners(parts[1:]))
    order.mark(parts[0])
    raw_text = order(raw_text)[0]
    qkv_txt = reduction(
        at_first([normed_txt.reshape(1, -1, width)]), at_first([raw_text.reshape(1, -1, triple)])
    )
    advance([], [qkv_txt])
    in_grads, in_sums, outs, gate_sums = {}, {}, {}, {}
    tokens = own_in()

    def input_back(u):
        came = order(*came_in[u])
        in_grad = times_t(raw_grads[u][0], w_qkv[0]) if kinds[u] == 0 else own_text["in"]
        for values in came:
            in_grad = in_grad + values.astype(F32)
        average, root = statistics(tokens[u])
        unit = (tokens[u] - average) * root
        in_sums[u] = [jnp.sum(in_grad, axis=1), jnp.sum(in_grad * unit, axis=1)]
        in_grads[u] = middle_grad[u] + norm_back(in_grad * (1.0 + vectors[u][1]), unit, root)
        order.mark(in_grads[u], *in_sums[u])

    def output(u):
        came = order(*came_mlp[u])
        mlp_out = times(active[u][0], w_fc2[0]) if kinds[u] == 0 else own_text["mlp"]
        for values in came:
            mlp_out = mlp_out + values.astype(F32)
        result = middle[u] + vectors[u][5] * mlp_out
        if kinds[u] == 1:
            result = result * text_rows
        outs[u] = result.astype(BF16)
        gate_sums[u] = jnp.sum(grads_late[u] * mlp_out, axis=1)
        order.mark(outs[u], gate_sums[u])

    advance([qkv_txt], [qkv_txt])
    grads_late = own_grad()
    for s in range(sequences - 1):
        input_back(s)
    output(0)
    advance([qkv_img], [qkv_img])
    input_back(text)
    input_back(sequences - 1)
    for u in units:
        if u:
            output(u)
    mod_rows = [
        jnp.concatenate([*in_sums[u], *late_grads[u], gate_sums[u]], axis=-1) for u in units
    ]
    img_out = jnp.concatenate([outs[s] for s in both], axis=0)
    txt_out = outs[text][:, :slots]
    img_grad = jnp.concatenate([in_grads[s] for s in both], axis=0)
    txt_grad = in_grads[text][:, :slots]

    gain_own = sum(jnp.sum(part, axis=0) for part in gain_parts)[:4]
    gain_own = (gain_own[:, :HEAD] + gain_own[:, HEAD:]).reshape(-1)
    mod_own = jnp.stack([jnp.concatenate(mod_rows[:-1], axis=0), mod_rows[-1]], axis=1)
    mod_count = mod_own.size
    own_shared = jnp.concatenate([mod_own.reshape(-1), gain_own])
    order.mark(own_shared)
    came_shared = gather_seq(own_shared)[1:]
    qkv_red = [qkv_img, qkv_txt]
    advance(qkv_red, qkv_red)
    shared = sum(order(*came_shared), own_shared)
    gain_high = shared[mod_count:].astype(BF16)
    gain_low = (shared[mod_count:] - gain_high.astype(F32)).astype(BF16)
    packed = jnp.concatenate([shared[:mod_count].astype(BF16), gain_high, gain_low])[None]
    order.mark(packed)
    packed = lax.all_gather(packed, "fsdp", axis=0, tiled=True)

    def finish(reds):
        while reds:
            advance(reds, reds)
            reds = [red for red in reds if red.bit < shards]

    def send_rows(values):
        blocks = values.reshape((members, -1) + values.shape[1:])
        own = pick(blocks, member, 0)
        parts = [pick(blocks, (member + k) % members, 0) for k in range(1, members)]
        order.mark(own, *parts)
        return [own] + [shift_seq(part, k) for k, part in enumerate(parts, 1)]

    def by_place(parts):
        stacked = jnp.stack([parts[0], *order(*parts[1:])])
        return [pick(stacked, (member - i) % members, 0) for i in every]

    finish([fc1_img])
    ready = order(fc2_img, fc2_txt, fc1_txt, proj_both)
    fc2_grad = jnp.stack(ready[:2]).astype(F32)
    fc1_rows = [send_rows(fc1_img.result()), send_rows(ready[2].astype(F32))]
    proj_rows = send_rows(jnp.transpose(ready[3].astype(F32), (1, 0, 2)))
    advance(qkv_red, qkv_red)
    fc1_grad = jnp.stack([join_units(by_place(rows), shards) for rows in fc1_rows])
    proj_grad = jnp.transpose(sum(order(*proj_rows[1:]), proj_rows[0]), (1, 0, 2))
    order.mark(fc1_grad, proj_grad)
    advance(qkv_red, qkv_red)

    packed = order(packed)[0]
    every_mod = packed[:, :mod_count].reshape(shards * sequences, 2, mod_width)
    gain_grad = jnp.sum(packed[:, mod_count:].astype(F32), axis=0).reshape(2, 2, 2 * HEAD).sum(axis=0)
    cond_part = jnp.einsum("stm,tdm->sd", every_mod, ada_w, preferred_element_type=F32)
    order.mark(cond_part)
    cond_full = lax.all_to_all(cond_part, "fsdp", split_axis=0, concat_axis=1, tiled=True)
    finish(qkv_red)
    qkv_rows = [send_rows(red.result()) for red in qkv_red]
    every_mod = order(every_mod)[0]
    out_rows = width // (shards * members)
    own_cols = lax.dynamic_slice_in_dim(cond_cols, member * out_rows, out_rows, 1)
    ada_grad = jnp.einsum("sr,stm->trm", own_cols, every_mod, preferred_element_type=F32)
    cond_grad = jax.vjp(jax.nn.silu, cond.astype(F32))[1](cond_full)[0]
    qkv_grad = []
    for rows in qkv_rows:
        parts = by_place(rows)
        qkv_grad.append(
            jnp.concatenate(
                [
                    parts[m][:, (g * 3 + part) * group_width :][
                        :, : min(group_width, head_width - g * group_width)
                    ]
                    for part in range(3)
                    for m in every
                    for g in range(groups)
                ],
                axis=1,
            )
        )
    qkv_grad = jnp.stack(qkv_grad)
    return (
        img_out,
        txt_out,
        img_grad,
        txt_grad,
        cond_grad,
        ada_grad,
        qkv_grad,
        proj_grad,
        fc1_grad,
        fc2_grad,
        gain_grad,
    )


def solution(mesh):
    tokens, rows = P("fsdp", "seq", None), P("fsdp", None)
    weight, weight_grad = P(None, "fsdp", None), P(None, ("fsdp", "seq"), None)
    in_specs = (tokens, tokens, rows, rows) + (weight,) * 5 + (P(), tokens, tokens)
    out_specs = (tokens,) * 4 + (rows,) + (weight_grad,) * 5 + (P(),)
    return jax.shard_map(body, mesh=mesh, in_specs=in_specs, out_specs=out_specs, check_vma=False)
```

time: 1710 us -> 1180 us (0.69)
  waiting for transfers between devices: 487 us -> 211 us
  matrix products: 478 us -> 254 us
  Pallas kernels: 242 us -> 388 us
  local copies, waits for them, and re-layouts: 205 us -> 82.4 us
  starting transfers between devices: 126 us -> 62.7 us
    dot_general x14 -> x0, matrix products: 164 us -> none  [outer(): lax.dot_general(left, right, (((0, 1), (0, 1)), ((), ())), preferred_elem...]
    pallas_call x2 -> x21, Pallas kernels: 242 us -> 388 us  [the longest x4 133 us: attend_back(): pl.pallas_call(kernel, grid=(count,), in_specs=in_specs, out_specs=[pl.Bl...]
    ppermute x24 -> x30, waiting for transfers between devices: 221 us -> 89.5 us  [shift_seq(): lax.ppermute(values, 'seq', [(i, (i + amount) % members) for i in range(m...]
    ppermute x32 -> x12, waiting for transfers between devices: 204 us -> 83.4 us  [send(): lax.ppermute(self.away, 'fsdp', [(i, i ^ self.bit) for i in range(size)])]
    dynamic_slice x26 -> x9, local copies, waits for them, and re-layouts: 108 us -> 13.5 us  [pick(): return lax.dynamic_index_in_dim(values, index, axis, keepdims=False)]
    ppermute x32 -> x12, starting transfers between devices: 83 us -> 17.2 us  [send(): lax.ppermute(self.away, 'fsdp', [(i, i ^ self.bit) for i in range(size)])]
    dot_general x14 -> x13, matrix products: 163 us -> 110 us  [times_t(): lax.dot_general(left, right, (((2,), (1,)), ((), ())), preferred_element_...]
    reshape x13 -> x1, local copies, waits for them, and re-layouts: 45.2 us -> 2.79 us  [body(): every_mod = packed[:, :mod_count].reshape(shards * sequences, 2, mod_width)]
  transfers between devices with their start and end apart: 64 -> 53, of which waited for: 25 -> 10; matrix products, arithmetic and copies ran while one was open for 46% -> 40% of each run, Pallas kernels for 14% -> 31%
where the time goes in v2:
time: 1180 us; the launch traced here: 1170 us
  Pallas kernels  388 us (33%)
  matrix products  254 us (22%)
  waiting for transfers between devices  211 us (18%)
  other arithmetic  153 us (13%)
  local copies, waits for them, and re-layouts  82.4 us (7%)
  starting transfers between devices  62.7 us (5%)
  between operations  16.8 us (1%)
    dot_general x16, matrix products, times(): lax.dot_general(left, right, (((2,), (0,)), ((), ())), preferred_element_...  136 us
    pallas_call x4, Pallas kernels, attend_back(): pl.pallas_call(kernel, grid=(count,), in_specs=in_specs, out_specs=[pl.Bl...  133 us
    pallas_call x8, Pallas kernels, weight_sum(): pl.pallas_call(kernel, grid=(rows // row_tile, columns // tile), in_specs...  116 us
    dot_general x13, matrix products, times_t(): lax.dot_general(left, right, (((2,), (1,)), ((), ())), preferred_element_...  110 us
    ppermute x30, waiting for transfers between devices, shift_seq(): lax.ppermute(values, 'seq', [(i, (i + amount) % members) for i in range(m...  89.5 us
    ppermute x12, waiting for transfers between devices, send(): lax.ppermute(self.away, 'fsdp', [(i, i ^ self.bit) for i in range(size)])  83.4 us
    pallas_call x2, Pallas kernels, attend(): pl.pallas_call(kernel, grid=(pairs,), in_specs=[pl.BlockSpec((1, array.sh...  70 us
    pallas_call x3, Pallas kernels, hidden_back(): pl.pallas_call(kernel, grid=(units // tile,), in_specs=[pl.BlockSpec((1,...  57 us
  transfers between devices with their start and end apart: 53, of which 10 were waited for; matrix products, arithmetic and copies ran while one was open for 40% of the time, Pallas kernels for 31%

profile of v2, /device:TPU:0, one launch (start us, length us, event | category | flops | bytes accessed | tf_op | source)
XLA Modules:
  0.0 1168.0 jit_solution(9544258779279270336)
XLA Ops:
  51.7 31.7 %all-to-all-done.1 = f32[16,2,2,4608]{3,2,1,0:T(2,128)} async-done(((f32[16,2,2,4608]{3,2,1,0:T(2,128)}), f32[16,2,2,4608]{3,2,1,0:T(2,128)}, u32[]{:S(2)}, u32[]{:S(2)}) %all-to-all-start.1) | async-done | bytes 1179680 | tf_op jit(solution)/shard_map/all_to_all | solution.py:655
  92.0 34.1 %collective-permute-done = f32[2,2,4608]{2,1,0:T(2,128)} collective-permute-done((f32[2,2,4608]{2,1,0:T(2,128)}, f32[2,2,4608]{2,1,0:T(2,128)}, u32[]{:S(2)}, u32[]{:S(2)}) %collective-permute-start) | collective-permute-done | bytes 73760 | tf_op jit(solution)/shard_map/ppermute | solution.py:521
  163.1 12.9 %fusion.7.refs_3_.refs_4_.refs_5_.refs_7_.refs_8_.refs_9_ = f32[2,512,2304]{2,1,0:T(8,128)} fusion(bf16[2,512,1536]{2,1,0:T(8,128)(2,1)S(1)} %copy-done.42, bf16[2,1536,3840]{2,1,0:T(8,128)(2,1)} %all-gather.8.cloned.1.call-done), kind=kOutput, calls=%fused_computation.17 | convolution fusion | flops 7247757312 | bytes 19660800 | tf_op jit(solution)/shard_map/dot_general | solution.py:593
  176.0 13.0 %fusion.9.refs_0_.refs_1_.refs_2_.refs_4_.refs_5_.refs_6_ = f32[2,512,2304]{2,1,0:T(8,128)} fusion(bf16[2,512,1536]{2,1,0:T(8,128)(2,1)S(1)} %copy-done.43, bf16[2,1536,3840]{2,1,0:T(8,128)(2,1)} %all-gather.8.cloned.1.call-done), kind=kOutput, calls=%fused_computation.19 | convolution fusion | flops 7247757312 | bytes 19660800 | tf_op jit(solution)/shard_map/dot_general | solution.py:593
  189.8 34.7 %attend.2 = (bf16[1,512,768]{2,1,0:T(8,128)(2,1)}, bf16[1,512,768]{2,1,0:T(8,128)(2,1)}, bf16[1,96,768]{2,1,0:T(8,128)(2,1)}, bf16[1,96,768]{2,1,0:T(8,128)(2,1)}, f32[1,6,16,1216]{3,2,1,0:T(8,128)}) custom-call(f32[2,512,2304]{2,1,0:T(8,128)} %fusion.9.refs_0_.refs_1_.refs_2_.refs_4_.refs_5_.refs_6_, ...), custom_call_target="tpu_custom_call" | custom-call | flops 9084862464 | bytes 13074432 | tf_op jit(solution)/shard_map/attend/pallas_call | solution.py:230
  226.6 35.3 %attend.3 = (bf16[1,512,768]{2,1,0:T(8,128)(2,1)}, bf16[1,512,768]{2,1,0:T(8,128)(2,1)}, bf16[1,96,768]{2,1,0:T(8,128)(2,1)}, bf16[1,96,768]{2,1,0:T(8,128)(2,1)}, f32[1,6,16,1216]{3,2,1,0:T(8,128)}) custom-call(f32[2,512,2304]{2,1,0:T(8,128)} %fusion.9.refs_0_.refs_1_.refs_2_.refs_4_.refs_5_.refs_6_, ...), custom_call_target="tpu_custom_call" | custom-call | flops 9084862464 | bytes 13074432 | tf_op jit(solution)/shard_map/attend/pallas_call | solution.py:230
  306.9 10.1 convolution_bitcast_fusion.4.refs_0_
  337.4 25.5 %collective-permute-done.9 = bf16[2,96,1536]{2,1,0:T(8,128)(2,1)} collective-permute-done((bf16[2,96,1536]{2,1,0:T(8,128)(2,1)}, bf16[2,96,1536]{2,1,0:T(8,128)(2,1)}, u32[]{:S(2)}, u32[]{:S(2)}) %collective-permute-start.9) | collective-permute-done | bytes 589856 | tf_op jit(solution)/shard_map/ppermute | solution.py:521
  378.9 11.5 hidden_back.3
  400.1 9.5 weight_sum.8
  423.9 23.6 %hidden_back.4 = (bf16[1,512,3072]{2,1,0:T(8,128)(2,1)}, bf16[1,512,3072]{2,1,0:T(8,128)(2,1)}, bf16[1,512,3072]{2,1,0:T(8,128)(2,1)}, bf16[1,512,3072]{2,1,0:T(8,128)(2,1)}) custom-call(f32[1,512,3072]{2,1,0:T(8,128)} %convolution_bitcast_fusion.4.refs_0_, f32[1,512,3072]{2,1,0:T(8,128)} %convolution_bitcast_fusion.2.refs_1_, ...), custom_call_target="tpu_custom_call" | custom-call | flops 9663676416 | bytes 37748736 | tf_op jit(solution)/shard_map/hidden_back/pallas_call | solution.py:347
  447.5 11.1 fusion.122
  460.6 21.9 %hidden_back.5 = (bf16[1,512,3072]{2,1,0:T(8,128)(2,1)}, bf16[1,512,3072]{2,1,0:T(8,128)(2,1)}, bf16[1,512,3072]{2,1,0:T(8,128)(2,1)}, bf16[1,512,3072]{2,1,0:T(8,128)(2,1)}) custom-call(f32[1,512,3072]{2,1,0:T(8,128)} %convolution_bitcast_fusion.3.refs_0_, f32[1,512,3072]{2,1,0:T(8,128)} %convolution_bitcast_fusion.1.refs_1_, ...), custom_call_target="tpu_custom_call" | custom-call | flops 9663676416 | bytes 37748736 | tf_op jit(solution)/shard_map/hidden_back/pallas_call | solution.py:347
  482.5 10.7 fusion.119
  494.6 28.9 %weight_sum.10 = bf16[16,1,192,1536]{3,2,1,0:T(8,128)(2,1)} custom-call(bf16[1,512,3072]{2,1,0:T(8,128)(2,1)} %get-tuple-element.233.refs_0_, bf16[1,512,3072]{2,1,0:T(8,128)(2,1)} %get-tuple-element.234.refs_1_, bf16[1,512,3072]{2,1,0:T(8,128)(2,1)} %get-tuple-element.275.refs_2_, bf16[1,512,3072]{2,1,0:T(8,128)(2,1)} %get-tuple-element.236.refs_3_, ...), custom_call_target="tpu_custom_call" | custom-call | flops 19327352832 | bytes 28311552 | tf_op jit(solution)/shard_map/weight_sum/pallas_call | solution.py:412
  524.2 11.6 multiply_reduce_fusion.1
  562.2 11.0 multiply_reduce_fusion
  587.0 9.2 weight_sum.11.refs_0_
  600.5 26.8 %weight_sum.13 = (bf16[8,96,3072]{2,1,0:T(8,128)(2,1)}, bf16[8,96,3072]{2,1,0:T(8,128)(2,1)}) custom-call(s32[1]{0:T(128)} %bitcast.52.refs_0_, bf16[1,512,1536]{2,1,0:T(8,128)(2,1)} %add_convert_fusion.6.refs_1_, bf16[1,512,1536]{2,1,0:T(8,128)(2,1)} %collective-permute-done.10.refs_2_, bf16[1,512,1536]{2,1,0:T(8,128)(2,1)} %add_convert_fusion.5.refs_3_, ...), custom_call_target="tpu_custom_call" | custom-call | flops 19327352832 | bytes 28311552 | tf_op jit(solution)/shard_map/weight_sum/pallas_call | solution.py:412
  631.3 22.6 %collective-permute-done.17 = bf16[2,96,768]{2,1,0:T(8,128)(2,1)} collective-permute-done((bf16[2,96,768]{2,1,0:T(8,128)(2,1)}, bf16[2,96,768]{2,1,0:T(8,128)(2,1)}, u32[]{:S(2)}, u32[]{:S(2)}) %collective-permute-start.17) | collective-permute-done | bytes 294944 | tf_op jit(solution)/shard_map/ppermute | solution.py:521
  655.7 33.4 %attend_back.4 = (bf16[1,512,2304]{2,1,0:T(8,128)(2,1)}, bf16[1,512,2304]{2,1,0:T(8,128)(2,1)}, bf16[1,96,2304]{2,1,0:T(8,128)(2,1)}, bf16[1,96,2304]{2,1,0:T(8,128)(2,1)}, f32[3,8,128]{2,1,0:T(8,128)}) custom-call(f32[2,512,2304]{2,1,0:T(8,128)} %fusion.9.refs_0_.refs_1_.refs_2_.refs_4_.refs_5_.refs_6_, ...), custom_call_target="tpu_custom_call" | custom-call | flops 11356078080 | bytes 10272768 | tf_op jit(solution)/shard_map/attend_back/pallas_call | solution.py:296
  700.7 33.5 %attend_back.5 = (bf16[1,512,2304]{2,1,0:T(8,128)(2,1)}, bf16[1,512,2304]{2,1,0:T(8,128)(2,1)}, bf16[1,96,2304]{2,1,0:T(8,128)(2,1)}, bf16[1,96,2304]{2,1,0:T(8,128)(2,1)}, f32[3,8,128]{2,1,0:T(8,128)}) custom-call(bf16[1,512,2304]{2,1,0:T(8,128)(2,1)} %get-tuple-element.226.refs_0_, ...), custom_call_target="tpu_custom_call", output_to_operand_aliasing={{0}: (0, {}), {1}: (1, {}), {2}: (2, {}), {3}: (3, {})} | custom-call | flops 11356078080 | bytes 10272768 | tf_op jit(solution)/shard_map/attend_back/pallas_call | solution.py:296
  734.2 31.1 %collective-permute-done.18 = bf16[4,96,3072]{2,1,0:T(8,128)(2,1)} collective-permute-done((bf16[4,96,3072]{2,1,0:T(8,128)(2,1)}, bf16[4,96,3072]{2,1,0:T(8,128)(2,1)}, u32[]{:S(2)}, u32[]{:S(2)}) %collective-permute-start.18) | collective-permute-done | bytes 2359328 | tf_op jit(solution)/shard_map/ppermute | solution.py:539
  810.9 33.1 %attend_back.6 = (bf16[1,512,2304]{2,1,0:T(8,128)(2,1)}, bf16[1,512,2304]{2,1,0:T(8,128)(2,1)}, bf16[1,96,2304]{2,1,0:T(8,128)(2,1)}, bf16[1,96,2304]{2,1,0:T(8,128)(2,1)}, f32[3,8,128]{2,1,0:T(8,128)}) custom-call(f32[2,512,2304]{2,1,0:T(8,128)} %fusion.9.refs_0_.refs_1_.refs_2_.refs_4_.refs_5_.refs_6_, ...), custom_call_target="tpu_custom_call" | custom-call | flops 11356078080 | bytes 10272768 | tf_op jit(solution)/shard_map/attend_back/pallas_call | solution.py:296
  846.9 33.3 %attend_back.7 = (bf16[1,512,2304]{2,1,0:T(8,128)(2,1)}, bf16[1,512,2304]{2,1,0:T(8,128)(2,1)}, bf16[1,96,2304]{2,1,0:T(8,128)(2,1)}, bf16[1,96,2304]{2,1,0:T(8,128)(2,1)}, f32[3,8,128]{2,1,0:T(8,128)}) custom-call(bf16[1,512,2304]{2,1,0:T(8,128)(2,1)} %get-tuple-element.242.refs_0_, ...), custom_call_target="tpu_custom_call", output_to_operand_aliasing={{0}: (0, {}), {1}: (1, {}), {2}: (2, {}), {3}: (3, {})} | custom-call | flops 11356078080 | bytes 10272768 | tf_op jit(solution)/shard_map/attend_back/pallas_call | solution.py:296
  883.1 21.3 %weight_sum.14 = (bf16[8,96,2304]{2,1,0:T(8,128)(2,1)}, bf16[8,96,2304]{2,1,0:T(8,128)(2,1)}) custom-call(s32[1]{0:T(128)} %bitcast.52.refs_0_, bf16[2,512,1536]{2,1,0:T(8,128)(2,1)} %get-tuple-element.473.refs_1_.refs_3_, bf16[2,512,1536]{2,1,0:T(8,128)(2,1)} %get-tuple-element.472.refs_2_.refs_4_, ...), custom_call_target="tpu_custom_call" | custom-call | flops 14495514624 | bytes 22806528 | tf_op jit(solution)/shard_map/weight_sum/pallas_call | solution.py:412
  968.2 10.5 fusion.69
  1010.2 10.7 fusion.63
  1030.3 9.4 multiply_reduce_fusion.2
  1055.2 11.9 %collective-permute-done.35 = bf16[1,96,2304]{2,1,0:T(8,128)(2,1)S(1)} collective-permute-done((bf16[1,96,2304]{2,1,0:T(8,128)(2,1)S(1)}, bf16[1,96,2304]{2,1,0:T(8,128)(2,1)S(1)}, u32[]{:S(2)}, u32[]{:S(2)}) %collective-permute-start.35) | collective-permute-done | bytes 442400 | tf_op jit(solution)/shard_map/ppermute | solution.py:539
  1075.4 23.6 %collective-permute-done.34 = bf16[2,96,2304]{2,1,0:T(8,128)(2,1)} collective-permute-done((bf16[2,96,2304]{2,1,0:T(8,128)(2,1)}, bf16[2,96,2304]{2,1,0:T(8,128)(2,1)}, u32[]{:S(2)}, u32[]{:S(2)}) %collective-permute-start.34) | collective-permute-done | bytes 884768 | tf_op jit(solution)/shard_map/ppermute | solution.py:539
  1114.7 16.9 %collective-permute-done.36 = bf16[1,96,2304]{2,1,0:T(8,128)(2,1)S(1)} collective-permute-done((bf16[1,96,2304]{2,1,0:T(8,128)(2,1)S(1)}, bf16[1,96,2304]{2,1,0:T(8,128)(2,1)S(1)}, u32[]{:S(2)}, u32[]{:S(2)}) %collective-permute-start.36) | collective-permute-done | bytes 442400 | tf_op jit(solution)/shard_map/ppermute | solution.py:539
  (690 shorter events, 486.9 us)
Async XLA Ops:
  7.2 147.4 %all-gather.8.cloned.1.call-start = ((), (), s32[]{:S(2)}) async-start(), calls=%async_computation.7 | async-start | bytes 25067520 | tf_op jit(solution)/shard_map/all_gather | solution.py:639
  18.4 288.4 %all-gather.10.cloned.1.call-start = ((), (), s32[]{:S(2)}) async-start(), calls=%async_computation.8 | async-start | bytes 20054016 | tf_op jit(solution)/shard_map/all_gather | solution.py:664
  29.3 349.6 %all-gather.12.cloned.1.call-start = ((), (), s32[]{:S(2)}) async-start(), calls=%async_computation.13 | async-start | bytes 20054016 | tf_op jit(solution)/shard_map/all_gather | solution.py:665
  39.3 917.2 %reduce-scatter.7.cloned.1.call-start = ((), (), s32[]{:S(2)}) async-start(), calls=%async_computation.10 | async-start | bytes 10027008 | tf_op jit(solution)/shard_map/reduce_scatter | solution.py:784
  41.3 96.2 %collective-permute-start.2 = (bf16[2,96,1536]{2,1,0:T(8,128)(2,1)}, bf16[2,96,1536]{2,1,0:T(8,128)(2,1)}, u32[]{:S(2)}, u32[]{:S(2)}) collective-permute-start(bf16[2,96,1536]{2,1,0:T(8,128)(2,1)} %pad.7), channel_id=1, source_target_pairs={{0,1},{1,0},{2,3},{3,2},{4,5},{5,4},{6,7},{7,6},{8,9},{9,8},{10,11... | collective-permute-start | bytes 1769480 | tf_op jit(solution)/shard_map/ppermute | solution.py:521
  42.8 94.7 %collective-permute-start.1 = (bf16[2,512,1536]{2,1,0:T(8,128)(2,1)}, bf16[2,512,1536]{2,1,0:T(8,128)(2,1)}, u32[]{:S(2)}, u32[]{:S(2)}) collective-permute-start(bf16[2,512,1536]{2,1,0:T(8,128)(2,1)} %param.16), channel_id=1, source_target_pairs={{0,1},{1,0},{2,3},{3,2},{4,5},{5,4},{6,7},{7,6},{8,9},{9,8},{10,11... | collective-permute-start | bytes 9437192 | tf_op jit(solution)/shard_map/ppermute | solution.py:521
  137.6 124.3 %collective-permute-start.5 = (bf16[2,96,1536]{2,1,0:T(8,128)(2,1)}, bf16[2,96,1536]{2,1,0:T(8,128)(2,1)}, u32[]{:S(2)}, u32[]{:S(2)}) collective-permute-start(bf16[2,96,1536]{2,1,0:T(8,128)(2,1)} %pad.8), channel_id=1, source_target_pairs={{0,1},{1,0},{2,3},{3,2},{4,5},{5,4},{6,7},{7,6},{8,9},{9,8},{10,11... | collective-permute-start | bytes 1769480 | tf_op jit(solution)/shard_map/ppermute | solution.py:521
  139.0 122.8 %collective-permute-start.4 = (bf16[2,512,1536]{2,1,0:T(8,128)(2,1)}, bf16[2,512,1536]{2,1,0:T(8,128)(2,1)}, u32[]{:S(2)}, u32[]{:S(2)}) collective-permute-start(bf16[2,512,1536]{2,1,0:T(8,128)(2,1)} %param.26), channel_id=1, source_target_pairs={{0,1},{1,0},{2,3},{3,2},{4,5},{5,4},{6,7},{7,6},{8,9},{9,8},{10,11... | collective-permute-start | bytes 9437192 | tf_op jit(solution)/shard_map/ppermute | solution.py:521
  224.5 73.0 %collective-permute-start.6 = (bf16[1,96,768]{2,1,0:T(8,128)(2,1)}, bf16[1,96,768]{2,1,0:T(8,128)(2,1)S(1)}, u32[]{:S(2)}, u32[]{:S(2)}) collective-permute-start(bf16[1,96,768]{2,1,0:T(8,128)(2,1)} %get-tuple-element.178.refs_19_.refs_23_), channel_id=1, source_target_pairs={{0,1},{1,0},{2,3},{3,2},{4,5},{5,4},{6,7},{7,6},{8,9},{9,8},{10,11... | collective-permute-start | bytes 442376 | tf_op jit(solution)/shard_map/ppermute | solution.py:521
  296.7 73.9 %collective-permute-start.11 = (bf16[1,512,1536]{2,1,0:T(8,128)(2,1)}, bf16[1,512,1536]{2,1,0:T(8,128)(2,1)}, u32[]{:S(2)}, u32[]{:S(2)}) collective-permute-start(bf16[1,512,1536]{2,1,0:T(8,128)(2,1)} %add_convert_fusion.5.refs_3_), channel_id=1, source_target_pairs={{0,1},{1,0},{2,3},{3,2},{4,5},{5,4},{6,7},{7,6},{8,9},{9,8},{10,11... | collective-permute-start | bytes 4718600 | tf_op jit(solution)/shard_map/ppermute | solution.py:521
  305.6 57.3 %collective-permute-start.9 = (bf16[2,96,1536]{2,1,0:T(8,128)(2,1)}, bf16[2,96,1536]{2,1,0:T(8,128)(2,1)}, u32[]{:S(2)}, u32[]{:S(2)}) collective-permute-start(bf16[2,96,1536]{2,1,0:T(8,128)(2,1)} %add_convert_fusion.12), channel_id=1, source_target_pairs={{0,1},{1,0},{2,3},{3,2},{4,5},{5,4},{6,7},{7,6},{8,9},{9,8},{10,11... | collective-permute-start | bytes 1769480 | tf_op jit(solution)/shard_map/ppermute | solution.py:521
  409.7 546.9 %reduce-scatter.9.cloned.1.call-start = ((), (), s32[]{:S(2)}) async-start(), calls=%async_computation.11 | async-start | bytes 10027008 | tf_op jit(solution)/shard_map/reduce_scatter | solution.py:784
  418.5 538.1 %reduce-scatter.5.cloned.1.call-start = ((), (), s32[]{:S(2)}) async-start(), calls=%async_computation.9 | async-start | bytes 10027008 | tf_op jit(solution)/shard_map/reduce_scatter | solution.py:784
  458.6 64.9 %collective-permute-start.13 = (bf16[1,512,1536]{2,1,0:T(8,128)(2,1)}, bf16[1,512,1536]{2,1,0:T(8,128)(2,1)}, u32[]{:S(2)}, u32[]{:S(2)}) collective-permute-start(bf16[1,512,1536]{2,1,0:T(8,128)(2,1)} %fusion.122), channel_id=1, source_target_pairs={{0,1},{1,0},{2,3},{3,2},{4,5},{5,4},{6,7},{7,6},{8,9},{9,8},{10,11... | collective-permute-start | bytes 4718600 | tf_op jit(solution)/shard_map/ppermute | solution.py:521
  460.0 90.3 %collective-permute-start.12 = (bf16[2,96,1536]{2,1,0:T(8,128)(2,1)}, bf16[2,96,1536]{2,1,0:T(8,128)(2,1)}, u32[]{:S(2)}, u32[]{:S(2)}) collective-permute-start(bf16[2,96,1536]{2,1,0:T(8,128)(2,1)} %bitcast.54), channel_id=1, source_target_pairs={{0,1},{1,0},{2,3},{3,2},{4,5},{5,4},{6,7},{7,6},{8,9},{9,8},{10,11... | collective-permute-start | bytes 1769480 | tf_op jit(solution)/shard_map/ppermute | solution.py:521
  493.2 68.9 %collective-permute-start.14 = (bf16[1,512,1536]{2,1,0:T(8,128)(2,1)}, bf16[1,512,1536]{2,1,0:T(8,128)(2,1)}, u32[]{:S(2)}, u32[]{:S(2)}) collective-permute-start(bf16[1,512,1536]{2,1,0:T(8,128)(2,1)} %fusion.119), channel_id=1, source_target_pairs={{0,1},{1,0},{2,3},{3,2},{4,5},{5,4},{6,7},{7,6},{8,9},{9,8},{10,11... | collective-permute-start | bytes 4718600 | tf_op jit(solution)/shard_map/ppermute | solution.py:521
  523.5 433.1 %reduce-scatter.11.cloned.1.call-start = ((), (), s32[]{:S(2)}) async-start(), calls=%async_computation.12 | async-start | bytes 10027008 | tf_op jit(solution)/shard_map/reduce_scatter | solution.py:883
  627.3 61.8 %collective-permute-start.15 = (bf16[8,96,3072]{2,1,0:T(8,128)(2,1)}, bf16[8,96,3072]{2,1,0:T(8,128)(2,1)}, u32[]{:S(2)}, u32[]{:S(2)}) collective-permute-start(bf16[8,96,3072]{2,1,0:T(8,128)(2,1)} %get-tuple-element.222), channel_id=1, source_target_pairs={{0,2},{2,0},{4,6},{6,4},{8,10},{10,8},{12,14},{14,12},{16,18},{18,... | collective-permute-start | bytes 14155784 | tf_op jit(solution)/shard_map/ppermute | solution.py:539
  693.3 72.0 %collective-permute-start.18 = (bf16[4,96,3072]{2,1,0:T(8,128)(2,1)}, bf16[4,96,3072]{2,1,0:T(8,128)(2,1)}, u32[]{:S(2)}, u32[]{:S(2)}) collective-permute-start(bf16[4,96,3072]{2,1,0:T(8,128)(2,1)} %fusion.134), channel_id=1, source_target_pairs={{0,4},{2,6},{4,0},{6,2},{8,12},{10,14},{12,8},{14,10},{16,20},{18,... | collective-permute-start | bytes 7077896 | tf_op jit(solution)/shard_map/ppermute | solution.py:539
  696.7 114.2 %collective-permute-start.21 = (bf16[1,512,768]{2,1,0:T(8,128)(2,1)}, bf16[1,512,768]{2,1,0:T(8,128)(2,1)}, u32[]{:S(2)}, u32[]{:S(2)}) collective-permute-start(bf16[1,512,768]{2,1,0:T(8,128)(2,1)} %get-tuple-element.433), channel_id=1, source_target_pairs={{0,1},{1,0},{2,3},{3,2},{4,5},{5,4},{6,7},{7,6},{8,9},{9,8},{10,11... | collective-permute-start | bytes 2359304 | tf_op jit(solution)/shard_map/ppermute | solution.py:521
  696.9 437.6 %all-gather.14.cloned.1.call-start = ((), (), s32[]{:S(2)}) async-start(), calls=%async_computation.14 | async-start | bytes 2541568 | tf_op jit(solution)/shard_map/all_gather | solution.py:1021
  768.3 75.7 %collective-permute-start.20 = (bf16[2,96,3072]{2,1,0:T(8,128)(2,1)}, bf16[2,96,3072]{2,1,0:T(8,128)(2,1)}, u32[]{:S(2)}, u32[]{:S(2)}) collective-permute-start(bf16[2,96,3072]{2,1,0:T(8,128)(2,1)} %fusion.177), channel_id=1, source_target_pairs={{0,8},{2,10},{4,12},{6,14},{8,0},{10,2},{12,4},{14,6},{16,24},{18,... | collective-permute-start | bytes 3538952 | tf_op jit(solution)/shard_map/ppermute | solution.py:539
  800.8 82.3 %collective-permute-start.23 = (bf16[1,512,1536]{2,1,0:T(8,128)(2,1)}, bf16[1,512,1536]{2,1,0:T(8,128)(2,1)}, u32[]{:S(2)}, u32[]{:S(2)}) collective-permute-start(bf16[1,512,1536]{2,1,0:T(8,128)(2,1)} %fusion.113), channel_id=1, source_target_pairs={{0,1},{1,0},{2,3},{3,2},{4,5},{5,4},{6,7},{7,6},{8,9},{9,8},{10,11... | collective-permute-start | bytes 4718600 | tf_op jit(solution)/shard_map/ppermute | solution.py:521
  800.8 82.3 %collective-permute-start.19 = (bf16[1,512,1536]{2,1,0:T(8,128)(2,1)}, bf16[1,512,1536]{2,1,0:T(8,128)(2,1)}, u32[]{:S(2)}, u32[]{:S(2)}) collective-permute-start(bf16[1,512,1536]{2,1,0:T(8,128)(2,1)} %fusion.116), channel_id=1, source_target_pairs={{0,1},{1,0},{2,3},{3,2},{4,5},{5,4},{6,7},{7,6},{8,9},{9,8},{10,11... | collective-permute-start | bytes 4718600 | tf_op jit(solution)/shard_map/ppermute | solution.py:521
  802.8 80.2 %collective-permute-start.24 = (bf16[2,96,1536]{2,1,0:T(8,128)(2,1)}, bf16[2,96,1536]{2,1,0:T(8,128)(2,1)}, u32[]{:S(2)}, u32[]{:S(2)}) collective-permute-start(bf16[2,96,1536]{2,1,0:T(8,128)(2,1)} %bitcast.91), channel_id=1, source_target_pairs={{0,1},{1,0},{2,3},{3,2},{4,5},{5,4},{6,7},{7,6},{8,9},{9,8},{10,11... | collective-permute-start | bytes 1769480 | tf_op jit(solution)/shard_map/ppermute | solution.py:521
  908.8 58.0 %collective-permute-start.26 = (bf16[1,512,1536]{2,1,0:T(8,128)(2,1)}, bf16[1,512,1536]{2,1,0:T(8,128)(2,1)}, u32[]{:S(2)}, u32[]{:S(2)}) collective-permute-start(bf16[1,512,1536]{2,1,0:T(8,128)(2,1)} %fusion.128), channel_id=1, source_target_pairs={{0,1},{1,0},{2,3},{3,2},{4,5},{5,4},{6,7},{7,6},{8,9},{9,8},{10,11... | collective-permute-start | bytes 4718600 | tf_op jit(solution)/shard_map/ppermute | solution.py:521
  916.9 184.7 %collective-permute-start.37 = (f32[48,3072]{1,0:T(8,128)}, f32[48,3072]{1,0:T(8,128)}, u32[]{:S(2)}, u32[]{:S(2)}) collective-permute-start(f32[48,3072]{1,0:T(8,128)} %get-tuple-element.440), channel_id=1, source_target_pairs={{0,1},{1,0},{2,3},{3,2},{4,5},{5,4},{6,7},{7,6},{8,9},{9,8},{10,11... | collective-permute-start | bytes 1769480 | tf_op jit(solution)/shard_map/ppermute | solution.py:521
  925.3 85.0 %collective-permute-start.28 = (bf16[1,512,1536]{2,1,0:T(8,128)(2,1)}, bf16[1,512,1536]{2,1,0:T(8,128)(2,1)}, u32[]{:S(2)}, u32[]{:S(2)}) collective-permute-start(bf16[1,512,1536]{2,1,0:T(8,128)(2,1)} %fusion.125), channel_id=1, source_target_pairs={{0,1},{1,0},{2,3},{3,2},{4,5},{5,4},{6,7},{7,6},{8,9},{9,8},{10,11... | collective-permute-start | bytes 4718600 | tf_op jit(solution)/shard_map/ppermute | solution.py:521
  931.3 62.8 %collective-permute-start.30 = (bf16[4,96,2304]{2,1,0:T(8,128)(2,1)}, bf16[4,96,2304]{2,1,0:T(8,128)(2,1)}, u32[]{:S(2)}, u32[]{:S(2)}) collective-permute-start(bf16[4,96,2304]{2,1,0:T(8,128)(2,1)} %fusion.145), channel_id=1, source_target_pairs={{0,4},{2,6},{4,0},{6,2},{8,12},{10,14},{12,8},{14,10},{16,20},{18,... | collective-permute-start | bytes 5308424 | tf_op jit(solution)/shard_map/ppermute | solution.py:539
  966.8 134.8 %collective-permute-start.38 = (f32[48,3072]{1,0:T(8,128)}, f32[48,3072]{1,0:T(8,128)}, u32[]{:S(2)}, u32[]{:S(2)}) collective-permute-start(f32[48,3072]{1,0:T(8,128)} %get-tuple-element.444), channel_id=1, source_target_pairs={{0,1},{1,0},{2,3},{3,2},{4,5},{5,4},{6,7},{7,6},{8,9},{9,8},{10,11... | collective-permute-start | bytes 1769480 | tf_op jit(solution)/shard_map/ppermute | solution.py:521
  994.1 107.5 %collective-permute-start.39 = (f32[48,2,1536]{2,0,1:T(8,128)}, f32[48,2,1536]{2,0,1:T(8,128)}, u32[]{:S(2)}, u32[]{:S(2)}) collective-permute-start(f32[48,2,1536]{2,0,1:T(8,128)} %get-tuple-element.445), channel_id=1, source_target_pairs={{0,1},{1,0},{2,3},{3,2},{4,5},{5,4},{6,7},{7,6},{8,9},{9,8},{10,11... | collective-permute-start | bytes 1769480 | tf_op jit(solution)/shard_map/ppermute | solution.py:521
  1073.6 70.9 %collective-permute-start.40 = (f32[48,2304]{1,0:T(8,128)}, f32[48,2304]{1,0:T(8,128)}, u32[]{:S(2)}, u32[]{:S(2)}) collective-permute-start(f32[48,2304]{1,0:T(8,128)} %get-tuple-element.453), channel_id=1, source_target_pairs={{0,1},{1,0},{2,3},{3,2},{4,5},{5,4},{6,7},{7,6},{8,9},{9,8},{10,11... | collective-permute-start | bytes 1327112 | tf_op jit(solution)/shard_map/ppermute | solution.py:521
  (178 other events, 1841.8 us)
Sparse Core Ops, SparseCore 0:
  10.4 142.8 all-gather.7
  155.4 104.3 all-gather.9
  261.4 98.9 all-gather.11
  409.8 117.7 reduce-scatter.6
  532.0 111.0 reduce-scatter.8
  647.1 128.6 reduce-scatter.4
  780.5 124.1 reduce-scatter.10
  1075.5 53.2 all-gather.13

commit v3 on v2

--- a/solution.py
+++ b/solution.py
@@ -322,48 +322,47 @@
     return extent
 
 
-def hidden_back(hidden, grads, weight, modality):
-    width = weight.shape[2]
-    units = weight.shape[1]
+def feed_forward(values, grads, weight_in, weight_out, modality):
+    width = weight_out.shape[2]
+    units = weight_out.shape[1]
     tile = tile_of(units)
-    rows = rows_of(hidden)
+    rows = rows_of(values)
     count = len(rows)
 
     def kernel(*refs):
-        weight_ref = refs[2 * count]
+        in_ref, out_ref = refs[2 * count : 2 * count + 2]
+        slope = math.sqrt(2 / math.pi)
         for i in range(count):
-            value = refs[i][0]
-            grad = dot(refs[count + i][0], weight_ref[0], NT)
+            value = dot(refs[i][0], in_ref[0])
+            grad = dot(refs[count + i][0], out_ref[0], NT)
             square = value * value
-            slope = math.sqrt(2 / math.pi)
             bent = jnp.tanh(value * (slope + (slope * 0.044715) * square))
             half = 0.5 * value
             rise = 0.5 + 0.5 * bent
-            refs[2 * count + 1 + i][0] = (half + half * bent).astype(BF16)
+            refs[2 * count + 2 + i][0] = (value * rise).astype(BF16)
             rise = rise + half * (1.0 - bent * bent) * (slope + (3 * slope * 0.044715) * square)
-            refs[3 * count + 1 + i][0] = (grad * rise).astype(BF16)
+            refs[3 * count + 2 + i][0] = (grad * rise).astype(BF16)
 
     total = sum(rows)
     outputs = pl.pallas_call(
         kernel,
         grid=(units // tile,),
         in_specs=[
-            pl.BlockSpec((1, size, tile), lambda j, sel=sel: (sel, 0, j))
-            for (_, sel), size in zip(hidden, rows)
+            pl.BlockSpec((1, size, width), lambda j, sel=sel: (sel, 0, 0))
+            for (_, sel), size in zip(list(values) + list(grads), rows * 2)
         ]
         + [
-            pl.BlockSpec((1, size, width), lambda j, sel=sel: (sel, 0, 0))
-            for (_, sel), size in zip(grads, rows)
-        ]
-        + [pl.BlockSpec((1, tile, width), lambda j: (modality, j, 0))],
+            pl.BlockSpec((1, width, tile), lambda j: (modality, 0, j)),
+            pl.BlockSpec((1, tile, width), lambda j: (modality, j, 0)),
+        ],
         out_specs=[pl.BlockSpec((1, size, tile), lambda j: (0, 0, j)) for size in rows] * 2,
         out_shape=[jax.ShapeDtypeStruct((1, size, units), BF16) for size in rows] * 2,
         compiler_params=PARAMS,
         cost_estimate=cost(
-            2 * total * width * units, total * (2 * width + 8 * units) + 2 * units * width, total * units
+            4 * total * width * units, total * 4 * (width + units) + 4 * units * width, total * units
         ),
-        name="hidden_back",
-    )(*[a for a, _ in hidden], *[a for a, _ in grads], weight)
+        name="feed_forward",
+    )(*[a for a, _ in values], *[a for a, _ in grads], weight_in, weight_out)
     return (list(outputs[:count]), list(outputs[count:]))
 
 
@@ -394,21 +393,25 @@
             for j in range(run // 2):
                 even_rows = total[2 * j * block : (2 * j + 1) * block]
                 odd_rows = total[(2 * j + 1) * block : (2 * j + 2) * block]
-                keep_ref[j] = jnp.where(odd, odd_rows, even_rows).astype(BF16)
-                away_ref[j] = jnp.where(odd, even_rows, odd_rows).astype(BF16)
+                keep_ref[j, 0] = jnp.where(odd, odd_rows, even_rows).astype(BF16)
+                away_ref[j, 0] = jnp.where(odd, even_rows, odd_rows).astype(BF16)
 
     total = sum(sizes)
     if bit is None:
-        out_shape = jax.ShapeDtypeStruct((blocks, places, block, columns), BF16)
-        out_specs = pl.BlockSpec((run, 1, block, tile), lambda i, j: (i, place, 0, j))
+        arrays, divide = 1, 1
     else:
-        out_shape = [jax.ShapeDtypeStruct((blocks // 2, block, columns), BF16)] * 2
-        out_specs = [pl.BlockSpec((run // 2, block, tile), lambda i, j: (i, 0, j))] * 2
-    first_specs, first = [], []
+        arrays, divide = 2, 2
+    out_shape = [jax.ShapeDtypeStruct((blocks // divide, places, block, columns), BF16)] * arrays
+    out_specs = [
+        pl.BlockSpec((run // divide, 1, block, tile), lambda i, j: (i, place, 0, j))
+    ] * arrays
+    first_specs, first, aliases = [], [], {}
     if bit is not None:
         first_specs, first = [pl.BlockSpec(memory_space=pltpu.SMEM)], [bit]
-    elif before is not None:
-        first_specs, first = [pl.BlockSpec(memory_space=pl.ANY)], [before]
+    if before is not None:
+        aliases = {len(first) + i: i for i in range(arrays)}
+        first_specs = first_specs + [pl.BlockSpec(memory_space=pl.ANY)] * arrays
+        first = first + list(before)
     return pl.pallas_call(
         kernel,
         grid=(rows // row_tile, columns // tile),
@@ -424,7 +427,7 @@
         out_specs=out_specs,
         out_shape=out_shape,
         compiler_params=PARAMS,
-        input_output_aliases={} if before is None else {0: 0},
+        input_output_aliases=aliases,
         cost_estimate=cost(
             2 * total * rows * columns, 2 * (total * (rows + columns) + rows * columns)
         ),
@@ -763,15 +766,8 @@
         order.mark(normed)
         normed_mid.append(gather_seq(normed))
 
-    hidden = [[None] * members for _ in both] + [None]
     mlp_pieces = [[(mlp_img[k], s) for k in every] for s in both]
     mlp_pieces.append([(mlp_txt.reshape(1, -1, width), 0)])
-
-    def rise(u, k):
-        values = order(normed_mid[u][k])[0]
-        normed_mid[u][k] = values
-        hidden[u][k] = times(values, w_fc1[0])
-        order.mark(hidden[u][k])
 
     def reduction(lefts, rights):
         red = Reduction(weight_sum(lefts, rights, shards, own_bit))
@@ -779,7 +775,7 @@
         return red
 
     def scattered(lefts, rights):
-        summed = weight_sum(lefts, rights, shards)
+        summed = weight_sum(lefts, rights, shards)[0]
         order.mark(summed)
         return lax.psum_scatter(summed, "fsdp", scatter_dimension=0, tiled=True)[0, 0]
 
@@ -801,9 +797,11 @@
 
     def feed(u):
         t = kinds[u]
-        hidden[u][0] = order(hidden[u][0])[0]
-        active[u], hidden_grad[u] = hidden_back(
-            [(h, 0) for h in hidden[u]], mlp_pieces[u], w_fc2, t
+        normed_mid[u] = order(*normed_mid[u])
+        if t == 1:
+            normed_mid[u] = [jnp.concatenate(normed_mid[u], axis=0).reshape(1, -1, width)]
+        active[u], hidden_grad[u] = feed_forward(
+            at_first(normed_mid[u]), mlp_pieces[u], w_fc1, w_fc2, t
         )
         if t == 0:
             products = [times_t(values, w_fc1[t]).astype(BF16) for values in hidden_grad[u][1:]]
@@ -814,23 +812,14 @@
             order.mark(parts[0])
         came_mid[u] = to_owners(products)
 
-    for s in both:
-        rise(s, 0)
-    for k in range(1, members):
-        rise(0, k)
-    values = order(*normed_mid[text])
-    normed_mid[text] = [jnp.concatenate(values, axis=0).reshape(1, -1, width)]
-    hidden[text] = [times(normed_mid[text][0], w_fc1[1])]
-    order.mark(hidden[text][0])
-    for s in range(1, sequences):
-        for k in range(1, members):
-            rise(s, k)
+    for u in [*both, text]:
+        normed_mid[u] = order(*normed_mid[u])
+    order.mark(*[values for u in units for values in normed_mid[u][1:]])
     feed(text)
     ready = order(active[text][0], hidden_grad[text][0])
     fc2_txt = scattered(at_first(ready[:1]), mlp_pieces[text])
     fc1_txt = scattered(at_first(normed_mid[text]), at_first(ready[1:]))
-    feed(0)
-    for s in range(1, sequences):
+    for s in both:
         feed(s)
     active[0][0] = order(active[0][0])[0]
     fc2_img = scattered(
@@ -869,18 +858,18 @@
         head_grads[u] = [shift_seq(part, k) if k else part for k, part in enumerate(parts)]
     ready = order(branch_grad[text], branch_grad[0])
     branch_grad[text], branch_grad[0] = ready
-    proj_both = None
+    halves = None
     for t in range(2):
-        proj_both = weight_sum(
+        halves = weight_sum(
             at_first([own_attended[u].reshape(1, -1, width) for u in units if kinds[u] == t]),
             at_first([branch_grad[u].reshape(1, -1, width) for u in units if kinds[u] == t]),
             shards,
-            before=proj_both,
+            before=halves,
             place=t,
             places=2,
         )
-    order.mark(proj_both)
-    proj_both = lax.psum_scatter(proj_both, "fsdp", scatter_dimension=0, tiled=True)[0]
+    order.mark(*halves)
+    proj_both = lax.psum_scatter(halves[0], "fsdp", scatter_dimension=0, tiled=True)[0]
     hidden_grad[0][0] = order(hidden_grad[0][0])[0]
     fc1_img = reduction(at_first(of(normed_mid, 0)), at_first(of(hidden_grad, 0)))
     advance([], [fc1_img])
@@ -888,13 +877,35 @@
         [head_grads[s][k] for k in every] + [head_grads[text][k][s : s + 1] for k in every]
         for s in both
     ]
-    steps = {
-        (0, 0): [fc1_img],
-        (0, groups - 1): [fc1_img],
-        (sequences - 1, 0): [fc1_img],
-        (sequences - 1, groups - 1): [fc1_img],
-    }
-    gain_parts, raw_grads, came_in, came_mlp = [], [], [], None
+    def finish(reds):
+        while reds:
+            advance(reds, reds)
+            reds = [red for red in reds if red.bit < shards]
+
+    def send_rows(values):
+        blocks = values.reshape((members, -1) + values.shape[1:])
+        own = pick(blocks, member, 0)
+        parts = [pick(blocks, (member + k) % members, 0) for k in range(1, members)]
+        order.mark(own, *parts)
+        return [own] + [shift_seq(part, k) for k, part in enumerate(parts, 1)]
+
+    def by_place(parts):
+        stacked = jnp.stack(parts)
+        return [pick(stacked, (member - i) % members, 0) for i in every]
+
+    gain_parts, raw_grads, came_in, came_mlp = [], [], [], []
+    for u in units:
+        values = order(*active[u])
+        active[u] = values
+        if kinds[u] == 0:
+            products = [times(v, w_fc2[0]).astype(BF16) for v in values[1:]]
+            order.mark(*products)
+        else:
+            parts = text_members(times(values[0], w_fc2[1]))
+            own_text["mlp"], products = parts[0], parts[1:]
+            order.mark(parts[0])
+        came_mlp.append(to_owners(products))
+    advance([fc1_img], [fc1_img])
 
     def in_products(s):
         values = order(*raw_grads[s][1:members])
@@ -920,26 +931,24 @@
             )
             gain_parts.append(gain_part)
             order.mark(gain_part)
-            reds = steps.pop((s, group), [])
-            advance(reds, reds)
+            if (s, group) in ((sequences - 1, 0), (sequences - 1, groups - 1)):
+                advance([fc1_img], [fc1_img])
+            if (s, group) == (sequences - 1, 0):
+                came_mlp = [order(*came) for came in came_mlp]
+                order.mark(*[values for came in came_mlp for values in came])
+            if (s, group) == (sequences - 1, 0):
+                fc1_txt = send_rows(order(fc1_txt)[0].astype(F32))
         raw_grads.append(before)
-        if came_mlp is None:
-            came_mlp = []
-            for u in units:
-                values = order(*active[u])
-                active[u] = values
-                if kinds[u] == 0:
-                    products = [times(v, w_fc2[0]).astype(BF16) for v in values[1:]]
-                    order.mark(*products)
-                else:
-                    parts = text_members(times(values[0], w_fc2[1]))
-                    own_text["mlp"], products = parts[0], parts[1:]
-                    order.mark(parts[0])
-                came_mlp.append(to_owners(products))
+        if s == 0:
+            advance([fc1_img], [fc1_img])
         if s < sequences - 1:
             came_in.append(in_products(s))
-    came_mlp = [order(*came) for came in came_mlp]
-    values = gate(*order(*raw_grads[-1][:members]), *[v for came in came_mlp for v in came])[:members]
+    came_in = [order(*came) for came in came_in]
+    fc2_img, fc2_txt = order(fc2_img, fc2_txt)
+    fc1_txt = [fc1_txt[0], *order(*fc1_txt[1:])]
+    order.mark(fc2_img, fc2_txt)
+    order.mark(*[values for came in came_in for values in came], *fc1_txt)
+    values = order(*raw_grads[-1][:members])
     raw_grads[-1] = [*values, *raw_grads[-1][members:]]
     qkv_img = reduction(
         [(normed_img[k], s) for s in both for k in every],
@@ -950,15 +959,15 @@
     advance([qkv_img], [qkv_img])
     raw_text = jnp.concatenate([raw_grads[s][members + k] for k in every for s in both], axis=0)
     raw_text = order(raw_text)[0]
+    qkv_txt = reduction(
+        at_first([normed_txt.reshape(1, -1, width)]), at_first([raw_text.reshape(1, -1, triple)])
+    )
+    advance([], [qkv_txt])
+    raw_text = order(raw_text)[0]
     parts = text_members(times_t(raw_text, w_qkv[1]))
     own_text["in"] = parts[0]
     came_in.append(to_owners(parts[1:]))
     order.mark(parts[0])
-    raw_text = order(raw_text)[0]
-    qkv_txt = reduction(
-        at_first([normed_txt.reshape(1, -1, width)]), at_first([raw_text.reshape(1, -1, triple)])
-    )
-    advance([], [qkv_txt])
     in_grads, in_sums, outs, gate_sums = {}, {}, {}, {}
     tokens = own_in()
 
@@ -985,14 +994,18 @@
         gate_sums[u] = jnp.sum(grads_late[u] * mlp_out, axis=1)
         order.mark(outs[u], gate_sums[u])
 
+    grads_late = own_grad()
+    output(0)
     advance([qkv_txt], [qkv_txt])
-    grads_late = own_grad()
+    proj_both = order(proj_both)[0]
+    order.mark(proj_both)
+    advance([qkv_img], [qkv_img])
+    input_back(sequences - 1)
+    advance([qkv_img], [qkv_img])
+    input_back(text)
     for s in range(sequences - 1):
         input_back(s)
-    output(0)
-    advance([qkv_img], [qkv_img])
-    input_back(text)
-    input_back(sequences - 1)
+    advance([qkv_txt], [qkv_txt])
     for u in units:
         if u:
             output(u)
@@ -1011,72 +1024,64 @@
     own_shared = jnp.concatenate([mod_own.reshape(-1), gain_own])
     order.mark(own_shared)
     came_shared = gather_seq(own_shared)[1:]
-    qkv_red = [qkv_img, qkv_txt]
-    advance(qkv_red, qkv_red)
+    finish([fc1_img])
+    finish([qkv_img])
+    ready = order(fc2_img, fc2_txt)
+    order.mark(*ready)
+    qkv_rows = send_rows(qkv_img.result()[0])
     shared = sum(order(*came_shared), own_shared)
     gain_high = shared[mod_count:].astype(BF16)
     gain_low = (shared[mod_count:] - gain_high.astype(F32)).astype(BF16)
-    packed = jnp.concatenate([shared[:mod_count].astype(BF16), gain_high, gain_low])[None]
+    packed = jnp.concatenate([shared[:mod_count].astype(BF16), gain_high, gain_low])
+    packed = jnp.broadcast_to(packed.reshape(1, -1, LANES), (shards, packed.size // LANES, LANES))
     order.mark(packed)
-    packed = lax.all_gather(packed, "fsdp", axis=0, tiled=True)
-
-    def finish(reds):
-        while reds:
-            advance(reds, reds)
-            reds = [red for red in reds if red.bit < shards]
-
-    def send_rows(values):
-        blocks = values.reshape((members, -1) + values.shape[1:])
-        own = pick(blocks, member, 0)
-        parts = [pick(blocks, (member + k) % members, 0) for k in range(1, members)]
-        order.mark(own, *parts)
-        return [own] + [shift_seq(part, k) for k, part in enumerate(parts, 1)]
-
-    def by_place(parts):
-        stacked = jnp.stack([parts[0], *order(*parts[1:])])
-        return [pick(stacked, (member - i) % members, 0) for i in every]
-
-    finish([fc1_img])
-    ready = order(fc2_img, fc2_txt, fc1_txt, proj_both)
+    packed = lax.all_to_all(packed, "fsdp", split_axis=0, concat_axis=0, tiled=True)
+    advance([qkv_txt], [qkv_txt])
+
+    ready = order(*ready)
     fc2_grad = jnp.stack(ready[:2]).astype(F32)
-    fc1_rows = [send_rows(fc1_img.result()), send_rows(ready[2].astype(F32))]
-    proj_rows = send_rows(jnp.transpose(ready[3].astype(F32), (1, 0, 2)))
-    advance(qkv_red, qkv_red)
-    fc1_grad = jnp.stack([join_units(by_place(rows), shards) for rows in fc1_rows])
-    proj_grad = jnp.transpose(sum(order(*proj_rows[1:]), proj_rows[0]), (1, 0, 2))
-    order.mark(fc1_grad, proj_grad)
-    advance(qkv_red, qkv_red)
+    fc1_rows = send_rows(fc1_img.result()[0])
+    proj_rows = send_rows(jnp.transpose(proj_both.astype(F32), (1, 0, 2)))
+
+    def heads_apart(parts):
+        parts = by_place(parts)
+        return jnp.concatenate(
+            [
+                parts[m][:, (g * 3 + part) * group_width :][
+                    :, : min(group_width, head_width - g * group_width)
+                ]
+                for part in range(3)
+                for m in every
+                for g in range(groups)
+            ],
+            axis=1,
+        )
+
+    qkv_rows = [qkv_rows[0], *order(*qkv_rows[1:])]
+    image_grad = heads_apart(qkv_rows)
+    order.mark(image_grad, fc2_grad)
 
     packed = order(packed)[0]
-    every_mod = packed[:, :mod_count].reshape(shards * sequences, 2, mod_width)
-    gain_grad = jnp.sum(packed[:, mod_count:].astype(F32), axis=0).reshape(2, 2, 2 * HEAD).sum(axis=0)
+    mod_lanes = mod_count // LANES
+    every_mod = packed[:, :mod_lanes].reshape(shards * sequences, 2, mod_width)
+    gain_grad = jnp.sum(packed[:, mod_lanes:].astype(F32), axis=0)
+    gain_grad = gain_grad.reshape(2, 2, 2 * HEAD).sum(axis=0)
     cond_part = jnp.einsum("stm,tdm->sd", every_mod, ada_w, preferred_element_type=F32)
     order.mark(cond_part)
     cond_full = lax.all_to_all(cond_part, "fsdp", split_axis=0, concat_axis=1, tiled=True)
-    finish(qkv_red)
-    qkv_rows = [send_rows(red.result()) for red in qkv_red]
+    finish([qkv_txt])
+    text_rows_sent = send_rows(qkv_txt.result()[0])
     every_mod = order(every_mod)[0]
     out_rows = width // (shards * members)
     own_cols = lax.dynamic_slice_in_dim(cond_cols, member * out_rows, out_rows, 1)
     ada_grad = jnp.einsum("sr,stm->trm", own_cols, every_mod, preferred_element_type=F32)
-    cond_grad = jax.vjp(jax.nn.silu, cond.astype(F32))[1](cond_full)[0]
-    qkv_grad = []
-    for rows in qkv_rows:
-        parts = by_place(rows)
-        qkv_grad.append(
-            jnp.concatenate(
-                [
-                    parts[m][:, (g * 3 + part) * group_width :][
-                        :, : min(group_width, head_width - g * group_width)
-                    ]
-                    for part in range(3)
-                    for m in every
-                    for g in range(groups)
-                ],
-                axis=1,
-            )
-        )
-    qkv_grad = jnp.stack(qkv_grad)
+    proj_grad = jnp.transpose(sum(order(*proj_rows[1:]), proj_rows[0]), (1, 0, 2))
+    fc1_rows = [fc1_rows[0], *order(*fc1_rows[1:])]
+    fc1_grad = jnp.stack([join_units(by_place(rows), shards) for rows in (fc1_rows, fc1_txt)])
+    order.mark(ada_grad, proj_grad, fc1_grad)
+    cond_grad = jax.vjp(jax.nn.silu, cond.astype(F32))[1](order(cond_full)[0])[0]
+    text_grad = heads_apart([text_rows_sent[0], *order(*text_rows_sent[1:])])
+    qkv_grad = jnp.stack([image_grad, text_grad])
     return (
         img_out,
         txt_out,

time: 1180 us -> 1110 us (0.941)
  matrix products: 254 us -> 212 us
  waiting for transfers between devices: 211 us -> 169 us
    ppermute x12, waiting for transfers between devices: 83.4 us -> 39.8 us  [send(): lax.ppermute(self.away, 'fsdp', [(i, i ^ self.bit) for i in range(size)])]
    dot_general x16 -> x11, matrix products: 136 us -> 96.8 us  [times(): lax.dot_general(left, right, (((2,), (0,)), ((), ())), preferred_element_...]
    unnamed x357 -> x366, local copies, waits for them, and re-layouts: 25.8 us -> 23.6 us
  transfers between devices with their start and end apart: 53 -> 53, of which waited for: 10 -> 11; matrix products, arithmetic and copies ran while one was open for 40% -> 38% of each run, Pallas kernels for 31% -> 34%
where the time goes in v3:
time: 1110 us; the launch traced here: 1100 us
  Pallas kernels  399 us (36%)
  matrix products  212 us (19%)
  waiting for transfers between devices  169 us (15%)
  other arithmetic  150 us (14%)
  local copies, waits for them, and re-layouts  85.9 us (8%)
  starting transfers between devices  67.4 us (6%)
  between operations  17.3 us (2%)
    pallas_call x4, Pallas kernels, attend_back(): pl.pallas_call(kernel, grid=(count,), in_specs=in_specs, out_specs=[pl.Bl...  134 us
    pallas_call x8, Pallas kernels, weight_sum(): pl.pallas_call(kernel, grid=(rows // row_tile, columns // tile), in_specs...  116 us
    dot_general x13, matrix products, times_t(): lax.dot_general(left, right, (((2,), (1,)), ((), ())), preferred_element_...  107 us
    dot_general x11, matrix products, times(): lax.dot_general(left, right, (((2,), (0,)), ((), ())), preferred_element_...  96.8 us
    ppermute x30, waiting for transfers between devices, shift_seq(): lax.ppermute(values, 'seq', [(i, (i + amount) % members) for i in range(m...  91.3 us
    pallas_call x2, Pallas kernels, attend(): pl.pallas_call(kernel, grid=(pairs,), in_specs=[pl.BlockSpec((1, array.sh...  69.9 us
    pallas_call x3, Pallas kernels, feed_forward(): pl.pallas_call(kernel, grid=(units // tile,), in_specs=[pl.BlockSpec((1,...  67.9 us
    ppermute x12, waiting for transfers between devices, send(): lax.ppermute(self.away, 'fsdp', [(i, i ^ self.bit) for i in range(size)])  39.8 us
  transfers between devices with their start and end apart: 53, of which 11 were waited for; matrix products, arithmetic and copies ran while one was open for 38% of the time, Pallas kernels for 34%

profile of v3, /device:TPU:0, one launch (start us, length us, event | category | flops | bytes accessed | tf_op | source)
XLA Modules:
  0.0 1100.4 jit_solution(7033124542340265765)
XLA Ops:
  51.7 31.8 %all-to-all-done.1 = f32[16,2,2,4608]{3,2,1,0:T(2,128)} async-done(((f32[16,2,2,4608]{3,2,1,0:T(2,128)}), f32[16,2,2,4608]{3,2,1,0:T(2,128)}, u32[]{:S(2)}, u32[]{:S(2)}) %all-to-all-start.1) | async-done | bytes 1179680 | tf_op jit(solution)/shard_map/all_to_all | solution.py:658
  92.0 34.2 %collective-permute-done = f32[2,2,4608]{2,1,0:T(2,128)} collective-permute-done((f32[2,2,4608]{2,1,0:T(2,128)}, f32[2,2,4608]{2,1,0:T(2,128)}, u32[]{:S(2)}, u32[]{:S(2)}) %collective-permute-start) | collective-permute-done | bytes 73760 | tf_op jit(solution)/shard_map/ppermute | solution.py:524
  154.7 8.4 fusion.27.refs_6_.refs_7_.refs_8_.refs_9_.refs_10_.refs_11_.refs_12_.refs_13_.refs_14_.refs_15_
  163.1 12.9 %fusion.6.refs_3_.refs_4_.refs_5_.refs_7_.refs_8_.refs_9_ = f32[2,512,2304]{2,1,0:T(8,128)} fusion(bf16[2,512,1536]{2,1,0:T(8,128)(2,1)S(1)} %copy-done.43, bf16[2,1536,3840]{2,1,0:T(8,128)(2,1)} %all-gather.5.cloned.1.call-done), kind=kOutput, calls=%fused_computation.16 | convolution fusion | flops 7247757312 | bytes 19660800 | tf_op jit(solution)/shard_map/dot_general | solution.py:596
  176.0 12.8 %fusion.8.refs_0_.refs_1_.refs_2_.refs_4_.refs_5_.refs_6_ = f32[2,512,2304]{2,1,0:T(8,128)} fusion(bf16[2,512,1536]{2,1,0:T(8,128)(2,1)S(1)} %copy-done.44, bf16[2,1536,3840]{2,1,0:T(8,128)(2,1)} %all-gather.5.cloned.1.call-done), kind=kOutput, calls=%fused_computation.18 | convolution fusion | flops 7247757312 | bytes 19660800 | tf_op jit(solution)/shard_map/dot_general | solution.py:596
  189.7 34.9 %attend.2 = (bf16[1,512,768]{2,1,0:T(8,128)(2,1)}, bf16[1,512,768]{2,1,0:T(8,128)(2,1)}, bf16[1,96,768]{2,1,0:T(8,128)(2,1)}, bf16[1,96,768]{2,1,0:T(8,128)(2,1)}, f32[1,6,16,1216]{3,2,1,0:T(8,128)}) custom-call(f32[2,512,2304]{2,1,0:T(8,128)} %fusion.8.refs_0_.refs_1_.refs_2_.refs_4_.refs_5_.refs_6_, ...), custom_call_target="tpu_custom_call" | custom-call | flops 9084862464 | bytes 13074432 | tf_op jit(solution)/shard_map/attend/pallas_call | solution.py:230
  226.7 35.0 %attend.3 = (bf16[1,512,768]{2,1,0:T(8,128)(2,1)}, bf16[1,512,768]{2,1,0:T(8,128)(2,1)}, bf16[1,96,768]{2,1,0:T(8,128)(2,1)}, bf16[1,96,768]{2,1,0:T(8,128)(2,1)}, f32[1,6,16,1216]{3,2,1,0:T(8,128)}) custom-call(f32[2,512,2304]{2,1,0:T(8,128)} %fusion.8.refs_0_.refs_1_.refs_2_.refs_4_.refs_5_.refs_6_, ...), custom_call_target="tpu_custom_call" | custom-call | flops 9084862464 | bytes 13074432 | tf_op jit(solution)/shard_map/attend/pallas_call | solution.py:230
  307.1 55.7 %collective-permute-done.10 = bf16[2,96,1536]{2,1,0:T(8,128)(2,1)S(1)} collective-permute-done((bf16[2,96,1536]{2,1,0:T(8,128)(2,1)S(1)}, bf16[2,96,1536]{2,1,0:T(8,128)(2,1)S(1)}, u32[]{:S(2)}, u32[]{:S(2)}) %collective-permute-start.10) | collective-permute-done | bytes 589856 | tf_op jit(solution)/shard_map/ppermute | solution.py:524
  366.3 13.1 %feed_forward.3 = (bf16[1,384,3072]{2,1,0:T(8,128)(2,1)}, bf16[1,384,3072]{2,1,0:T(8,128)(2,1)}) custom-call(bf16[1,384,1536]{2,1,0:T(8,128)(2,1)} %bitcast.549, bf16[1,384,1536]{2,1,0:T(8,128)(2,1)} %fusion.147.refs_1_, bf16[2,1536,3072]{2,1,0:T(8,128)(2,1)} %all-gather.7.cloned.1.call-done.refs_2_.refs_4_, bf16[2,3072,1536]{2,1,0:T(8,128)(2,1)} %bitcast.516), custom_call_target="tpu_custom_call" | custom-call | flops 7247757312 | bytes 25952256 | tf_op jit(solution)/shard_map/feed_forward/pallas_call | solution.py:347
  389.2 8.7 weight_sum.9
  398.0 9.4 weight_sum.8
  420.0 27.9 %feed_forward.4 = (bf16[1,512,3072]{2,1,0:T(8,128)(2,1)}, bf16[1,512,3072]{2,1,0:T(8,128)(2,1)}, bf16[1,512,3072]{2,1,0:T(8,128)(2,1)}, bf16[1,512,3072]{2,1,0:T(8,128)(2,1)}) custom-call(bf16[1,512,1536]{2,1,0:T(8,128)(2,1)} %copy-done.57, bf16[1,512,1536]{2,1,0:T(8,128)(2,1)} %copy-done.145, ...), custom_call_target="tpu_custom_call" | custom-call | flops 19327352832 | bytes 37748736 | tf_op jit(solution)/shard_map/feed_forward/pallas_call | solution.py:347
  447.9 10.4 fusion.118
  459.0 26.9 %feed_forward.5 = (bf16[1,512,3072]{2,1,0:T(8,128)(2,1)}, bf16[1,512,3072]{2,1,0:T(8,128)(2,1)}, bf16[1,512,3072]{2,1,0:T(8,128)(2,1)}, bf16[1,512,3072]{2,1,0:T(8,128)(2,1)}) custom-call(bf16[1,512,1536]{2,1,0:T(8,128)(2,1)} %copy-done.59, bf16[1,512,1536]{2,1,0:T(8,128)(2,1)} %copy-done.146, ...), custom_call_target="tpu_custom_call" | custom-call | flops 19327352832 | bytes 37748736 | tf_op jit(solution)/shard_map/feed_forward/pallas_call | solution.py:347
  485.9 10.4 fusion.115
  497.6 28.8 %weight_sum.10 = bf16[16,1,192,1536]{3,2,1,0:T(8,128)(2,1)} custom-call(bf16[1,512,3072]{2,1,0:T(8,128)(2,1)} %get-tuple-element.232.refs_0_, bf16[1,512,3072]{2,1,0:T(8,128)(2,1)} %get-tuple-element.233.refs_1_, bf16[1,512,3072]{2,1,0:T(8,128)(2,1)} %get-tuple-element.284.refs_2_, bf16[1,512,3072]{2,1,0:T(8,128)(2,1)} %get-tuple-element.235.refs_3_, ...), custom_call_target="tpu_custom_call" | custom-call | flops 19327352832 | bytes 28311552 | tf_op jit(solution)/shard_map/weight_sum/pallas_call | solution.py:415
  526.6 12.9 %multiply_reduce_fusion.1 = (f32[1536]{0:T(1024)}, f32[512]{0:T(512)S(1)}, f32[512]{0:T(512)S(1)}, f32[1536]{0:T(1024)}, f32[1,512,1536]{2,1,0:T(8,128)S(1)}) fusion(f32[1,512,1536]{2,1,0:T(8,128)} %copy-done.12, f32[512]{0:T(512)} %copy-done.114, f32[512]{0:T(512)S(1)} %broadcast_multiply_fusion.13, bf16[1,512,1536]{2,1,0:T(8,128)(2,1)} %collective-permute-done.13, ...), kind=kOutput, calls=%fused_computation.119 | convolution fusion | flops 4840484864 | bytes 20475904 | tf_op jit(solution)/shard_map/dot_general | solution.py:600
  567.2 9.9 multiply_reduce_fusion
  591.6 9.2 weight_sum.11.refs_0_
  605.1 27.2 %weight_sum.13 = (bf16[8,1,96,3072]{3,2,1,0:T(8,128)(2,1)}, bf16[8,1,96,3072]{3,2,1,0:T(8,128)(2,1)}) custom-call(s32[1]{0:T(128)} %bitcast.42.refs_0_, bf16[1,512,1536]{2,1,0:T(8,128)(2,1)} %copy-done.57, bf16[1,512,1536]{2,1,0:T(8,128)(2,1)} %copy-done.145, bf16[1,512,1536]{2,1,0:T(8,128)(2,1)} %copy-done.59, bf16[1,512,1536]{2,1,0:T(8,128)(2,1)} %copy-done.146, ...), custom_call_target="tpu_custom_call" | custom-call | flops 19327352832 | bytes 28311552 | tf_op jit(solution)/shard_map/weight_sum/pallas_call | solution.py:415
  632.5 9.9 fusion.124
  642.5 9.0 fusion.121
  671.6 33.0 %attend_back.4 = (bf16[1,512,2304]{2,1,0:T(8,128)(2,1)}, bf16[1,512,2304]{2,1,0:T(8,128)(2,1)}, bf16[1,96,2304]{2,1,0:T(8,128)(2,1)}, bf16[1,96,2304]{2,1,0:T(8,128)(2,1)}, f32[3,8,128]{2,1,0:T(8,128)}) custom-call(f32[2,512,2304]{2,1,0:T(8,128)} %fusion.8.refs_0_.refs_1_.refs_2_.refs_4_.refs_5_.refs_6_, ...), custom_call_target="tpu_custom_call" | custom-call | flops 11356078080 | bytes 10272768 | tf_op jit(solution)/shard_map/attend_back/pallas_call | solution.py:296
  706.4 33.9 %attend_back.5 = (bf16[1,512,2304]{2,1,0:T(8,128)(2,1)}, bf16[1,512,2304]{2,1,0:T(8,128)(2,1)}, bf16[1,96,2304]{2,1,0:T(8,128)(2,1)}, bf16[1,96,2304]{2,1,0:T(8,128)(2,1)}, f32[3,8,128]{2,1,0:T(8,128)}) custom-call(bf16[1,512,2304]{2,1,0:T(8,128)(2,1)} %get-tuple-element.239.refs_0_, ...), custom_call_target="tpu_custom_call", output_to_operand_aliasing={{0}: (0, {}), {1}: (1, {}), {2}: (2, {}), {3}: (3, {})} | custom-call | flops 11356078080 | bytes 10272768 | tf_op jit(solution)/shard_map/attend_back/pallas_call | solution.py:296
  763.2 33.0 %attend_back.6 = (bf16[1,512,2304]{2,1,0:T(8,128)(2,1)}, bf16[1,512,2304]{2,1,0:T(8,128)(2,1)}, bf16[1,96,2304]{2,1,0:T(8,128)(2,1)}, bf16[1,96,2304]{2,1,0:T(8,128)(2,1)}, f32[3,8,128]{2,1,0:T(8,128)}) custom-call(f32[2,512,2304]{2,1,0:T(8,128)} %fusion.8.refs_0_.refs_1_.refs_2_.refs_4_.refs_5_.refs_6_, ...), custom_call_target="tpu_custom_call" | custom-call | flops 11356078080 | bytes 10272768 | tf_op jit(solution)/shard_map/attend_back/pallas_call | solution.py:296
  802.8 33.7 %attend_back.7 = (bf16[1,512,2304]{2,1,0:T(8,128)(2,1)}, bf16[1,512,2304]{2,1,0:T(8,128)(2,1)}, bf16[1,96,2304]{2,1,0:T(8,128)(2,1)}, bf16[1,96,2304]{2,1,0:T(8,128)(2,1)}, f32[3,8,128]{2,1,0:T(8,128)}) custom-call(bf16[1,512,2304]{2,1,0:T(8,128)(2,1)} %get-tuple-element.254.refs_0_, ...), custom_call_target="tpu_custom_call", output_to_operand_aliasing={{0}: (0, {}), {1}: (1, {}), {2}: (2, {}), {3}: (3, {})} | custom-call | flops 11356078080 | bytes 10272768 | tf_op jit(solution)/shard_map/attend_back/pallas_call | solution.py:296
  840.2 21.1 %weight_sum.14 = (bf16[8,1,96,2304]{3,2,1,0:T(8,128)(2,1)}, bf16[8,1,96,2304]{3,2,1,0:T(8,128)(2,1)}) custom-call(s32[1]{0:T(128)} %bitcast.42.refs_0_, bf16[2,512,1536]{2,1,0:T(8,128)(2,1)} %get-tuple-element.493.refs_1_.refs_3_, bf16[2,512,1536]{2,1,0:T(8,128)(2,1)} %get-tuple-element.492.refs_2_.refs_4_, ...), custom_call_target="tpu_custom_call" | custom-call | flops 14495514624 | bytes 22806528 | tf_op jit(solution)/shard_map/weight_sum/pallas_call | solution.py:415
  907.5 11.2 %multiply_reduce_fusion.3 = (f32[1536]{0:T(1024)}, bf16[1,512,1536]{2,1,0:T(8,128)(2,1)}) fusion(bf16[2,512,1536]{2,1,0:T(8,128)(2,1)S(1)} %copy-done.21, f32[1,512,1536]{2,1,0:T(8,128)S(1)} %copy-done.14, f32[1536]{0:T(1024)S(1)} %copy-done.131, bf16[1,512,1536]{2,1,0:T(8,128)(2,1)} %collective-permute-done.15, ...), kind=kOutput, calls=%fused_computation.123 | convolution fusion | flops 4838128128 | bytes 20459520 | tf_op jit(solution)/shard_map/dot_general | solution.py:596
  936.8 8.7 fusion.67
  966.6 10.3 fusion.73
  990.7 9.0 multiply_reduce_fusion.2
  1024.9 24.0 %collective-permute-done.38 = bf16[1,1,96,2304]{3,2,1,0:T(8,128)(2,1)} collective-permute-done((bf16[1,1,96,2304]{3,2,1,0:T(8,128)(2,1)}, bf16[1,1,96,2304]{3,2,1,0:T(8,128)(2,1)}, u32[]{:S(2)}, u32[]{:S(2)}) %collective-permute-start.38) | collective-permute-done | bytes 442400 | tf_op jit(solution)/shard_map/ppermute | solution.py:542
  (689 shorter events, 425.9 us)
Async XLA Ops:
  7.2 147.4 %all-gather.5.cloned.1.call-start = ((), (), s32[]{:S(2)}) async-start(), calls=%async_computation.8 | async-start | bytes 25067520 | tf_op jit(solution)/shard_map/all_gather | solution.py:642
  18.4 347.9 %all-gather.7.cloned.1.call-start = ((), (), s32[]{:S(2)}) async-start(), calls=%async_computation.9 | async-start | bytes 20054016 | tf_op jit(solution)/shard_map/all_gather | solution.py:667
  29.3 337.0 %all-gather.9.cloned.1.call-start = ((), (), s32[]{:S(2)}) async-start(), calls=%async_computation.14 | async-start | bytes 20054016 | tf_op jit(solution)/shard_map/all_gather | solution.py:668
  35.0 48.5 %all-to-all-start.1 = ((f32[16,2,2,4608]{3,2,1,0:T(2,128)}), f32[16,2,2,4608]{3,2,1,0:T(2,128)}, u32[]{:S(2)}, u32[]{:S(2)}) async-start(f32[16,2,2,4608]{3,2,1,0:T(2,128)} %copy.184), calls=%async_computation.1 | async-start | bytes 2359296 | tf_op jit(solution)/shard_map/all_to_all | solution.py:658
  39.4 760.5 %reduce-scatter.5.cloned.1.call-start = ((), (), s32[]{:S(2)}) async-start(), calls=%async_computation.10 | async-start | bytes 10027008 | tf_op jit(solution)/shard_map/reduce_scatter | solution.py:780
  41.4 96.2 %collective-permute-start.2 = (bf16[2,96,1536]{2,1,0:T(8,128)(2,1)}, bf16[2,96,1536]{2,1,0:T(8,128)(2,1)}, u32[]{:S(2)}, u32[]{:S(2)}) collective-permute-start(bf16[2,96,1536]{2,1,0:T(8,128)(2,1)} %pad.7), channel_id=1, source_target_pairs={{0,1},{1,0},{2,3},{3,2},{4,5},{5,4},{6,7},{7,6},{8,9},{9,8},{10,11... | collective-permute-start | bytes 1769480 | tf_op jit(solution)/shard_map/ppermute | solution.py:524
  42.9 94.7 %collective-permute-start.1 = (bf16[2,512,1536]{2,1,0:T(8,128)(2,1)}, bf16[2,512,1536]{2,1,0:T(8,128)(2,1)}, u32[]{:S(2)}, u32[]{:S(2)}) collective-permute-start(bf16[2,512,1536]{2,1,0:T(8,128)(2,1)} %param.16), channel_id=1, source_target_pairs={{0,1},{1,0},{2,3},{3,2},{4,5},{5,4},{6,7},{7,6},{8,9},{9,8},{10,11... | collective-permute-start | bytes 9437192 | tf_op jit(solution)/shard_map/ppermute | solution.py:524
  137.6 124.1 %collective-permute-start.5 = (bf16[2,96,1536]{2,1,0:T(8,128)(2,1)}, bf16[2,96,1536]{2,1,0:T(8,128)(2,1)}, u32[]{:S(2)}, u32[]{:S(2)}) collective-permute-start(bf16[2,96,1536]{2,1,0:T(8,128)(2,1)} %pad.8), channel_id=1, source_target_pairs={{0,1},{1,0},{2,3},{3,2},{4,5},{5,4},{6,7},{7,6},{8,9},{9,8},{10,11... | collective-permute-start | bytes 1769480 | tf_op jit(solution)/shard_map/ppermute | solution.py:524
  139.1 122.6 %collective-permute-start.4 = (bf16[2,512,1536]{2,1,0:T(8,128)(2,1)}, bf16[2,512,1536]{2,1,0:T(8,128)(2,1)}, u32[]{:S(2)}, u32[]{:S(2)}) collective-permute-start(bf16[2,512,1536]{2,1,0:T(8,128)(2,1)} %param.26), channel_id=1, source_target_pairs={{0,1},{1,0},{2,3},{3,2},{4,5},{5,4},{6,7},{7,6},{8,9},{9,8},{10,11... | collective-permute-start | bytes 9437192 | tf_op jit(solution)/shard_map/ppermute | solution.py:524
  224.6 72.2 %collective-permute-start.7 = (bf16[1,96,768]{2,1,0:T(8,128)(2,1)}, bf16[1,96,768]{2,1,0:T(8,128)(2,1)S(1)}, u32[]{:S(2)}, u32[]{:S(2)}) collective-permute-start(bf16[1,96,768]{2,1,0:T(8,128)(2,1)} %get-tuple-element.185.refs_19_.refs_23_), channel_id=1, source_target_pairs={{0,1},{1,0},{2,3},{3,2},{4,5},{5,4},{6,7},{7,6},{8,9},{9,8},{10,11... | collective-permute-start | bytes 442376 | tf_op jit(solution)/shard_map/ppermute | solution.py:524
  281.6 81.2 %collective-permute-start.6 = (bf16[1,512,1536]{2,1,0:T(8,128)(2,1)S(1)}, bf16[1,512,1536]{2,1,0:T(8,128)(2,1)S(1)}, u32[]{:S(2)}, u32[]{:S(2)}) collective-permute-start(bf16[1,512,1536]{2,1,0:T(8,128)(2,1)S(1)} %add_convert_fusion.6.refs_0_.refs_1_), channel_id=1, source_target_pairs={{0,1},{1,0},{2,3},{3,2},{4,5},{5,4},{6,7},{7,6},{8,9},{9,8},{10,11... | collective-permute-start | bytes 4718600 | tf_op jit(solution)/shard_map/ppermute | solution.py:524
  295.4 67.5 %collective-permute-start.11 = (bf16[1,512,1536]{2,1,0:T(8,128)(2,1)S(1)}, bf16[1,512,1536]{2,1,0:T(8,128)(2,1)S(1)}, u32[]{:S(2)}, u32[]{:S(2)}) collective-permute-start(bf16[1,512,1536]{2,1,0:T(8,128)(2,1)S(1)} %add_convert_fusion.5.refs_0_.refs_3_), channel_id=1, source_target_pairs={{0,1},{1,0},{2,3},{3,2},{4,5},{5,4},{6,7},{7,6},{8,9},{9,8},{10,11... | collective-permute-start | bytes 4718600 | tf_op jit(solution)/shard_map/ppermute | solution.py:524
  303.6 59.2 %collective-permute-start.10 = (bf16[2,96,1536]{2,1,0:T(8,128)(2,1)S(1)}, bf16[2,96,1536]{2,1,0:T(8,128)(2,1)S(1)}, u32[]{:S(2)}, u32[]{:S(2)}) collective-permute-start(bf16[2,96,1536]{2,1,0:T(8,128)(2,1)S(1)} %add_convert_fusion.11), channel_id=1, source_target_pairs={{0,1},{1,0},{2,3},{3,2},{4,5},{5,4},{6,7},{7,6},{8,9},{9,8},{10,11... | collective-permute-start | bytes 1769480 | tf_op jit(solution)/shard_map/ppermute | solution.py:524
  397.9 442.2 %reduce-scatter.9.cloned.1.call-start = ((), (), s32[]{:S(2)}) async-start(), calls=%async_computation.12 | async-start | bytes 10027008 | tf_op jit(solution)/shard_map/reduce_scatter | solution.py:780
  407.4 432.8 %reduce-scatter.7.cloned.1.call-start = ((), (), s32[]{:S(2)}) async-start(), calls=%async_computation.11 | async-start | bytes 10027008 | tf_op jit(solution)/shard_map/reduce_scatter | solution.py:780
  418.6 135.5 %collective-permute-start.12 = (bf16[2,96,1536]{2,1,0:T(8,128)(2,1)}, bf16[2,96,1536]{2,1,0:T(8,128)(2,1)}, u32[]{:S(2)}, u32[]{:S(2)}) collective-permute-start(bf16[2,96,1536]{2,1,0:T(8,128)(2,1)} %bitcast.44), channel_id=1, source_target_pairs={{0,1},{1,0},{2,3},{3,2},{4,5},{5,4},{6,7},{7,6},{8,9},{9,8},{10,11... | collective-permute-start | bytes 1769480 | tf_op jit(solution)/shard_map/ppermute | solution.py:524
  458.3 68.2 %collective-permute-start.13 = (bf16[1,512,1536]{2,1,0:T(8,128)(2,1)}, bf16[1,512,1536]{2,1,0:T(8,128)(2,1)}, u32[]{:S(2)}, u32[]{:S(2)}) collective-permute-start(bf16[1,512,1536]{2,1,0:T(8,128)(2,1)} %fusion.118), channel_id=1, source_target_pairs={{0,1},{1,0},{2,3},{3,2},{4,5},{5,4},{6,7},{7,6},{8,9},{9,8},{10,11... | collective-permute-start | bytes 4718600 | tf_op jit(solution)/shard_map/ppermute | solution.py:524
  496.2 70.9 %collective-permute-start.14 = (bf16[1,512,1536]{2,1,0:T(8,128)(2,1)}, bf16[1,512,1536]{2,1,0:T(8,128)(2,1)}, u32[]{:S(2)}, u32[]{:S(2)}) collective-permute-start(bf16[1,512,1536]{2,1,0:T(8,128)(2,1)} %fusion.115), channel_id=1, source_target_pairs={{0,1},{1,0},{2,3},{3,2},{4,5},{5,4},{6,7},{7,6},{8,9},{9,8},{10,11... | collective-permute-start | bytes 4718600 | tf_op jit(solution)/shard_map/ppermute | solution.py:524
  526.4 404.6 %reduce-scatter.11.cloned.1.call-start = ((), (), s32[]{:S(2)}) async-start(), calls=%async_computation.13 | async-start | bytes 10027008 | tf_op jit(solution)/shard_map/reduce_scatter | solution.py:872
  553.5 116.7 %collective-permute-start.18 = (bf16[1,512,768]{2,1,0:T(8,128)(2,1)}, bf16[1,512,768]{2,1,0:T(8,128)(2,1)}, u32[]{:S(2)}, u32[]{:S(2)}) collective-permute-start(bf16[1,512,768]{2,1,0:T(8,128)(2,1)} %get-tuple-element.457), channel_id=1, source_target_pairs={{0,1},{1,0},{2,3},{3,2},{4,5},{5,4},{6,7},{7,6},{8,9},{9,8},{10,11... | collective-permute-start | bytes 2359304 | tf_op jit(solution)/shard_map/ppermute | solution.py:524
  565.8 96.0 %collective-permute-start.19 = (bf16[2,96,768]{2,1,0:T(8,128)(2,1)}, bf16[2,96,768]{2,1,0:T(8,128)(2,1)}, u32[]{:S(2)}, u32[]{:S(2)}) collective-permute-start(bf16[2,96,768]{2,1,0:T(8,128)(2,1)} %slice.376), channel_id=1, source_target_pairs={{0,1},{1,0},{2,3},{3,2},{4,5},{5,4},{6,7},{7,6},{8,9},{9,8},{10,11... | collective-permute-start | bytes 884744 | tf_op jit(solution)/shard_map/ppermute | solution.py:524
  591.2 170.5 %collective-permute-start.21 = (bf16[1,512,768]{2,1,0:T(8,128)(2,1)}, bf16[1,512,768]{2,1,0:T(8,128)(2,1)}, u32[]{:S(2)}, u32[]{:S(2)}) collective-permute-start(bf16[1,512,768]{2,1,0:T(8,128)(2,1)} %get-tuple-element.455), channel_id=1, source_target_pairs={{0,1},{1,0},{2,3},{3,2},{4,5},{5,4},{6,7},{7,6},{8,9},{9,8},{10,11... | collective-permute-start | bytes 2359304 | tf_op jit(solution)/shard_map/ppermute | solution.py:524
  657.4 142.5 %collective-permute-start.22 = (bf16[1,512,1536]{2,1,0:T(8,128)(2,1)}, bf16[1,512,1536]{2,1,0:T(8,128)(2,1)}, u32[]{:S(2)}, u32[]{:S(2)}) collective-permute-start(bf16[1,512,1536]{2,1,0:T(8,128)(2,1)} %fusion.121), channel_id=1, source_target_pairs={{0,1},{1,0},{2,3},{3,2},{4,5},{5,4},{6,7},{7,6},{8,9},{9,8},{10,11... | collective-permute-start | bytes 4718600 | tf_op jit(solution)/shard_map/ppermute | solution.py:524
  661.8 138.1 %collective-permute-start.15 = (bf16[1,512,1536]{2,1,0:T(8,128)(2,1)}, bf16[1,512,1536]{2,1,0:T(8,128)(2,1)}, u32[]{:S(2)}, u32[]{:S(2)}) collective-permute-start(bf16[1,512,1536]{2,1,0:T(8,128)(2,1)} %fusion.124), channel_id=1, source_target_pairs={{0,1},{1,0},{2,3},{3,2},{4,5},{5,4},{6,7},{7,6},{8,9},{9,8},{10,11... | collective-permute-start | bytes 4718600 | tf_op jit(solution)/shard_map/ppermute | solution.py:524
  664.0 135.9 %collective-permute-start.23 = (bf16[2,96,1536]{2,1,0:T(8,128)(2,1)}, bf16[2,96,1536]{2,1,0:T(8,128)(2,1)}, u32[]{:S(2)}, u32[]{:S(2)}) collective-permute-start(bf16[2,96,1536]{2,1,0:T(8,128)(2,1)} %bitcast.79), channel_id=1, source_target_pairs={{0,1},{1,0},{2,3},{3,2},{4,5},{5,4},{6,7},{7,6},{8,9},{9,8},{10,11... | collective-permute-start | bytes 1769480 | tf_op jit(solution)/shard_map/ppermute | solution.py:524
  670.2 77.7 %collective-permute-start.17 = (bf16[4,1,96,3072]{3,2,0,1:T(8,128)(2,1)}, bf16[4,1,96,3072]{3,2,0,1:T(8,128)(2,1)}, u32[]{:S(2)}, u32[]{:S(2)}) collective-permute-start(bf16[4,1,96,3072]{3,2,0,1:T(8,128)(2,1)} %fusion.136), channel_id=1, source_target_pairs={{0,4},{2,6},{4,0},{6,2},{8,12},{10,14},{12,8},{14,10},{16,20},{18,... | collective-permute-start | bytes 7077896 | tf_op jit(solution)/shard_map/ppermute | solution.py:542
  761.7 78.4 %collective-permute-start.25 = (bf16[1,512,1536]{2,1,0:T(8,128)(2,1)}, bf16[1,512,1536]{2,1,0:T(8,128)(2,1)}, u32[]{:S(2)}, u32[]{:S(2)}) collective-permute-start(bf16[1,512,1536]{2,1,0:T(8,128)(2,1)} %fusion.130), channel_id=1, source_target_pairs={{0,1},{1,0},{2,3},{3,2},{4,5},{5,4},{6,7},{7,6},{8,9},{9,8},{10,11... | collective-permute-start | bytes 4718600 | tf_op jit(solution)/shard_map/ppermute | solution.py:524
  870.4 182.4 %collective-permute-start.40 = (f32[48,3072]{1,0:T(8,128)}, f32[48,3072]{1,0:T(8,128)}, u32[]{:S(2)}, u32[]{:S(2)}) collective-permute-start(f32[48,3072]{1,0:T(8,128)} %get-tuple-element.462), channel_id=1, source_target_pairs={{0,1},{1,0},{2,3},{3,2},{4,5},{5,4},{6,7},{7,6},{8,9},{9,8},{10,11... | collective-permute-start | bytes 1769480 | tf_op jit(solution)/shard_map/ppermute | solution.py:524
  882.5 54.3 %collective-permute-start.33 = (bf16[1,512,1536]{2,1,0:T(8,128)(2,1)}, bf16[1,512,1536]{2,1,0:T(8,128)(2,1)}, u32[]{:S(2)}, u32[]{:S(2)}) collective-permute-start(bf16[1,512,1536]{2,1,0:T(8,128)(2,1)} %fusion.127), channel_id=1, source_target_pairs={{0,1},{1,0},{2,3},{3,2},{4,5},{5,4},{6,7},{7,6},{8,9},{9,8},{10,11... | collective-permute-start | bytes 4718600 | tf_op jit(solution)/shard_map/ppermute | solution.py:524
  930.3 55.4 %collective-permute-start.29 = (bf16[4,1,96,2304]{3,2,0,1:T(8,128)(2,1)}, bf16[4,1,96,2304]{3,2,0,1:T(8,128)(2,1)}, u32[]{:S(2)}, u32[]{:S(2)}) collective-permute-start(bf16[4,1,96,2304]{3,2,0,1:T(8,128)(2,1)} %fusion.149), channel_id=1, source_target_pairs={{0,4},{2,6},{4,0},{6,2},{8,12},{10,14},{12,8},{14,10},{16,20},{18,... | collective-permute-start | bytes 5308424 | tf_op jit(solution)/shard_map/ppermute | solution.py:542
  946.5 106.3 %collective-permute-start.39 = (f32[48,2,1536]{2,0,1:T(8,128)}, f32[48,2,1536]{2,0,1:T(8,128)}, u32[]{:S(2)}, u32[]{:S(2)}) collective-permute-start(f32[48,2,1536]{2,0,1:T(8,128)} %dynamic-slice_bitcast_fusion.1), channel_id=1, source_target_pairs={{0,1},{1,0},{2,3},{3,2},{4,5},{5,4},{6,7},{7,6},{8,9},{9,8},{10,11... | collective-permute-start | bytes 1769480 | tf_op jit(solution)/shard_map/ppermute | solution.py:524
  1017.2 50.5 %all-to-all-start.2 = ((bf16[16,292,128]{2,1,0:T(8,128)(2,1)}), bf16[16,292,128]{2,1,0:T(8,128)(2,1)}, u32[]{:S(2)}, u32[]{:S(2)}) async-start(bf16[16,292,128]{2,1,0:T(8,128)(2,1)} %broadcast_in_dim.8), calls=%async_computation.6 | async-start | bytes 2424832 | tf_op jit(solution)/shard_map/all_to_all | solution.py:1038
  (181 other events, 2084.7 us)
Sparse Core Ops, SparseCore 0:
  10.4 142.8 all-gather.4
  154.9 104.3 all-gather.6
  260.8 98.9 all-gather.8
  398.1 116.6 reduce-scatter.4
  519.2 111.1 reduce-scatter.8
  634.4 144.1 reduce-scatter.6
  783.2 123.6 reduce-scatter.10

commit v4 on v3

--- a/solution.py
+++ b/solution.py
@@ -9,7 +9,7 @@
 
 HEAD = 64
 LANES = 128
-BLOCK = 512
+BLOCK = 1024
 BF16 = jnp.bfloat16
 F32 = jnp.float32
 SCALE = HEAD**-0.5

time: 1110 us -> 1100 us (level)
  Pallas kernels: 399 us -> 374 us
    pallas_call x4, Pallas kernels: 134 us -> 118 us  [attend_back(): pl.pallas_call(kernel, grid=(count,), in_specs=in_specs, out_specs=[pl.Bl...]
  transfers between devices with their start and end apart: 53 -> 53, of which waited for: 11 -> 12; matrix products, arithmetic and copies ran while one was open for 38% -> 39% of each run, Pallas kernels for 34% -> 32%
where the time goes in v4:
time: 1100 us; the launch traced here: 1090 us
  Pallas kernels  374 us (34%)
  matrix products  212 us (19%)
  waiting for transfers between devices  180 us (16%)
  other arithmetic  149 us (14%)
  local copies, waits for them, and re-layouts  86 us (8%)
  starting transfers between devices  69.7 us (6%)
  between operations  17 us (2%)
    pallas_call x4, Pallas kernels, attend_back(): pl.pallas_call(kernel, grid=(count,), in_specs=in_specs, out_specs=[pl.Bl...  118 us
    pallas_call x8, Pallas kernels, weight_sum(): pl.pallas_call(kernel, grid=(rows // row_tile, columns // tile), in_specs...  116 us
    dot_general x13, matrix products, times_t(): lax.dot_general(left, right, (((2,), (1,)), ((), ())), preferred_element_...  107 us
    dot_general x11, matrix products, times(): lax.dot_general(left, right, (((2,), (0,)), ((), ())), preferred_element_...  96.7 us
    ppermute x30, waiting for transfers between devices, shift_seq(): lax.ppermute(values, 'seq', [(i, (i + amount) % members) for i in range(m...  91.7 us
    pallas_call x3, Pallas kernels, feed_forward(): pl.pallas_call(kernel, grid=(units // tile,), in_specs=[pl.BlockSpec((1,...  67.5 us
    pallas_call x2, Pallas kernels, attend(): pl.pallas_call(kernel, grid=(pairs,), in_specs=[pl.BlockSpec((1, array.sh...  60.9 us
    ppermute x12, waiting for transfers between devices, send(): lax.ppermute(self.away, 'fsdp', [(i, i ^ self.bit) for i in range(size)])  48 us
  transfers between devices with their start and end apart: 53, of which 12 were waited for; matrix products, arithmetic and copies ran while one was open for 39% of the time, Pallas kernels for 32%

profile of v4, /device:TPU:0, one launch (start us, length us, event | category | flops | bytes accessed | tf_op | source)
XLA Modules:
  0.0 1088.7 jit_solution(10002027447226759147)
XLA Ops:
  51.7 31.8 %all-to-all-done.1 = f32[16,2,2,4608]{3,2,1,0:T(2,128)} async-done(((f32[16,2,2,4608]{3,2,1,0:T(2,128)}), f32[16,2,2,4608]{3,2,1,0:T(2,128)}, u32[]{:S(2)}, u32[]{:S(2)}) %all-to-all-start.1) | async-done | bytes 1179680 | tf_op jit(solution)/shard_map/all_to_all | solution.py:658
  92.0 34.2 %collective-permute-done = f32[2,2,4608]{2,1,0:T(2,128)} collective-permute-done((f32[2,2,4608]{2,1,0:T(2,128)}, f32[2,2,4608]{2,1,0:T(2,128)}, u32[]{:S(2)}, u32[]{:S(2)}) %collective-permute-start) | collective-permute-done | bytes 73760 | tf_op jit(solution)/shard_map/ppermute | solution.py:524
  163.2 12.9 %fusion.6.refs_3_.refs_4_.refs_5_.refs_7_.refs_8_.refs_9_ = f32[2,512,2304]{2,1,0:T(8,128)} fusion(bf16[2,512,1536]{2,1,0:T(8,128)(2,1)S(1)} %copy-done.43, bf16[2,1536,3840]{2,1,0:T(8,128)(2,1)} %all-gather.5.cloned.1.call-done), kind=kOutput, calls=%fused_computation.16 | convolution fusion | flops 7247757312 | bytes 19660800 | tf_op jit(solution)/shard_map/dot_general | solution.py:596
  176.1 12.8 %fusion.8.refs_0_.refs_1_.refs_2_.refs_4_.refs_5_.refs_6_ = f32[2,512,2304]{2,1,0:T(8,128)} fusion(bf16[2,512,1536]{2,1,0:T(8,128)(2,1)S(1)} %copy-done.44, bf16[2,1536,3840]{2,1,0:T(8,128)(2,1)} %all-gather.5.cloned.1.call-done), kind=kOutput, calls=%fused_computation.18 | convolution fusion | flops 7247757312 | bytes 19660800 | tf_op jit(solution)/shard_map/dot_general | solution.py:596
  189.7 30.5 %attend.2 = (bf16[1,512,768]{2,1,0:T(8,128)(2,1)}, bf16[1,512,768]{2,1,0:T(8,128)(2,1)}, bf16[1,96,768]{2,1,0:T(8,128)(2,1)}, bf16[1,96,768]{2,1,0:T(8,128)(2,1)}, f32[1,6,16,1216]{3,2,1,0:T(8,128)}) custom-call(f32[2,512,2304]{2,1,0:T(8,128)} %fusion.8.refs_0_.refs_1_.refs_2_.refs_4_.refs_5_.refs_6_, ...), custom_call_target="tpu_custom_call" | custom-call | flops 9084862464 | bytes 13074432 | tf_op jit(solution)/shard_map/attend/pallas_call | solution.py:230
  222.3 30.4 %attend.3 = (bf16[1,512,768]{2,1,0:T(8,128)(2,1)}, bf16[1,512,768]{2,1,0:T(8,128)(2,1)}, bf16[1,96,768]{2,1,0:T(8,128)(2,1)}, bf16[1,96,768]{2,1,0:T(8,128)(2,1)}, f32[1,6,16,1216]{3,2,1,0:T(8,128)}) custom-call(f32[2,512,2304]{2,1,0:T(8,128)} %fusion.8.refs_0_.refs_1_.refs_2_.refs_4_.refs_5_.refs_6_, ...), custom_call_target="tpu_custom_call" | custom-call | flops 9084862464 | bytes 13074432 | tf_op jit(solution)/shard_map/attend/pallas_call | solution.py:230
  298.3 55.7 %collective-permute-done.10 = bf16[2,96,1536]{2,1,0:T(8,128)(2,1)S(1)} collective-permute-done((bf16[2,96,1536]{2,1,0:T(8,128)(2,1)S(1)}, bf16[2,96,1536]{2,1,0:T(8,128)(2,1)S(1)}, u32[]{:S(2)}, u32[]{:S(2)}) %collective-permute-start.10) | collective-permute-done | bytes 589856 | tf_op jit(solution)/shard_map/ppermute | solution.py:524
  359.8 13.1 %feed_forward.3 = (bf16[1,384,3072]{2,1,0:T(8,128)(2,1)}, bf16[1,384,3072]{2,1,0:T(8,128)(2,1)}) custom-call(bf16[1,384,1536]{2,1,0:T(8,128)(2,1)} %bitcast.549, bf16[1,384,1536]{2,1,0:T(8,128)(2,1)} %fusion.147.refs_1_, bf16[2,1536,3072]{2,1,0:T(8,128)(2,1)} %all-gather.7.cloned.1.call-done.refs_2_.refs_4_, bf16[2,3072,1536]{2,1,0:T(8,128)(2,1)} %bitcast.516), custom_call_target="tpu_custom_call" | custom-call | flops 7247757312 | bytes 25952256 | tf_op jit(solution)/shard_map/feed_forward/pallas_call | solution.py:347
  382.6 8.7 weight_sum.9
  391.4 9.4 weight_sum.8
  413.5 27.5 %feed_forward.4 = (bf16[1,512,3072]{2,1,0:T(8,128)(2,1)}, bf16[1,512,3072]{2,1,0:T(8,128)(2,1)}, bf16[1,512,3072]{2,1,0:T(8,128)(2,1)}, bf16[1,512,3072]{2,1,0:T(8,128)(2,1)}) custom-call(bf16[1,512,1536]{2,1,0:T(8,128)(2,1)} %copy-done.57, bf16[1,512,1536]{2,1,0:T(8,128)(2,1)} %copy-done.145, ...), custom_call_target="tpu_custom_call" | custom-call | flops 19327352832 | bytes 37748736 | tf_op jit(solution)/shard_map/feed_forward/pallas_call | solution.py:347
  441.0 10.4 fusion.118
  452.2 26.9 %feed_forward.5 = (bf16[1,512,3072]{2,1,0:T(8,128)(2,1)}, bf16[1,512,3072]{2,1,0:T(8,128)(2,1)}, bf16[1,512,3072]{2,1,0:T(8,128)(2,1)}, bf16[1,512,3072]{2,1,0:T(8,128)(2,1)}) custom-call(bf16[1,512,1536]{2,1,0:T(8,128)(2,1)} %copy-done.59, bf16[1,512,1536]{2,1,0:T(8,128)(2,1)} %copy-done.146, ...), custom_call_target="tpu_custom_call" | custom-call | flops 19327352832 | bytes 37748736 | tf_op jit(solution)/shard_map/feed_forward/pallas_call | solution.py:347
  479.1 10.4 fusion.115
  490.7 28.9 %weight_sum.10 = bf16[16,1,192,1536]{3,2,1,0:T(8,128)(2,1)} custom-call(bf16[1,512,3072]{2,1,0:T(8,128)(2,1)} %get-tuple-element.232.refs_0_, bf16[1,512,3072]{2,1,0:T(8,128)(2,1)} %get-tuple-element.233.refs_1_, bf16[1,512,3072]{2,1,0:T(8,128)(2,1)} %get-tuple-element.284.refs_2_, bf16[1,512,3072]{2,1,0:T(8,128)(2,1)} %get-tuple-element.235.refs_3_, ...), custom_call_target="tpu_custom_call" | custom-call | flops 19327352832 | bytes 28311552 | tf_op jit(solution)/shard_map/weight_sum/pallas_call | solution.py:415
  519.7 12.8 %multiply_reduce_fusion.1 = (f32[1536]{0:T(1024)}, f32[512]{0:T(512)S(1)}, f32[512]{0:T(512)S(1)}, f32[1536]{0:T(1024)}, f32[1,512,1536]{2,1,0:T(8,128)S(1)}) fusion(f32[1,512,1536]{2,1,0:T(8,128)} %copy-done.12, f32[512]{0:T(512)} %copy-done.114, f32[512]{0:T(512)S(1)} %broadcast_multiply_fusion.13, bf16[1,512,1536]{2,1,0:T(8,128)(2,1)} %collective-permute-done.13, ...), kind=kOutput, calls=%fused_computation.119 | convolution fusion | flops 4840484864 | bytes 20475904 | tf_op jit(solution)/shard_map/dot_general | solution.py:600
  560.3 9.9 multiply_reduce_fusion
  584.9 9.2 weight_sum.11.refs_0_
  598.5 27.1 %weight_sum.13 = (bf16[8,1,96,3072]{3,2,1,0:T(8,128)(2,1)}, bf16[8,1,96,3072]{3,2,1,0:T(8,128)(2,1)}) custom-call(s32[1]{0:T(128)} %bitcast.42.refs_0_, bf16[1,512,1536]{2,1,0:T(8,128)(2,1)} %copy-done.57, bf16[1,512,1536]{2,1,0:T(8,128)(2,1)} %copy-done.145, bf16[1,512,1536]{2,1,0:T(8,128)(2,1)} %copy-done.59, bf16[1,512,1536]{2,1,0:T(8,128)(2,1)} %copy-done.146, ...), custom_call_target="tpu_custom_call" | custom-call | flops 19327352832 | bytes 28311552 | tf_op jit(solution)/shard_map/weight_sum/pallas_call | solution.py:415
  625.7 9.9 fusion.124
  635.7 9.0 fusion.121
  664.7 29.3 %attend_back.4 = (bf16[1,512,2304]{2,1,0:T(8,128)(2,1)}, bf16[1,512,2304]{2,1,0:T(8,128)(2,1)}, bf16[1,96,2304]{2,1,0:T(8,128)(2,1)}, bf16[1,96,2304]{2,1,0:T(8,128)(2,1)}, f32[3,8,128]{2,1,0:T(8,128)}) custom-call(f32[2,512,2304]{2,1,0:T(8,128)} %fusion.8.refs_0_.refs_1_.refs_2_.refs_4_.refs_5_.refs_6_, ...), custom_call_target="tpu_custom_call" | custom-call | flops 11356078080 | bytes 10272768 | tf_op jit(solution)/shard_map/attend_back/pallas_call | solution.py:296
  695.9 30.0 %attend_back.5 = (bf16[1,512,2304]{2,1,0:T(8,128)(2,1)}, bf16[1,512,2304]{2,1,0:T(8,128)(2,1)}, bf16[1,96,2304]{2,1,0:T(8,128)(2,1)}, bf16[1,96,2304]{2,1,0:T(8,128)(2,1)}, f32[3,8,128]{2,1,0:T(8,128)}) custom-call(bf16[1,512,2304]{2,1,0:T(8,128)(2,1)} %get-tuple-element.239.refs_0_, ...), custom_call_target="tpu_custom_call", output_to_operand_aliasing={{0}: (0, {}), {1}: (1, {}), {2}: (2, {}), {3}: (3, {})} | custom-call | flops 11356078080 | bytes 10272768 | tf_op jit(solution)/shard_map/attend_back/pallas_call | solution.py:296
  725.9 15.8 %collective-permute-done.17 = bf16[4,1,96,3072]{3,2,0,1:T(8,128)(2,1)} collective-permute-done((bf16[4,1,96,3072]{3,2,0,1:T(8,128)(2,1)}, bf16[4,1,96,3072]{3,2,0,1:T(8,128)(2,1)}, u32[]{:S(2)}, u32[]{:S(2)}) %collective-permute-start.17) | collective-permute-done | bytes 2359328 | tf_op jit(solution)/shard_map/ppermute | solution.py:542
  755.4 29.3 %attend_back.6 = (bf16[1,512,2304]{2,1,0:T(8,128)(2,1)}, bf16[1,512,2304]{2,1,0:T(8,128)(2,1)}, bf16[1,96,2304]{2,1,0:T(8,128)(2,1)}, bf16[1,96,2304]{2,1,0:T(8,128)(2,1)}, f32[3,8,128]{2,1,0:T(8,128)}) custom-call(f32[2,512,2304]{2,1,0:T(8,128)} %fusion.8.refs_0_.refs_1_.refs_2_.refs_4_.refs_5_.refs_6_, ...), custom_call_target="tpu_custom_call" | custom-call | flops 11356078080 | bytes 10272768 | tf_op jit(solution)/shard_map/attend_back/pallas_call | solution.py:296
  792.9 29.8 %attend_back.7 = (bf16[1,512,2304]{2,1,0:T(8,128)(2,1)}, bf16[1,512,2304]{2,1,0:T(8,128)(2,1)}, bf16[1,96,2304]{2,1,0:T(8,128)(2,1)}, bf16[1,96,2304]{2,1,0:T(8,128)(2,1)}, f32[3,8,128]{2,1,0:T(8,128)}) custom-call(bf16[1,512,2304]{2,1,0:T(8,128)(2,1)} %get-tuple-element.254.refs_0_, ...), custom_call_target="tpu_custom_call", output_to_operand_aliasing={{0}: (0, {}), {1}: (1, {}), {2}: (2, {}), {3}: (3, {})} | custom-call | flops 11356078080 | bytes 10272768 | tf_op jit(solution)/shard_map/attend_back/pallas_call | solution.py:296
  826.1 21.1 %weight_sum.14 = (bf16[8,1,96,2304]{3,2,1,0:T(8,128)(2,1)}, bf16[8,1,96,2304]{3,2,1,0:T(8,128)(2,1)}) custom-call(s32[1]{0:T(128)} %bitcast.42.refs_0_, bf16[2,512,1536]{2,1,0:T(8,128)(2,1)} %get-tuple-element.493.refs_1_.refs_3_, bf16[2,512,1536]{2,1,0:T(8,128)(2,1)} %get-tuple-element.492.refs_2_.refs_4_, ...), custom_call_target="tpu_custom_call" | custom-call | flops 14495514624 | bytes 22806528 | tf_op jit(solution)/shard_map/weight_sum/pallas_call | solution.py:415
  893.6 11.1 %multiply_reduce_fusion.3 = (f32[1536]{0:T(1024)}, bf16[1,512,1536]{2,1,0:T(8,128)(2,1)}) fusion(bf16[2,512,1536]{2,1,0:T(8,128)(2,1)S(1)} %copy-done.21, f32[1,512,1536]{2,1,0:T(8,128)S(1)} %copy-done.14, f32[1536]{0:T(1024)S(1)} %copy-done.131, bf16[1,512,1536]{2,1,0:T(8,128)(2,1)} %collective-permute-done.15, ...), kind=kOutput, calls=%fused_computation.123 | convolution fusion | flops 4838128128 | bytes 20459520 | tf_op jit(solution)/shard_map/dot_general | solution.py:596
  925.9 8.7 fusion.67
  955.4 10.3 fusion.73
  979.2 9.2 multiply_reduce_fusion.2
  1013.6 23.3 %collective-permute-done.38 = bf16[1,1,96,2304]{3,2,1,0:T(8,128)(2,1)} collective-permute-done((bf16[1,1,96,2304]{3,2,1,0:T(8,128)(2,1)}, bf16[1,1,96,2304]{3,2,1,0:T(8,128)(2,1)}, u32[]{:S(2)}, u32[]{:S(2)}) %collective-permute-start.38) | collective-permute-done | bytes 442400 | tf_op jit(solution)/shard_map/ppermute | solution.py:542
  (689 shorter events, 432.3 us)
Async XLA Ops:
  7.2 147.5 %all-gather.5.cloned.1.call-start = ((), (), s32[]{:S(2)}) async-start(), calls=%async_computation.8 | async-start | bytes 25067520 | tf_op jit(solution)/shard_map/all_gather | solution.py:642
  18.4 339.1 %all-gather.7.cloned.1.call-start = ((), (), s32[]{:S(2)}) async-start(), calls=%async_computation.9 | async-start | bytes 20054016 | tf_op jit(solution)/shard_map/all_gather | solution.py:667
  29.3 330.5 %all-gather.9.cloned.1.call-start = ((), (), s32[]{:S(2)}) async-start(), calls=%async_computation.14 | async-start | bytes 20054016 | tf_op jit(solution)/shard_map/all_gather | solution.py:668
  35.0 48.5 %all-to-all-start.1 = ((f32[16,2,2,4608]{3,2,1,0:T(2,128)}), f32[16,2,2,4608]{3,2,1,0:T(2,128)}, u32[]{:S(2)}, u32[]{:S(2)}) async-start(f32[16,2,2,4608]{3,2,1,0:T(2,128)} %copy.184), calls=%async_computation.1 | async-start | bytes 2359296 | tf_op jit(solution)/shard_map/all_to_all | solution.py:658
  39.4 750.6 %reduce-scatter.5.cloned.1.call-start = ((), (), s32[]{:S(2)}) async-start(), calls=%async_computation.10 | async-start | bytes 10027008 | tf_op jit(solution)/shard_map/reduce_scatter | solution.py:780
  41.4 96.2 %collective-permute-start.2 = (bf16[2,96,1536]{2,1,0:T(8,128)(2,1)}, bf16[2,96,1536]{2,1,0:T(8,128)(2,1)}, u32[]{:S(2)}, u32[]{:S(2)}) collective-permute-start(bf16[2,96,1536]{2,1,0:T(8,128)(2,1)} %pad.7), channel_id=1, source_target_pairs={{0,1},{1,0},{2,3},{3,2},{4,5},{5,4},{6,7},{7,6},{8,9},{9,8},{10,11... | collective-permute-start | bytes 1769480 | tf_op jit(solution)/shard_map/ppermute | solution.py:524
  42.9 94.7 %collective-permute-start.1 = (bf16[2,512,1536]{2,1,0:T(8,128)(2,1)}, bf16[2,512,1536]{2,1,0:T(8,128)(2,1)}, u32[]{:S(2)}, u32[]{:S(2)}) collective-permute-start(bf16[2,512,1536]{2,1,0:T(8,128)(2,1)} %param.16), channel_id=1, source_target_pairs={{0,1},{1,0},{2,3},{3,2},{4,5},{5,4},{6,7},{7,6},{8,9},{9,8},{10,11... | collective-permute-start | bytes 9437192 | tf_op jit(solution)/shard_map/ppermute | solution.py:524
  137.6 115.2 %collective-permute-start.5 = (bf16[2,96,1536]{2,1,0:T(8,128)(2,1)}, bf16[2,96,1536]{2,1,0:T(8,128)(2,1)}, u32[]{:S(2)}, u32[]{:S(2)}) collective-permute-start(bf16[2,96,1536]{2,1,0:T(8,128)(2,1)} %pad.8), channel_id=1, source_target_pairs={{0,1},{1,0},{2,3},{3,2},{4,5},{5,4},{6,7},{7,6},{8,9},{9,8},{10,11... | collective-permute-start | bytes 1769480 | tf_op jit(solution)/shard_map/ppermute | solution.py:524
  139.1 113.7 %collective-permute-start.4 = (bf16[2,512,1536]{2,1,0:T(8,128)(2,1)}, bf16[2,512,1536]{2,1,0:T(8,128)(2,1)}, u32[]{:S(2)}, u32[]{:S(2)}) collective-permute-start(bf16[2,512,1536]{2,1,0:T(8,128)(2,1)} %param.26), channel_id=1, source_target_pairs={{0,1},{1,0},{2,3},{3,2},{4,5},{5,4},{6,7},{7,6},{8,9},{9,8},{10,11... | collective-permute-start | bytes 9437192 | tf_op jit(solution)/shard_map/ppermute | solution.py:524
  220.2 67.6 %collective-permute-start.7 = (bf16[1,96,768]{2,1,0:T(8,128)(2,1)}, bf16[1,96,768]{2,1,0:T(8,128)(2,1)S(1)}, u32[]{:S(2)}, u32[]{:S(2)}) collective-permute-start(bf16[1,96,768]{2,1,0:T(8,128)(2,1)} %get-tuple-element.185.refs_19_.refs_23_), channel_id=1, source_target_pairs={{0,1},{1,0},{2,3},{3,2},{4,5},{5,4},{6,7},{7,6},{8,9},{9,8},{10,11... | collective-permute-start | bytes 442376 | tf_op jit(solution)/shard_map/ppermute | solution.py:524
  272.6 81.4 %collective-permute-start.6 = (bf16[1,512,1536]{2,1,0:T(8,128)(2,1)S(1)}, bf16[1,512,1536]{2,1,0:T(8,128)(2,1)S(1)}, u32[]{:S(2)}, u32[]{:S(2)}) collective-permute-start(bf16[1,512,1536]{2,1,0:T(8,128)(2,1)S(1)} %add_convert_fusion.6.refs_0_.refs_1_), channel_id=1, source_target_pairs={{0,1},{1,0},{2,3},{3,2},{4,5},{5,4},{6,7},{7,6},{8,9},{9,8},{10,11... | collective-permute-start | bytes 4718600 | tf_op jit(solution)/shard_map/ppermute | solution.py:524
  286.4 67.6 %collective-permute-start.11 = (bf16[1,512,1536]{2,1,0:T(8,128)(2,1)S(1)}, bf16[1,512,1536]{2,1,0:T(8,128)(2,1)S(1)}, u32[]{:S(2)}, u32[]{:S(2)}) collective-permute-start(bf16[1,512,1536]{2,1,0:T(8,128)(2,1)S(1)} %add_convert_fusion.5.refs_0_.refs_3_), channel_id=1, source_target_pairs={{0,1},{1,0},{2,3},{3,2},{4,5},{5,4},{6,7},{7,6},{8,9},{9,8},{10,11... | collective-permute-start | bytes 4718600 | tf_op jit(solution)/shard_map/ppermute | solution.py:524
  294.7 59.3 %collective-permute-start.10 = (bf16[2,96,1536]{2,1,0:T(8,128)(2,1)S(1)}, bf16[2,96,1536]{2,1,0:T(8,128)(2,1)S(1)}, u32[]{:S(2)}, u32[]{:S(2)}) collective-permute-start(bf16[2,96,1536]{2,1,0:T(8,128)(2,1)S(1)} %add_convert_fusion.11), channel_id=1, source_target_pairs={{0,1},{1,0},{2,3},{3,2},{4,5},{5,4},{6,7},{7,6},{8,9},{9,8},{10,11... | collective-permute-start | bytes 1769480 | tf_op jit(solution)/shard_map/ppermute | solution.py:524
  391.4 434.6 %reduce-scatter.9.cloned.1.call-start = ((), (), s32[]{:S(2)}) async-start(), calls=%async_computation.12 | async-start | bytes 10027008 | tf_op jit(solution)/shard_map/reduce_scatter | solution.py:780
  400.9 425.2 %reduce-scatter.7.cloned.1.call-start = ((), (), s32[]{:S(2)}) async-start(), calls=%async_computation.11 | async-start | bytes 10027008 | tf_op jit(solution)/shard_map/reduce_scatter | solution.py:780
  412.1 135.3 %collective-permute-start.12 = (bf16[2,96,1536]{2,1,0:T(8,128)(2,1)}, bf16[2,96,1536]{2,1,0:T(8,128)(2,1)}, u32[]{:S(2)}, u32[]{:S(2)}) collective-permute-start(bf16[2,96,1536]{2,1,0:T(8,128)(2,1)} %bitcast.44), channel_id=1, source_target_pairs={{0,1},{1,0},{2,3},{3,2},{4,5},{5,4},{6,7},{7,6},{8,9},{9,8},{10,11... | collective-permute-start | bytes 1769480 | tf_op jit(solution)/shard_map/ppermute | solution.py:524
  451.4 68.3 %collective-permute-start.13 = (bf16[1,512,1536]{2,1,0:T(8,128)(2,1)}, bf16[1,512,1536]{2,1,0:T(8,128)(2,1)}, u32[]{:S(2)}, u32[]{:S(2)}) collective-permute-start(bf16[1,512,1536]{2,1,0:T(8,128)(2,1)} %fusion.118), channel_id=1, source_target_pairs={{0,1},{1,0},{2,3},{3,2},{4,5},{5,4},{6,7},{7,6},{8,9},{9,8},{10,11... | collective-permute-start | bytes 4718600 | tf_op jit(solution)/shard_map/ppermute | solution.py:524
  489.5 70.8 %collective-permute-start.14 = (bf16[1,512,1536]{2,1,0:T(8,128)(2,1)}, bf16[1,512,1536]{2,1,0:T(8,128)(2,1)}, u32[]{:S(2)}, u32[]{:S(2)}) collective-permute-start(bf16[1,512,1536]{2,1,0:T(8,128)(2,1)} %fusion.115), channel_id=1, source_target_pairs={{0,1},{1,0},{2,3},{3,2},{4,5},{5,4},{6,7},{7,6},{8,9},{9,8},{10,11... | collective-permute-start | bytes 4718600 | tf_op jit(solution)/shard_map/ppermute | solution.py:524
  519.6 397.8 %reduce-scatter.11.cloned.1.call-start = ((), (), s32[]{:S(2)}) async-start(), calls=%async_computation.13 | async-start | bytes 10027008 | tf_op jit(solution)/shard_map/reduce_scatter | solution.py:872
  546.6 116.6 %collective-permute-start.18 = (bf16[1,512,768]{2,1,0:T(8,128)(2,1)}, bf16[1,512,768]{2,1,0:T(8,128)(2,1)}, u32[]{:S(2)}, u32[]{:S(2)}) collective-permute-start(bf16[1,512,768]{2,1,0:T(8,128)(2,1)} %get-tuple-element.457), channel_id=1, source_target_pairs={{0,1},{1,0},{2,3},{3,2},{4,5},{5,4},{6,7},{7,6},{8,9},{9,8},{10,11... | collective-permute-start | bytes 2359304 | tf_op jit(solution)/shard_map/ppermute | solution.py:524
  559.0 95.7 %collective-permute-start.19 = (bf16[2,96,768]{2,1,0:T(8,128)(2,1)}, bf16[2,96,768]{2,1,0:T(8,128)(2,1)}, u32[]{:S(2)}, u32[]{:S(2)}) collective-permute-start(bf16[2,96,768]{2,1,0:T(8,128)(2,1)} %slice.376), channel_id=1, source_target_pairs={{0,1},{1,0},{2,3},{3,2},{4,5},{5,4},{6,7},{7,6},{8,9},{9,8},{10,11... | collective-permute-start | bytes 884744 | tf_op jit(solution)/shard_map/ppermute | solution.py:524
  584.1 169.8 %collective-permute-start.21 = (bf16[1,512,768]{2,1,0:T(8,128)(2,1)}, bf16[1,512,768]{2,1,0:T(8,128)(2,1)}, u32[]{:S(2)}, u32[]{:S(2)}) collective-permute-start(bf16[1,512,768]{2,1,0:T(8,128)(2,1)} %get-tuple-element.455), channel_id=1, source_target_pairs={{0,1},{1,0},{2,3},{3,2},{4,5},{5,4},{6,7},{7,6},{8,9},{9,8},{10,11... | collective-permute-start | bytes 2359304 | tf_op jit(solution)/shard_map/ppermute | solution.py:524
  650.6 139.3 %collective-permute-start.22 = (bf16[1,512,1536]{2,1,0:T(8,128)(2,1)}, bf16[1,512,1536]{2,1,0:T(8,128)(2,1)}, u32[]{:S(2)}, u32[]{:S(2)}) collective-permute-start(bf16[1,512,1536]{2,1,0:T(8,128)(2,1)} %fusion.121), channel_id=1, source_target_pairs={{0,1},{1,0},{2,3},{3,2},{4,5},{5,4},{6,7},{7,6},{8,9},{9,8},{10,11... | collective-permute-start | bytes 4718600 | tf_op jit(solution)/shard_map/ppermute | solution.py:524
  654.8 135.1 %collective-permute-start.15 = (bf16[1,512,1536]{2,1,0:T(8,128)(2,1)}, bf16[1,512,1536]{2,1,0:T(8,128)(2,1)}, u32[]{:S(2)}, u32[]{:S(2)}) collective-permute-start(bf16[1,512,1536]{2,1,0:T(8,128)(2,1)} %fusion.124), channel_id=1, source_target_pairs={{0,1},{1,0},{2,3},{3,2},{4,5},{5,4},{6,7},{7,6},{8,9},{9,8},{10,11... | collective-permute-start | bytes 4718600 | tf_op jit(solution)/shard_map/ppermute | solution.py:524
  657.2 132.7 %collective-permute-start.23 = (bf16[2,96,1536]{2,1,0:T(8,128)(2,1)}, bf16[2,96,1536]{2,1,0:T(8,128)(2,1)}, u32[]{:S(2)}, u32[]{:S(2)}) collective-permute-start(bf16[2,96,1536]{2,1,0:T(8,128)(2,1)} %bitcast.79), channel_id=1, source_target_pairs={{0,1},{1,0},{2,3},{3,2},{4,5},{5,4},{6,7},{7,6},{8,9},{9,8},{10,11... | collective-permute-start | bytes 1769480 | tf_op jit(solution)/shard_map/ppermute | solution.py:524
  663.2 78.5 %collective-permute-start.17 = (bf16[4,1,96,3072]{3,2,0,1:T(8,128)(2,1)}, bf16[4,1,96,3072]{3,2,0,1:T(8,128)(2,1)}, u32[]{:S(2)}, u32[]{:S(2)}) collective-permute-start(bf16[4,1,96,3072]{3,2,0,1:T(8,128)(2,1)} %fusion.136), channel_id=1, source_target_pairs={{0,4},{2,6},{4,0},{6,2},{8,12},{10,14},{12,8},{14,10},{16,20},{18,... | collective-permute-start | bytes 7077896 | tf_op jit(solution)/shard_map/ppermute | solution.py:542
  754.0 72.1 %collective-permute-start.25 = (bf16[1,512,1536]{2,1,0:T(8,128)(2,1)}, bf16[1,512,1536]{2,1,0:T(8,128)(2,1)}, u32[]{:S(2)}, u32[]{:S(2)}) collective-permute-start(bf16[1,512,1536]{2,1,0:T(8,128)(2,1)} %fusion.130), channel_id=1, source_target_pairs={{0,1},{1,0},{2,3},{3,2},{4,5},{5,4},{6,7},{7,6},{8,9},{9,8},{10,11... | collective-permute-start | bytes 4718600 | tf_op jit(solution)/shard_map/ppermute | solution.py:524
  856.3 185.0 %collective-permute-start.40 = (f32[48,3072]{1,0:T(8,128)}, f32[48,3072]{1,0:T(8,128)}, u32[]{:S(2)}, u32[]{:S(2)}) collective-permute-start(f32[48,3072]{1,0:T(8,128)} %get-tuple-element.462), channel_id=1, source_target_pairs={{0,1},{1,0},{2,3},{3,2},{4,5},{5,4},{6,7},{7,6},{8,9},{9,8},{10,11... | collective-permute-start | bytes 1769480 | tf_op jit(solution)/shard_map/ppermute | solution.py:524
  868.8 57.1 %collective-permute-start.33 = (bf16[1,512,1536]{2,1,0:T(8,128)(2,1)}, bf16[1,512,1536]{2,1,0:T(8,128)(2,1)}, u32[]{:S(2)}, u32[]{:S(2)}) collective-permute-start(bf16[1,512,1536]{2,1,0:T(8,128)(2,1)} %fusion.127), channel_id=1, source_target_pairs={{0,1},{1,0},{2,3},{3,2},{4,5},{5,4},{6,7},{7,6},{8,9},{9,8},{10,11... | collective-permute-start | bytes 4718600 | tf_op jit(solution)/shard_map/ppermute | solution.py:524
  916.6 57.7 %collective-permute-start.29 = (bf16[4,1,96,2304]{3,2,0,1:T(8,128)(2,1)}, bf16[4,1,96,2304]{3,2,0,1:T(8,128)(2,1)}, u32[]{:S(2)}, u32[]{:S(2)}) collective-permute-start(bf16[4,1,96,2304]{3,2,0,1:T(8,128)(2,1)} %fusion.149), channel_id=1, source_target_pairs={{0,4},{2,6},{4,0},{6,2},{8,12},{10,14},{12,8},{14,10},{16,20},{18,... | collective-permute-start | bytes 5308424 | tf_op jit(solution)/shard_map/ppermute | solution.py:542
  935.6 105.7 %collective-permute-start.39 = (f32[48,2,1536]{2,0,1:T(8,128)}, f32[48,2,1536]{2,0,1:T(8,128)}, u32[]{:S(2)}, u32[]{:S(2)}) collective-permute-start(f32[48,2,1536]{2,0,1:T(8,128)} %dynamic-slice_bitcast_fusion.1), channel_id=1, source_target_pairs={{0,1},{1,0},{2,3},{3,2},{4,5},{5,4},{6,7},{7,6},{8,9},{9,8},{10,11... | collective-permute-start | bytes 1769480 | tf_op jit(solution)/shard_map/ppermute | solution.py:524
  1005.5 50.8 %all-to-all-start.2 = ((bf16[16,292,128]{2,1,0:T(8,128)(2,1)}), bf16[16,292,128]{2,1,0:T(8,128)(2,1)}, u32[]{:S(2)}, u32[]{:S(2)}) async-start(bf16[16,292,128]{2,1,0:T(8,128)(2,1)} %broadcast_in_dim.8), calls=%async_computation.6 | async-start | bytes 2424832 | tf_op jit(solution)/shard_map/all_to_all | solution.py:1038
  (181 other events, 2072.6 us)
Sparse Core Ops, SparseCore 0:
  10.4 142.8 all-gather.4
  154.9 104.3 all-gather.6
  260.8 98.9 all-gather.8
  391.5 114.3 reduce-scatter.4
  510.4 111.0 reduce-scatter.8
  625.5 141.9 reduce-scatter.6
  772.2 127.2 reduce-scatter.10
